TPU v7x, 32 devices: a whole 2x2x4 slice. The times are simulated.
32 devices in a mesh: parts: 2 (over y), seq: 4 (over z), head: 4 (over x, core).
Axes of the slice: x: 2, y: 2, z: 4, core: 2. Of those that a mesh axis runs over, the one named last changes fastest.
Arguments:
- queries: bfloat16 [2048, 16, 128], P(('parts', 'seq'), 'head'), parts along dimension 0, may hold values from -6 to 6
- keys: bfloat16 [2048, 16, 128], P(('parts', 'seq'), 'head'), parts along dimension 0, may hold values from -8 to 8
- values: bfloat16 [2048, 16, 128], P(('parts', 'seq'), 'head'), parts along dimension 0, may hold values from -6 to 6
- delta_keys: bfloat16 [2048, 2, 16, 128], P(('parts', 'seq'), None, 'head'), parts along dimension 0, may hold values from -6 to 6
- delta_values: bfloat16 [2048, 2, 16, 128], P(('parts', 'seq'), None, 'head'), parts along dimension 0, may hold values from -6 to 6
- betas: float32 [2, 16, 2048], P(None, 'head', ('parts', 'seq')), parts along dimension 2, may hold values from 0.2 to 1.8
- decays: float32 [16, 2048], P('head', ('parts', 'seq')), parts along dimension 1, may hold values from 0.4 to 1
- grad_out: bfloat16 [2048, 16, 128], P(('parts', 'seq'), 'head'), parts along dimension 0, may hold values from -6 to 6
Outputs:
- grad_queries: bfloat16 [2048, 16, 128], P(('parts', 'seq'), 'head'), parts along dimension 0
- grad_keys: bfloat16 [2048, 16, 128], P(('parts', 'seq'), 'head'), parts along dimension 0
- grad_values: bfloat16 [2048, 16, 128], P(('parts', 'seq'), 'head'), parts along dimension 0
- grad_delta_keys: bfloat16 [2048, 2, 16, 128], P(('parts', 'seq'), None, 'head'), parts along dimension 0
- grad_delta_values: bfloat16 [2048, 2, 16, 128], P(('parts', 'seq'), None, 'head'), parts along dimension 0
- grad_betas: float32 [2, 16, 2048], P(None, 'head', ('parts', 'seq')), parts along dimension 2
- grad_decays: float32 [16, 2048], P('head', ('parts', 'seq')), parts along dimension 1
There are 2 independent parts, one for each index of `parts`. A program takes and returns all parts, laid end to end along the dimension named above; each array names one. Nothing has to cross between parts.
All inputs are finite; a program needn't handle non-finite values.
Results may differ from a plain program's by a relative error of at most 0.02.
Values may be sent and summed in bfloat16 or wider, within the bound.
No kernel may reach another device: no remote copies, remote signals or barrier semaphores. Data moves between devices by JAX's collectives and lax.ppermute only.
A program may use at most 128 MiB of HBM per device.

v0:
```python
import math

import jax
import jax.numpy as jnp
from jax import lax
from jax.sharding import PartitionSpec as P

WINDOW = 1024


PRECISE = lax.Precision.HIGHEST
EPS = 1e-06


def shifted(value, axis, steps):
    count = lax.axis_size(axis)
    initial, last = (max(0, -steps), min(count, count - steps))
    return lax.ppermute(value, axis, [(source, source + steps) for source in range(initial, last)])


def entering(part, axis, combine, identity, reverse):
    count = lax.axis_size(axis)
    place = lax.axis_index(axis)
    ahead = count - 1 - place if reverse else place
    gathered = jax.tree.map(lambda a: lax.all_gather(a, axis), part)
    state = jax.tree.map(lambda a, e: jnp.zeros_like(a) + jnp.asarray(e, a.dtype), part, identity)

    def one(step, state):
        source = count - 1 - step if reverse else step
        return combine(
            state, jax.tree.map(lambda a: lax.dynamic_index_in_dim(a, source, 0, False), gathered)
        )

    return lax.fori_loop(0, ahead, one, state)


def compose(earlier, later):
    joined = jnp.einsum("hij,hjk->hik", later[0], earlier[0], precision=PRECISE)
    offset = jnp.einsum("hij,hjk->hik", later[0], earlier[1], precision=PRECISE) + later[1]
    return (joined, offset)


def block_core(state, keys_block, values_block, beta_block, logs_block):
    size = keys_block.shape[1]
    running = jnp.cumsum(logs_block, axis=-1)
    order = jnp.arange(size)
    strict = order[:, None] > order[None, :]
    gap = running[:, :, None] - running[:, None, :]
    fade = jnp.where(strict, jnp.exp(jnp.where(strict, gap, 0.0)), 0.0)
    gram = jnp.einsum("hie,hje->hij", keys_block, keys_block, precision=PRECISE)
    system = jnp.eye(size, dtype=jnp.float32) + beta_block[:, :, None] * fade * gram
    recalled = jnp.einsum("hie,hef->hif", keys_block, state, precision=PRECISE)
    target = beta_block[:, :, None] * (values_block - jnp.exp(running)[:, :, None] * recalled)
    updates = jax.scipy.linalg.solve_triangular(system, target, lower=True, unit_diagonal=True)
    tail = jnp.exp(running[:, -1:] - running)
    advanced = jnp.exp(running[:, -1])[:, None, None] * state + jnp.einsum(
        "hje,hjf->hef", keys_block * tail[:, :, None], updates, precision=PRECISE
    )
    return (running, updates, advanced)


def block_step(carry, query_block, keys_block, values_block, beta_block, logs_block):
    running, updates, advanced = block_core(carry, keys_block, values_block, beta_block, logs_block)
    size = keys_block.shape[1]
    running_query = running[:, 1::2]
    seen = jnp.arange(size)[None, :] <= 2 * jnp.arange(size // 2)[:, None] + 1
    gap = running_query[:, :, None] - running[:, None, :]
    fade = jnp.where(seen, jnp.exp(jnp.where(seen, gap, 0.0)), 0.0)
    weights = jnp.einsum("hte,hje->htj", query_block, keys_block, precision=PRECISE) * fade
    outputs = jnp.exp(running_query)[:, :, None] * jnp.einsum(
        "hte,hef->htf", query_block, carry, precision=PRECISE
    )
    outputs = outputs + jnp.einsum("htj,hjf->htf", weights, updates, precision=PRECISE)
    return (advanced, outputs)


def arrange(keys_float, values_float, beta_raw, decay_raw, block):
    rows, mirrors, heads, width = keys_float.shape
    count = rows // block
    size = mirrors * block
    key_norm = keys_float * lax.rsqrt(
        jnp.sum(keys_float * keys_float, axis=-1, keepdims=True) + EPS
    )

    def to_blocks(array):
        return (
            array.reshape(count, block, mirrors, heads, width)
            .transpose(0, 3, 1, 2, 4)
            .reshape(count, heads, size, width)
        )

    def scalars(array):
        return array.reshape(heads, count, size).transpose(1, 0, 2)

    logs = jnp.stack([jnp.log(decay_raw), jnp.zeros_like(decay_raw)], axis=-1)
    return (
        to_blocks(key_norm),
        to_blocks(values_float),
        scalars(beta_raw.transpose(1, 2, 0)),
        scalars(logs),
    )


def query_blocks(query_raw, block):
    rows, heads, width = query_raw.shape
    query_norm = query_raw * lax.rsqrt(
        jnp.mean(query_raw * query_raw, axis=-1, keepdims=True) + EPS
    )
    return query_norm.reshape(rows // block, block, heads, width).transpose(0, 2, 1, 3)


def delta_local(query_raw, keys_float, values_float, beta_raw, decay_raw, state):
    rows, heads, width = query_raw.shape
    block = math.gcd(rows, 64)
    query_parts = query_blocks(query_raw, block)
    key_parts, value_parts, beta_parts, log_parts = arrange(
        keys_float, values_float, beta_raw, decay_raw, block
    )

    def delta_advance(carry, items):
        return block_step(carry, *items)

    final, outputs = lax.scan(
        delta_advance, state, (query_parts, key_parts, value_parts, beta_parts, log_parts)
    )
    return (outputs.transpose(0, 2, 1, 3).reshape(rows, heads, width), final)


def adjoint_source(query_raw, keys_float, beta_raw, decay_raw, cotangent):
    rows, heads, width = query_raw.shape
    block = math.gcd(rows, 64)
    query_parts = query_blocks(query_raw, block)
    key_parts, value_parts, beta_parts, log_parts = arrange(
        keys_float, jnp.zeros_like(keys_float), beta_raw, decay_raw, block
    )
    cot_parts = cotangent.reshape(rows // block, block, heads, width).transpose(0, 2, 1, 3)

    def retreat(adjoint, items):
        query_block, keys_block, values_block, beta_block, logs_block, cot_block = items

        def linear(carry):
            return block_step(carry, query_block, keys_block, values_block, beta_block, logs_block)

        pull = jax.vjp(linear, jnp.zeros_like(adjoint))[1]
        return (pull((adjoint, cot_block))[0], None)

    start = jnp.zeros((heads, width, width), jnp.float32)
    source, unused = lax.scan(
        retreat,
        start,
        (query_parts, key_parts, value_parts, beta_parts, log_parts, cot_parts),
        reverse=True,
    )
    return source


def shard_affine(keys_float, values_float, beta_raw, decay_raw):
    rows, mirrors, heads, width = keys_float.shape
    block = math.gcd(rows, 64)
    key_parts, value_parts, beta_parts, log_parts = arrange(
        keys_float, values_float, beta_raw, decay_raw, block
    )
    extended = jnp.concatenate([value_parts, jnp.zeros_like(value_parts)], axis=-1)
    identity = jnp.broadcast_to(jnp.eye(width, dtype=jnp.float32), (heads, width, width))
    start = jnp.concatenate([jnp.zeros((heads, width, width), jnp.float32), identity], axis=-1)

    def shard_advance(carry, items):
        keys_block, values_block, beta_block, logs_block = items
        return (block_core(carry, keys_block, values_block, beta_block, logs_block)[2], None)

    final, unused = lax.scan(shard_advance, start, (key_parts, extended, beta_parts, log_parts))
    return (final[:, :, width:], final[:, :, :width])


def body(queries, keys, values, delta_keys, delta_values, betas, decays, grad_out):
    rows, heads, width = queries.shape
    span = WINDOW // rows
    scale = 1.0 / math.sqrt(width)
    place = lax.axis_index("seq")
    couple = jnp.stack([keys, values])
    earlier = []
    for step in range(span):
        earlier.append(shifted(couple, "seq", step + 1))
    ordered = earlier[::-1] + [couple]
    window_keys = jnp.concatenate([piece[0] for piece in ordered], axis=0)
    window_values = jnp.concatenate([piece[1] for piece in ordered], axis=0)
    relative = jnp.arange((span + 1) * rows, dtype=jnp.int32) - span * rows
    local = jnp.arange(rows, dtype=jnp.int32)
    visible = (
        (relative[None, :] <= local[:, None])
        & (relative[None, :] > local[:, None] - WINDOW)
        & (place * rows + relative[None, :] >= 0)
    )
    scores = (
        jnp.einsum("qhe,khe->hqk", queries, window_keys, preferred_element_type=jnp.float32) * scale
    )
    top = jnp.max(jnp.where(visible, scores, -jnp.inf), axis=-1)
    lifted = jnp.where(visible, jnp.exp(jnp.where(visible, scores - top[:, :, None], 0.0)), 0.0)
    total = jnp.sum(lifted, axis=-1)
    attention = lifted / total[:, :, None]
    attention_low = attention.astype(jnp.bfloat16)
    mixed = jnp.einsum(
        "hqk,khe->qhe", attention_low, window_values, preferred_element_type=jnp.float32
    )
    attended = mixed.astype(jnp.bfloat16)
    query_raw = attended.astype(jnp.float32)
    keys_float = delta_keys.astype(jnp.float32)
    values_float = delta_values.astype(jnp.float32)
    cotangent = grad_out.astype(jnp.float32)
    transition, offset = shard_affine(keys_float, values_float, betas, decays)
    identity = jnp.broadcast_to(jnp.eye(width, dtype=jnp.float32), transition.shape)
    zero_state = jnp.zeros_like(offset)
    source = adjoint_source(query_raw, keys_float, betas, decays, cotangent)
    entry = entering((transition, offset), "seq", compose, (identity, zero_state), False)[1]
    exit_grad = entering(
        (jnp.swapaxes(transition, 1, 2), source), "seq", compose, (identity, zero_state), True
    )[1]
    grads = jax.vjp(delta_local, query_raw, keys_float, values_float, betas, decays, entry)[1](
        (cotangent, exit_grad)
    )
    grad_mixed = grads[0].astype(jnp.bfloat16)
    row_dots = jnp.sum(grad_mixed.astype(jnp.float32) * mixed, axis=-1).T
    grad_attention = jnp.einsum(
        "qhe,khe->hqk", grad_mixed, window_values, preferred_element_type=jnp.float32
    )
    grad_scores = (attention * (grad_attention - row_dots[:, :, None]) * scale).astype(jnp.bfloat16)
    grad_queries = jnp.einsum(
        "hqk,khe->qhe", grad_scores, window_keys, preferred_element_type=jnp.float32
    ).astype(jnp.bfloat16)
    key_parts = jnp.einsum("hqk,qhe->khe", grad_scores, queries, preferred_element_type=jnp.float32)
    value_parts = jnp.einsum(
        "hqk,qhe->khe", attention_low, grad_mixed, preferred_element_type=jnp.float32
    )
    gathered = jnp.stack([key_parts[span * rows :], value_parts[span * rows :]])
    for later in range(1, span + 1):
        first = (span - later) * rows
        gathered = gathered + shifted(
            jnp.stack([key_parts[first : first + rows], value_parts[first : first + rows]]),
            "seq",
            -later,
        )
    return (
        grad_queries,
        gathered[0].astype(jnp.bfloat16),
        gathered[1].astype(jnp.bfloat16),
        grads[1].astype(jnp.bfloat16),
        grads[2].astype(jnp.bfloat16),
        grads[3],
        grads[4],
    )


def solution(mesh):
    in_specs = (
        P(("parts", "seq"), "head", None),
        P(("parts", "seq"), "head", None),
        P(("parts", "seq"), "head", None),
        P(("parts", "seq"), None, "head", None),
        P(("parts", "seq"), None, "head", None),
        P(None, "head", ("parts", "seq")),
        P("head", ("parts", "seq")),
        P(("parts", "seq"), "head", None),
    )
    out_specs = (
        P(("parts", "seq"), "head", None),
        P(("parts", "seq"), "head", None),
        P(("parts", "seq"), "head", None),
        P(("parts", "seq"), None, "head", None),
        P(("parts", "seq"), None, "head", None),
        P(None, "head", ("parts", "seq")),
        P("head", ("parts", "seq")),
    )
    return jax.shard_map(body, mesh=mesh, in_specs=in_specs, out_specs=out_specs, check_vma=False)
```

profile of v0, /device:TPU:0, one launch (start us, length us, event | category | flops | bytes accessed | tf_op | source)
XLA Modules:
  0.0 1245.2 jit_solution(11356402761721298906)
XLA Ops:
  15.1 175.8 %while.143 = (s32[]{:T(128)}, f32[4,128,256]{2,1,0:T(8,128)S(1)}, f32[4,4,128]{2,1,0:T(4,128)S(1)}, f32[4,4,128,128]{3,2,1,0:T(8,128)S(1)}, f32[4,4,128]{2,1,0:T...) while((s32[]{:T(128)}, f32[4,128,256]{2,1,0:T(8,128)S(1)}, f32[4,4,128]{2,1,0:T(4,128)S(1)}, ...), condition=%wide.region_5.6_spmd, body=%wide.region_3.5_spmd.sunk | while | flops 706052224 | bytes 5866165 | solution.py:171
  18.2 39.3 %custom-call.43 = f32[4,1,128,128]{2,3,1,0:T(8,128)S(1)} custom-call(f32[4,1,128,128]{3,2,1,0:T(8,128)S(1)} %fusion.366), custom_call_target="InvertDiagBlocksLowerTriangular" | custom-call | tf_op jit(solution)/shard_map/while/body/eval_jaxpr/jit(_solve_triangular)/vmap()/triangular_solve | solution.py:54
  62.2 39.3 %custom-call.43 = f32[4,1,128,128]{2,3,1,0:T(8,128)S(1)} custom-call(f32[4,1,128,128]{3,2,1,0:T(8,128)S(1)} %fusion.366), custom_call_target="InvertDiagBlocksLowerTriangular" | custom-call | tf_op jit(solution)/shard_map/while/body/eval_jaxpr/jit(_solve_triangular)/vmap()/triangular_solve | solution.py:54
  106.1 39.3 %custom-call.43 = f32[4,1,128,128]{2,3,1,0:T(8,128)S(1)} custom-call(f32[4,1,128,128]{3,2,1,0:T(8,128)S(1)} %fusion.366), custom_call_target="InvertDiagBlocksLowerTriangular" | custom-call | tf_op jit(solution)/shard_map/while/body/eval_jaxpr/jit(_solve_triangular)/vmap()/triangular_solve | solution.py:54
  150.1 39.3 %custom-call.43 = f32[4,1,128,128]{2,3,1,0:T(8,128)S(1)} custom-call(f32[4,1,128,128]{3,2,1,0:T(8,128)S(1)} %fusion.366), custom_call_target="InvertDiagBlocksLowerTriangular" | custom-call | tf_op jit(solution)/shard_map/while/body/eval_jaxpr/jit(_solve_triangular)/vmap()/triangular_solve | solution.py:54
  216.0 10.2 collective-permute-done.1
  228.2 14.8 %collective-permute-done.2 = bf16[2,256,4,128]{3,1,2,0:T(8,128)(2,1)} collective-permute-done((bf16[2,256,4,128]{3,1,2,0:T(8,128)(2,1)}, bf16[2,256,4,128]{3,1,2,0:T(8,128)(2,1)}, u32[]{:S(2)}, u32[]{:S(2)}) %collective-permute-start.2) | collective-permute-done | bytes 524320 | tf_op jit(solution)/shard_map/ppermute | solution.py:18
  272.5 183.6 %while.148 = (s32[]{:T(128)}, f32[4,128,128]{2,1,0:T(8,128)S(1)}, f32[4,4,64,128]{3,2,1,0:T(8,128)S(1)}, f32[4,4,128]{2,1,0:T(4,128)S(1)}, f32[4,4,64,128]{3,2,1...) while((s32[]{:T(128)}, f32[4,128,128]{2,1,0:T(8,128)S(1)}, ...), condition=%wide.region_9.11_spmd.clone, body=%wide.region_7.10_spmd.clone.sunk | while | flops 555163904 | bytes 5632747 | solution.py:148
  276.6 40.1 %custom-call.46 = f32[4,1,128,128]{2,3,1,0:T(8,128)S(1)} custom-call(f32[4,1,128,128]{3,2,1,0:T(8,128)} %fusion.435), custom_call_target="InvertDiagBlocksLowerTriangular" | custom-call | tf_op jit(solution)/shard_map/while/body/eval_jaxpr/transpose(jvp(jit(_solve_triangular)))/vmap()/triangular_solve/custom-call.0 | solution.py:54
  322.5 40.1 %custom-call.46 = f32[4,1,128,128]{2,3,1,0:T(8,128)S(1)} custom-call(f32[4,1,128,128]{3,2,1,0:T(8,128)} %fusion.435), custom_call_target="InvertDiagBlocksLowerTriangular" | custom-call | tf_op jit(solution)/shard_map/while/body/eval_jaxpr/transpose(jvp(jit(_solve_triangular)))/vmap()/triangular_solve/custom-call.0 | solution.py:54
  368.4 40.1 %custom-call.46 = f32[4,1,128,128]{2,3,1,0:T(8,128)S(1)} custom-call(f32[4,1,128,128]{3,2,1,0:T(8,128)} %fusion.435), custom_call_target="InvertDiagBlocksLowerTriangular" | custom-call | tf_op jit(solution)/shard_map/while/body/eval_jaxpr/transpose(jvp(jit(_solve_triangular)))/vmap()/triangular_solve/custom-call.0 | solution.py:54
  414.3 40.1 %custom-call.46 = f32[4,1,128,128]{2,3,1,0:T(8,128)S(1)} custom-call(f32[4,1,128,128]{3,2,1,0:T(8,128)} %fusion.435), custom_call_target="InvertDiagBlocksLowerTriangular" | custom-call | tf_op jit(solution)/shard_map/while/body/eval_jaxpr/transpose(jvp(jit(_solve_triangular)))/vmap()/triangular_solve/custom-call.0 | solution.py:54
  469.3 219.9 %while.146 = (s32[]{:T(128)}, f32[4,128,128]{2,1,0:T(8,128)S(1)}, f32[4,4,128,128]{3,2,1,0:T(8,128)}, f32[4,4,128,128]{3,2,1,0:T(8,128)}, f32[4,4,128,1]{2,1,3,0...) while((s32[]{:T(128)}, f32[4,128,128]{2,1,0:T(8,128)S(1)}, ...), condition=%wide.region_16.18_spmd.clone.clone, body=%wide.region_14.17_spmd.clone.clone.sunk | while | flops 505463936 | bytes 9296889 | solution.py:123
  471.7 39.3 %custom-call.44 = f32[4,1,128,128]{2,3,1,0:T(8,128)S(1)} custom-call(f32[4,1,128,128]{3,2,1,0:T(8,128)S(1)} %add_bitcast_fusion.2), custom_call_target="InvertDiagBlocksLowerTriangular" | custom-call | tf_op jit(solution)/shard_map/jvp()/while/body/eval_jaxpr/jit(_solve_triangular)/vmap()/triangular_solve | solution.py:54
  526.6 39.3 %custom-call.44 = f32[4,1,128,128]{2,3,1,0:T(8,128)S(1)} custom-call(f32[4,1,128,128]{3,2,1,0:T(8,128)S(1)} %add_bitcast_fusion.2), custom_call_target="InvertDiagBlocksLowerTriangular" | custom-call | tf_op jit(solution)/shard_map/jvp()/while/body/eval_jaxpr/jit(_solve_triangular)/vmap()/triangular_solve | solution.py:54
  581.7 39.3 %custom-call.44 = f32[4,1,128,128]{2,3,1,0:T(8,128)S(1)} custom-call(f32[4,1,128,128]{3,2,1,0:T(8,128)S(1)} %add_bitcast_fusion.2), custom_call_target="InvertDiagBlocksLowerTriangular" | custom-call | tf_op jit(solution)/shard_map/jvp()/while/body/eval_jaxpr/jit(_solve_triangular)/vmap()/triangular_solve | solution.py:54
  636.6 39.3 %custom-call.44 = f32[4,1,128,128]{2,3,1,0:T(8,128)S(1)} custom-call(f32[4,1,128,128]{3,2,1,0:T(8,128)S(1)} %add_bitcast_fusion.2), custom_call_target="InvertDiagBlocksLowerTriangular" | custom-call | tf_op jit(solution)/shard_map/jvp()/while/body/eval_jaxpr/jit(_solve_triangular)/vmap()/triangular_solve | solution.py:54
  696.9 399.5 %while.147 = (s32[]{:T(128)}, f32[4,128,128]{2,1,0:T(8,128)S(1)}, f32[4,4,64,128]{3,2,0,1:T(8,128)}, f32[4,4,128,128]{3,2,1,0:T(8,128)}, bf16[4,4,128,128]{3,2,1...) while((s32[]{:T(128)}, f32[4,128,128]{2,1,0:T(8,128)S(1)}, ...), condition=%wide.region_30.32_spmd.clone.clone, body=%wide.region_17.31_spmd.clone.clone.sunk | while | flops 1211256448 | bytes 30195504 | solution.py:123
  701.2 39.3 %custom-call.45 = f32[4,1,128,128]{2,3,1,0:T(8,128)S(1)} custom-call(f32[4,1,128,128]{3,2,1,0:T(8,128)S(1)} %fusion.403), custom_call_target="InvertDiagBlocksLowerTriangular" | custom-call | tf_op jit(solution)/shard_map/transpose(jvp())/while/body/eval_jaxpr/jit(_solve_triangular)/vmap()/triangular_solve/custom-call.0 | solution.py:54
  801.0 39.3 %custom-call.45 = f32[4,1,128,128]{2,3,1,0:T(8,128)S(1)} custom-call(f32[4,1,128,128]{3,2,1,0:T(8,128)S(1)} %fusion.403), custom_call_target="InvertDiagBlocksLowerTriangular" | custom-call | tf_op jit(solution)/shard_map/transpose(jvp())/while/body/eval_jaxpr/jit(_solve_triangular)/vmap()/triangular_solve/custom-call.0 | solution.py:54
  900.7 39.3 %custom-call.45 = f32[4,1,128,128]{2,3,1,0:T(8,128)S(1)} custom-call(f32[4,1,128,128]{3,2,1,0:T(8,128)S(1)} %fusion.403), custom_call_target="InvertDiagBlocksLowerTriangular" | custom-call | tf_op jit(solution)/shard_map/transpose(jvp())/while/body/eval_jaxpr/jit(_solve_triangular)/vmap()/triangular_solve/custom-call.0 | solution.py:54
  1000.5 39.3 %custom-call.45 = f32[4,1,128,128]{2,3,1,0:T(8,128)S(1)} custom-call(f32[4,1,128,128]{3,2,1,0:T(8,128)S(1)} %fusion.403), custom_call_target="InvertDiagBlocksLowerTriangular" | custom-call | tf_op jit(solution)/shard_map/transpose(jvp())/while/body/eval_jaxpr/jit(_solve_triangular)/vmap()/triangular_solve/custom-call.0 | solution.py:54
  1142.3 21.1 %collective-permute-done.4 = f32[2,256,4,128]{3,1,2,0:T(8,128)} collective-permute-done((f32[2,256,4,128]{3,1,2,0:T(8,128)}, f32[2,256,4,128]{3,1,2,0:T(8,128)}, u32[]{:S(2)}, u32[]{:S(2)}) %collective-permute-start.4) | collective-permute-done | bytes 1048608 | tf_op jit(solution)/shard_map/ppermute | solution.py:18
  1163.4 70.5 %collective-permute-done.5 = f32[2,256,4,128]{3,1,2,0:T(8,128)} collective-permute-done((f32[2,256,4,128]{3,1,2,0:T(8,128)}, f32[2,256,4,128]{3,1,2,0:T(8,128)}, u32[]{:S(2)}, u32[]{:S(2)}) %collective-permute-start.5) | collective-permute-done | bytes 1048608 | tf_op jit(solution)/shard_map/ppermute | solution.py:18
  (666 shorter events, 483.8 us)
Async XLA Ops:
  7.2 250.0 %copy-start = (bf16[256,4,128]{2,1,0:T(4,128)(2,1)S(1)}, bf16[256,4,128]{2,1,0:T(4,128)(2,1)}, u32[]{:S(2)}) copy-start(bf16[256,4,128]{2,1,0:T(4,128)(2,1)} %param.22) | copy-start | bytes 786436
  7.2 449.8 %all-gather.13.cloned.1.call-start = ((), (), s32[]{:S(2)}) async-start(), calls=%async_computation.2 | async-start | bytes 1310720 | tf_op jit(solution)/shard_map/all_gather | solution.py:25
  191.9 17.0 %copy-start.21 = (bf16[256,4,128]{2,1,0:T(4,128)(2,1)S(1)}, bf16[256,4,128]{2,1,0:T(4,128)(2,1)}, u32[]{:S(2)}) copy-start(bf16[256,4,128]{2,1,0:T(4,128)(2,1)} %param.29) | copy-start | bytes 786436
  192.7 264.2 %all-gather.15.cloned.1.call-start = ((), (), s32[]{:S(2)}) async-start(), calls=%async_computation.3 | async-start | bytes 1310720 | tf_op jit(solution)/shard_map/all_gather | solution.py:25
  193.6 495.7 %all-gather.9.cloned.1.call-start = ((), (), s32[]{:S(2)}) async-start(), calls=%async_computation | async-start | bytes 1310720 | tf_op jit(solution)/shard_map/all_gather | solution.py:25
  194.5 19.5 %collective-permute-start = (bf16[2,256,4,128]{3,1,2,0:T(8,128)(2,1)}, bf16[2,256,4,128]{3,1,2,0:T(8,128)(2,1)}, u32[]{:S(2)}, u32[]{:S(2)}) collective-permute-start(bf16[2,256,4,128]{3,1,2,0:T(8,128)(2,1)} %pad_maximum_fusion.4), channel_id=1, source_target_pairs={} | collective-permute-start | bytes 1572872 | tf_op jit(solution)/shard_map/ppermute | solution.py:18
  196.0 30.2 %collective-permute-start.1 = (bf16[2,256,4,128]{3,1,2,0:T(8,128)(2,1)}, bf16[2,256,4,128]{3,1,2,0:T(8,128)(2,1)}, u32[]{:S(2)}, u32[]{:S(2)}) collective-permute-start(bf16[2,256,4,128]{3,1,2,0:T(8,128)(2,1)} %pad_maximum_fusion.4), channel_id=1, source_target_pairs={{0,12},{1,13},{2,14},{3,15},{16,28},{17,29},{18,30},{19,31}} | collective-permute-start | bytes 1572872 | tf_op jit(solution)/shard_map/ppermute | solution.py:18
  203.7 39.3 %collective-permute-start.2 = (bf16[2,256,4,128]{3,1,2,0:T(8,128)(2,1)}, bf16[2,256,4,128]{3,1,2,0:T(8,128)(2,1)}, u32[]{:S(2)}, u32[]{:S(2)}) collective-permute-start(bf16[2,256,4,128]{3,1,2,0:T(8,128)(2,1)} %pad_maximum_fusion.4), channel_id=1, source_target_pairs={{0,8},{4,12},{1,9},{5,13},{2,10},{6,14},{3,11},{7,15},{16,24},{20,... | collective-permute-start | bytes 1572872 | tf_op jit(solution)/shard_map/ppermute | solution.py:18
  205.8 47.9 %collective-permute-start.3 = (bf16[2,256,4,128]{3,1,2,0:T(8,128)(2,1)}, bf16[2,256,4,128]{3,1,2,0:T(8,128)(2,1)}, u32[]{:S(2)}, u32[]{:S(2)}) collective-permute-start(bf16[2,256,4,128]{3,1,2,0:T(8,128)(2,1)} %pad_maximum_fusion.4), channel_id=1, source_target_pairs={{0,4},{4,8},{8,12},{1,5},{5,9},{9,13},{2,6},{6,10},{10,14},{3,7},{... | collective-permute-start | bytes 1572872 | tf_op jit(solution)/shard_map/ppermute | solution.py:18
  208.3 480.9 %all-gather.11.cloned.1.call-start = ((), (), s32[]{:S(2)}) async-start(), calls=%async_computation.1 | async-start | bytes 1310720 | tf_op jit(solution)/shard_map/all_gather | solution.py:25
  226.2 31.0 %copy-start.20 = (pred[256,1280]{0,1:T(8,128)(4,1)S(1)}, pred[256,1280]{0,1:T(8,128)(4,1)}, u32[]{:S(2)}) copy-start(pred[256,1280]{0,1:T(8,128)(4,1)} %fusion.208) | copy-start | bytes 983044
  697.1 84.2 %copy-start.1 = (f32[4,4,64,128]{3,2,1,0:T(8,128)}, f32[4,4,64,128]{3,2,1,0:T(8,128)S(1)}, u32[]{:S(2)}) copy-start(f32[4,4,64,128]{3,2,1,0:T(8,128)S(1)} %get-tuple-element.3868) | copy-start | bytes 1572868 | tf_op jit(solution)/shard_map/transpose(jvp())/while
  796.9 84.1 %copy-start.1 = (f32[4,4,64,128]{3,2,1,0:T(8,128)}, f32[4,4,64,128]{3,2,1,0:T(8,128)S(1)}, u32[]{:S(2)}) copy-start(f32[4,4,64,128]{3,2,1,0:T(8,128)S(1)} %get-tuple-element.3868) | copy-start | bytes 1572868 | tf_op jit(solution)/shard_map/transpose(jvp())/while
  888.7 7.9 copy-start.2
  896.6 84.1 %copy-start.1 = (f32[4,4,64,128]{3,2,1,0:T(8,128)}, f32[4,4,64,128]{3,2,1,0:T(8,128)S(1)}, u32[]{:S(2)}) copy-start(f32[4,4,64,128]{3,2,1,0:T(8,128)S(1)} %get-tuple-element.3868) | copy-start | bytes 1572868 | tf_op jit(solution)/shard_map/transpose(jvp())/while
  988.4 7.9 copy-start.2
  996.4 84.1 %copy-start.1 = (f32[4,4,64,128]{3,2,1,0:T(8,128)}, f32[4,4,64,128]{3,2,1,0:T(8,128)S(1)}, u32[]{:S(2)}) copy-start(f32[4,4,64,128]{3,2,1,0:T(8,128)S(1)} %get-tuple-element.3868) | copy-start | bytes 1572868 | tf_op jit(solution)/shard_map/transpose(jvp())/while
  1120.3 43.2 %collective-permute-start.4 = (f32[2,256,4,128]{3,1,2,0:T(8,128)}, f32[2,256,4,128]{3,1,2,0:T(8,128)}, u32[]{:S(2)}, u32[]{:S(2)}) collective-permute-start(f32[2,256,4,128]{3,1,2,0:T(8,128)} %pad_maximum_fusion), channel_id=1, source_target_pairs={{4,0},{8,4},{12,8},{5,1},{9,5},{13,9},{6,2},{10,6},{14,10},{7,3},{... | collective-permute-start | bytes 3145736 | tf_op jit(solution)/shard_map/ppermute | solution.py:18
  1122.6 111.3 %collective-permute-start.5 = (f32[2,256,4,128]{3,1,2,0:T(8,128)}, f32[2,256,4,128]{3,1,2,0:T(8,128)}, u32[]{:S(2)}, u32[]{:S(2)}) collective-permute-start(f32[2,256,4,128]{3,1,2,0:T(8,128)} %pad_maximum_fusion.1), channel_id=1, source_target_pairs={{8,0},{12,4},{9,1},{13,5},{10,2},{14,6},{11,3},{15,7},{24,16},{28,... | collective-permute-start | bytes 3145736 | tf_op jit(solution)/shard_map/ppermute | solution.py:18
  1125.0 108.9 %collective-permute-start.6 = (f32[2,256,4,128]{3,1,2,0:T(8,128)}, f32[2,256,4,128]{3,1,2,0:T(8,128)}, u32[]{:S(2)}, u32[]{:S(2)}) collective-permute-start(f32[2,256,4,128]{3,1,2,0:T(8,128)} %pad_maximum_fusion.2), channel_id=1, source_target_pairs={{12,0},{13,1},{14,2},{15,3},{28,16},{29,17},{30,18},{31,19}} | collective-permute-start | bytes 3145736 | tf_op jit(solution)/shard_map/ppermute | solution.py:18
  1127.4 10.1 copy-start.26
  1127.4 106.5 %collective-permute-start.7 = (f32[2,256,4,128]{3,1,2,0:T(8,128)}, f32[2,256,4,128]{3,1,2,0:T(8,128)}, u32[]{:S(2)}, u32[]{:S(2)}) collective-permute-start(f32[2,256,4,128]{3,1,2,0:T(8,128)} %pad_maximum_fusion.3), channel_id=1, source_target_pairs={} | collective-permute-start | bytes 3145736 | tf_op jit(solution)/shard_map/ppermute | solution.py:18
  1129.4 10.7 copy-start.11
  1132.6 101.3 %copy-start.14 = (f32[1,256,4,128]{3,1,2,0:T(8,128)S(1)}, f32[1,256,4,128]{3,1,2,0:T(8,128)}, u32[]{:S(2)}) copy-start(f32[1,256,4,128]{3,1,2,0:T(8,128)} %get-tuple-element.2850) | copy-start | bytes 1572868
  (28 other events, 82.5 us)
Sparse Core Ops, SparseCore 0:
  192.9 44.4 all-gather.12
  238.9 44.0 all-gather.14
  285.2 29.1 all-gather.8
  457.0 46.0 all-gather.10
where the time goes:
time: 1260 us; the launch traced here: 1250 us
  other arithmetic  720 us (57%)
  matrix products  202 us (16%)
  local copies, waits for them, and re-layouts  160 us (13%)
  waiting for transfers between devices  126 us (10%)
  starting transfers between devices  20 us (2%)
  between operations  14.9 us (1%)
    another operation x56, other arithmetic, block_core(): jax.scipy.linalg.solve_triangular(system, target, lower=True, unit_diagon...  638 us
    ppermute x8, waiting for transfers between devices, shifted(): lax.ppermute(value, axis, [(source, source + steps) for source in range(i...  125 us
    dynamic_slice x56, local copies, waits for them, and re-layouts, shard_affine(): lax.scan(shard_advance, start, (key_parts, extended, beta_parts, log_parts))  44 us
    dot_general x20, matrix products, block_core(): recalled = jnp.einsum('hie,hef->hif', keys_block, state, precision=PRECISE)  29.3 us
    another operation x20, matrix products, block_core(): jax.scipy.linalg.solve_triangular(system, target, lower=True, unit_diagon...  27.1 us
    dot_general x20, matrix products, block_core(): gram = jnp.einsum('hie,hje->hij', keys_block, keys_block, precision=PRECISE)  26 us
  transfers between devices with their start and end apart: 12, of which 5 were waited for; matrix products, arithmetic and copies ran while one was open for 37% of the time, Pallas kernels for 0%

commit v1 on v0

v1 whole, which is shorter than its diff:
```python
import functools, math
import jax
import jax.numpy as jnp
from jax import lax
from jax.experimental import pallas as pl
from jax.experimental.pallas import tpu as pltpu
from jax.sharding import PartitionSpec as P

WINDOW = 1024

F32 = jnp.float32
BF16 = jnp.bfloat16
EPS = 1e-06
C = 64
N = 128
LIMIT = 56 * 1024 * 1024


def split(a):
    high = a.astype(BF16)
    return high, (a - high.astype(F32)).astype(BF16)


def contract(a, b, ca, cb):
    return lax.dot_general(a, b, (((ca,), (cb,)), ((), ())), preferred_element_type=F32)


def mm(a, b):
    ah, al = split(a)
    bh, bl = split(b)
    wide = jnp.concatenate([bh, bl], axis=1)
    both = contract(jnp.concatenate([ah, al], axis=1), jnp.concatenate([wide, wide], axis=0), 1, 0)
    half = b.shape[1]
    return both[:, :half] + both[:, half:]


def mm_nt(a, b):
    ah, al = split(a)
    bh, bl = split(b)
    tall = jnp.concatenate([bh, bl], axis=0)
    both = contract(jnp.concatenate([ah, al], axis=1), jnp.concatenate([tall, tall], axis=1), 1, 1)
    half = b.shape[0]
    return both[:, :half] + both[:, half:]


def mm_tn(a, b):
    ah, al = split(a)
    bh, bl = split(b)
    wide = jnp.concatenate([bh, bl], axis=1)
    both = contract(jnp.concatenate([ah, al], axis=0), jnp.concatenate([wide, wide], axis=0), 0, 0)
    half = b.shape[1]
    return both[:, :half] + both[:, half:]


def low_nt(low, b):
    bh, bl = split(b)
    both = contract(low, jnp.concatenate([bh, bl], axis=0), 1, 1)
    half = b.shape[0]
    return both[:, :half] + both[:, half:]


def low_tn(a, low):
    ah, al = split(a)
    return contract(jnp.concatenate([ah, al], axis=0), jnp.concatenate([low, low], axis=0), 0, 0)


def iota(shape, axis):
    return lax.broadcasted_iota(jnp.int32, shape, axis)


class Grid:
    def __init__(self):
        self.row = iota((N, N), 0)
        self.lane = iota((N, N), 1)
        self.row_pos = self.row & (C - 1)
        self.lane_pos = self.lane & (C - 1)
        key_row = 2 * self.row_pos + (self.row >> 6)
        key_lane = 2 * self.lane_pos + (self.lane >> 6)
        self.strict = key_row > key_lane
        self.differ = key_row ^ key_lane
        self.diag = self.row == self.lane

    def to_row(self, column):
        return jnp.sum(jnp.where(self.diag, column, 0.0), axis=0, keepdims=True)

    def to_column(self, line):
        return jnp.sum(jnp.where(self.diag, line, 0.0), axis=1, keepdims=True)


def pick_row(block, h):
    return jnp.sum(jnp.where(iota(block.shape, 0) == h, block, 0.0), axis=0, keepdims=True)


def put_row(block, h, line):
    return jnp.where(iota(block.shape, 0) == h, line, block)


def gates(grid, betas_ref, decays_ref, h, c):
    pair, half = c // 2, C * (c % 2)
    lanes = pl.ds(pair * N, N)
    first = pick_row(betas_ref[0, :, lanes], h)
    second = pick_row(betas_ref[1, :, lanes], h)
    logs = jnp.log(pick_row(decays_ref[:, lanes], h))
    offset = grid.lane - half
    chosen = jnp.where(grid.row < C, first, second)
    beta = jnp.sum(jnp.where(offset == grid.row_pos, chosen, 0.0), axis=1, keepdims=True)
    seen = (offset >= 0) & (offset <= grid.row_pos)
    run = jnp.sum(jnp.where(seen, logs, 0.0), axis=1, keepdims=True)
    inside = (offset[:1] >= 0) & (offset[:1] < C)
    end = jnp.sum(jnp.where(inside, logs, 0.0), axis=1, keepdims=True)
    return beta, run, grid.to_row(run), end


def strict_fade(grid, run, line):
    return jnp.where(grid.strict, jnp.exp(jnp.minimum(run - line, 0.0)), 0.0)


def query_fade(grid, run, line):
    seen = grid.lane_pos[:C] <= grid.row_pos[:C]
    return jnp.where(seen, jnp.exp(jnp.minimum(run[:C] - line, 0.0)), 0.0)


def pair_rows(ref, heads, h, c):
    base = c * C * 2 * heads
    return jnp.concatenate(
        [
            ref[pl.ds(base + h, C, stride=2 * heads), :],
            ref[pl.ds(base + heads + h, C, stride=2 * heads), :],
        ],
        axis=0,
    )


def local_kernel(heads, count, dk_ref, dv_ref, betas_ref, decays_ref,
                 k_ref, inv_ref, p_ref, y_ref, t_ref, o_ref, aux_ref, tsh_ref, osh_ref,
                 keys_scr, values_scr):
    h = pl.program_id(0)

    @pl.when(h == 0)
    def _():
        keys_scr[...] = dk_ref[...].astype(F32)
        values_scr[...] = dv_ref[...].astype(F32)

    grid = Grid()
    eye = jnp.where(grid.diag, 1.0, 0.0)
    state = []
    for c in range(count):
        raw = pair_rows(keys_scr, heads, h, c)
        values = pair_rows(values_scr, heads, h, c)
        scale = lax.rsqrt(jnp.sum(raw * raw, axis=1, keepdims=True) + EPS)
        keys = raw * scale
        beta, run, line, end = gates(grid, betas_ref, decays_ref, h, c)
        k_ref[0, c] = keys
        aux_ref[0, c] = jnp.broadcast_to(grid.to_row(scale), (8, N))
        system = beta * strict_fade(grid, run, line) * mm_nt(keys, keys)
        inverse = eye - jnp.where(grid.differ == 1, system, 0.0)
        rhs = jnp.concatenate([(beta * jnp.exp(run)) * keys, beta * values], axis=1)
        state.append([system, inverse, rhs, keys * jnp.exp(end - run), end])
    for level in range(1, 7):
        near = (grid.differ >= (1 << level)) & (grid.differ < (2 << level))
        for item in state:
            item.append(mm(jnp.where(near, item[0], 0.0), item[1]))
        for item in state:
            item[1] = item[1] - mm(item[1], item.pop())
    for c, item in enumerate(state):
        inv_ref[0, c] = item[1]
        both = mm(item[1], item[2])
        p_ref[0, c] = both[:, :N]
        y_ref[0, c] = both[:, N:]
        maps = mm_tn(item[3], both)
        item.append(jnp.concatenate([jnp.exp(item[4]) * eye - maps[:, :N], maps[:, N:]], axis=1))
        t_ref[0, c] = item[5][:, :N]
        o_ref[0, c] = item[5][:, N:]
    total = state[0][5]
    zero = jnp.zeros((N, N), F32)
    for c in range(1, count):
        step = state[c][5]
        total = mm(step[:, :N], total) + jnp.concatenate([zero, step[:, N:]], axis=1)
    tsh_ref[0] = total[:, :N]
    osh_ref[0] = total[:, N:]


def place_index(place, s, total):
    return lax.rem(place + s, total)


def readout_kernel(heads, count, place_ref, g_ref, betas_ref, decays_ref, s_in_ref,
                   k_ref, p_ref, y_ref, t_ref, o_ref,
                   s_ref, u_ref, dw_ref, dq_ref, *rest):
    outs, (g_scr, dq_scr, sem) = rest[:heads], rest[heads:]
    h = pl.program_id(0)

    @pl.when(h == 0)
    def _():
        g_scr[...] = g_ref[...].astype(F32)

    grid = Grid()
    current = s_in_ref[0].astype(F32)
    s_ref[0, 0] = current
    updates = []
    states = [current]
    for c in range(count):
        both = mm(jnp.concatenate([t_ref[0, c], p_ref[0, c]], axis=0), current)
        updates.append(y_ref[0, c] - both[N:])
        current = both[:N] + o_ref[0, c]
        u_ref[0, c] = updates[c]
        s_ref[0, c + 1] = current
        states.append(current)
    for c in range(count):
        beta, run, line, end = gates(grid, betas_ref, decays_ref, h, c)
        cot = g_scr[pl.ds(c * C * heads + h, C, stride=heads), :].astype(BF16)
        both = low_nt(cot, jnp.concatenate([updates[c], states[c]], axis=0))
        weights = both[:, :N] * query_fade(grid, run, line)
        dw_ref[0, c] = weights
        grad = mm(weights, k_ref[0, c]) + jnp.exp(run[:C]) * both[:, N:]
        dq_ref[0, c] = grad
        dq_scr[h, pl.ds(c * C, C), :] = grad.astype(BF16)

    @pl.when(h == heads - 1)
    def _():
        copies = []
        for s in range(heads):
            target = place_index(place_ref[0], s, heads)
            copies.append(pltpu.make_async_copy(dq_scr.at[target], outs[s], sem.at[s]))
        for copy in copies:
            copy.start()
        for copy in copies:
            copy.wait()


def unit_queries(low):
    raw = low.astype(F32)
    return raw * lax.rsqrt(jnp.mean(raw * raw, axis=1, keepdims=True) + EPS)


def source_kernel(heads, count, place_ref, g_ref, betas_ref, decays_ref, k_ref, p_ref, t_ref, *rest):
    ins, (q_ref, z_ref, b_ref, bsh_ref, g_scr, q_scr, sem) = rest[:heads], rest[heads:]
    h = pl.program_id(0)

    @pl.when(h == 0)
    def _():
        copies = []
        for s in range(heads):
            target = lax.rem(place_ref[0] + heads - s, heads)
            copies.append(pltpu.make_async_copy(ins[s], q_scr.at[target], sem.at[s]))
        for copy in copies:
            copy.start()
        g_scr[...] = g_ref[...].astype(F32)
        for copy in copies:
            copy.wait()

    grid = Grid()
    sources = []
    for c in range(count):
        beta, run, line, end = gates(grid, betas_ref, decays_ref, h, c)
        query = unit_queries(q_scr[h, pl.ds(c * C, C), :])
        q_ref[0, c] = query
        cot = g_scr[pl.ds(c * C * heads + h, C, stride=heads), :].astype(BF16)
        weights = mm_nt(query, k_ref[0, c]) * query_fade(grid, run, line)
        z = low_tn(weights, cot)
        z_ref[0, c] = z
        source = low_tn(query * jnp.exp(run[:C]), cot) - mm_tn(p_ref[0, c], z)
        b_ref[0, c] = source
        sources.append(source)
    total = sources[count - 1]
    for c in range(count - 2, -1, -1):
        total = sources[c] + mm_tn(t_ref[0, c], total)
    bsh_ref[0] = total


def final_kernel(heads, count, betas_ref, decays_ref, lam_ref, k_ref, inv_ref, t_ref, aux_ref,
                 s_ref, u_ref, dw_ref, dq_ref, q_ref, z_ref, b_ref,
                 gk_ref, gv_ref, gb_ref, gd_ref, gk_scr, gv_scr):
    h = pl.program_id(0)
    grid = Grid()
    lam = [None] * count
    lam[count - 1] = lam_ref[0].astype(F32)
    for c in range(count - 1, 0, -1):
        lam[c - 1] = mm_tn(t_ref[0, c], lam[c]) + b_ref[0, c]
    lines = [[], [], []]
    for c in range(count):
        beta, run, line, end = gates(grid, betas_ref, decays_ref, h, c)
        keys, upd, inverse, state, later = k_ref[0, c], u_ref[0, c], inv_ref[0, c], s_ref[0, c], lam[c]
        tail = jnp.exp(end - run)
        du = z_ref[0, c] + mm(keys * tail, later)
        r = mm_tn(inverse, du)
        gb = jnp.sum(r * upd, axis=1, keepdims=True) / beta
        both = mm_nt(r, jnp.concatenate([upd, state], axis=0))
        d = -both[:, :N] * (beta * strict_fade(grid, run, line))
        read = mm(d, keys) - (beta * jnp.exp(run)) * both[:, N:]
        query = q_ref[0, c]
        write = mm_tn(d, keys) + tail * mm_nt(upd, later) + mm_tn(dw_ref[0, c], query)
        grad = read + write
        scale = grid.to_column(aux_ref[0, c][:1])
        gk = scale * (grad - keys * jnp.sum(keys * grad, axis=1, keepdims=True))
        gv = beta * r
        base = c * C * 2 * heads
        for m in range(2):
            rows = pl.ds(base + m * heads + h, C, stride=2 * heads)
            gk_scr[rows, :] = gk[m * C:(m + 1) * C]
            gv_scr[rows, :] = gv[m * C:(m + 1) * C]
        pulls = jnp.sum(keys * (read - write), axis=1, keepdims=True)
        asks = jnp.sum(query * dq_ref[0, c], axis=1, keepdims=True)
        pulls = pulls[:C] + pulls[C:] + asks
        after = grid.row_pos[:C] >= grid.lane_pos[:C]
        total = jnp.sum(jnp.sum(s_ref[0, c + 1] * later, axis=1, keepdims=True), axis=0, keepdims=True)
        gd = jnp.sum(jnp.where(after, pulls, 0.0), axis=0, keepdims=True) + total
        half = C * (c % 2)
        mine = (grid.lane[:1] >= half) & (grid.lane[:1] < half + C)
        lines[2].append(jnp.where(mine, gd, 0.0))
        for m in range(2):
            pick = (grid.lane - half == grid.row - m * C) & (grid.row >= m * C) & (grid.row < (m + 1) * C)
            lines[m].append(jnp.sum(jnp.where(pick, gb, 0.0), axis=0, keepdims=True))
    for p in range(count // 2):
        lanes = pl.ds(p * N, N)
        for m in range(2):
            gb_ref[m, :, lanes] = put_row(gb_ref[m, :, lanes], h, lines[m][2 * p] + lines[m][2 * p + 1])
        gd = (lines[2][2 * p] + lines[2][2 * p + 1]) / decays_ref[:, lanes]
        gd_ref[:, lanes] = put_row(gd_ref[:, lanes], h, gd)

    @pl.when(h == heads - 1)
    def _():
        gk_ref[...] = gk_scr[...].astype(BF16)
        gv_ref[...] = gv_scr[...].astype(BF16)


def full(shape):
    return pl.BlockSpec(shape, lambda h: (0,) * len(shape))


def per_head(shape):
    return pl.BlockSpec((1,) + shape, lambda h: (h,) + (0,) * len(shape))


ANY = pl.BlockSpec(memory_space=pl.ANY)
SCALAR = pl.BlockSpec(memory_space=pltpu.SMEM)


def shaped(shape, dtype=F32):
    return jax.ShapeDtypeStruct(shape, dtype)


def call(body, name, heads, in_specs, outs, out_specs, scratch, flops):
    return pl.pallas_call(
        body,
        name=name,
        grid=(heads,),
        in_specs=in_specs,
        out_shape=outs,
        out_specs=out_specs,
        scratch_shapes=scratch,
        compiler_params=pltpu.CompilerParams(
            dimension_semantics=("arbitrary",), vmem_limit_bytes=LIMIT
        ),
        cost_estimate=pl.CostEstimate(flops=flops, bytes_accessed=8 << 20, transcendentals=0),
    )


def delta_local(dk, dv, betas, decays):
    heads, rows = decays.shape
    count = rows // C
    big, gate, dec = full(dk.shape), full(betas.shape), full(decays.shape)
    block = per_head((count, N, N))
    square = shaped((heads, count, N, N))
    return call(
        functools.partial(local_kernel, heads, count), "delta_local", heads,
        [big, big, gate, dec],
        [square] * 6 + [shaped((heads, count, 8, N))] + [shaped((heads, N, N))] * 2,
        [block] * 6 + [per_head((count, 8, N))] + [per_head((N, N))] * 2,
        [pltpu.VMEM(dk.shape, F32)] * 2,
        10 << 30,
    )(dk, dv, betas, decays)


def delta_readout(place, g, betas, decays, entry, k, p, y, t, o):
    heads, rows = decays.shape
    count = rows // C
    block, square = per_head((count, N, N)), shaped((heads, count, N, N))
    thin = per_head((count, C, N))
    return call(
        functools.partial(readout_kernel, heads, count), "delta_readout", heads,
        [SCALAR, full(g.shape), full(betas.shape), full(decays.shape), per_head((N, N))] + [block] * 5,
        [shaped((heads, count + 1, N, N)), square] + [shaped((heads, count, C, N))] * 2
        + [shaped((rows, N), BF16)] * heads,
        [per_head((count + 1, N, N)), block, thin, thin] + [ANY] * heads,
        [pltpu.VMEM(g.shape, F32), pltpu.VMEM((heads, rows, N), BF16), pltpu.SemaphoreType.DMA((heads,))],
        3 << 30,
    )(place, g, betas, decays, entry, k, p, y, t, o)


def delta_source(place, g, betas, decays, k, p, t, attended):
    heads, rows = decays.shape
    count = rows // C
    block, square = per_head((count, N, N)), shaped((heads, count, N, N))
    return call(
        functools.partial(source_kernel, heads, count), "delta_source", heads,
        [SCALAR, full(g.shape), full(betas.shape), full(decays.shape)] + [block] * 3 + [ANY] * heads,
        [shaped((heads, count, C, N)), square, square, shaped((heads, N, N))],
        [per_head((count, C, N)), block, block, per_head((N, N))],
        [pltpu.VMEM(g.shape, F32), pltpu.VMEM((heads, rows, N), BF16), pltpu.SemaphoreType.DMA((heads,))],
        3 << 30,
    )(place, g, betas, decays, k, p, t, *attended)


def delta_final(betas, decays, lam, k, inv, t, aux, s, u, dw, dq, q, z, b):
    heads, rows = decays.shape
    count = rows // C
    block = per_head((count, N, N))
    thin = per_head((count, C, N))
    wide = (2 * rows * heads, N)
    return call(
        functools.partial(final_kernel, heads, count), "delta_final", heads,
        [full(betas.shape), full(decays.shape), per_head((N, N)), block, block, block,
         per_head((count, 8, N)), per_head((count + 1, N, N)), block, thin, thin, thin, block, block],
        [shaped(wide, BF16), shaped(wide, BF16), shaped(betas.shape), shaped(decays.shape)],
        [full(wide), full(wide), full(betas.shape), full(decays.shape)],
        [pltpu.VMEM(wide, F32)] * 2,
        8 << 30,
    )(betas, decays, lam, k, inv, t, aux, s, u, dw, dq, q, z, b)


def rounds(refs, index, count, sign):
    return [lax.rem(index + (s if sign > 0 else count - s), count) for s in range(count)]


def send_kernel(count, place_ref, q_ref, k_ref, v_ref, *rest):
    outs, (scr,) = rest[:count], rest[count:]
    heads = count
    rows = q_ref.shape[0] // heads
    for m, ref in enumerate((q_ref, k_ref, v_ref)):
        scr[...] = ref[...].astype(F32)
        for s in range(count):
            head = lax.rem(place_ref[0] + s, count)
            outs[s][m] = scr[pl.ds(head, rows, stride=heads), :].astype(BF16)


def take_kernel(count, place_ref, *rest):
    ins, outs, (scr,) = rest[:count], rest[count:count + 3], rest[count + 3:]
    heads = count
    rows = outs[0].shape[0] // heads
    for m in range(3):
        for s in range(count):
            head = lax.rem(place_ref[0] + count - s, count)
            scr[pl.ds(head, rows, stride=heads), :] = ins[s][m].astype(F32)
        outs[m][...] = scr[...].astype(BF16)


def gather_blocks(place_ref, refs, scr, sem, first):
    copies = []
    count = len(refs)
    for s in range(count):
        source = lax.rem(place_ref[0] + count - s, count)
        copies.append(pltpu.make_async_copy(refs[s], scr.at[source], sem.at[first + s]))
    return copies


def scatter_blocks(place_ref, scr, refs, sem, first):
    copies = []
    count = len(refs)
    for s in range(count):
        target = lax.rem(place_ref[0] + s, count)
        copies.append(pltpu.make_async_copy(scr.at[target], refs[s], sem.at[first + s]))
    return copies


def attend_kernel(count, scale, place_ref, *rest):
    ins, (prob_ref, mixed_ref), outs = rest[:count], rest[count:count + 2], rest[count + 2:2 * count + 2]
    scr, att_scr, sem = rest[2 * count + 2:]
    copies = gather_blocks(place_ref, ins, scr, sem, 0)
    for copy in copies:
        copy.start()
    for copy in copies:
        copy.wait()
    rows = scr.shape[2]
    causal = iota((rows, rows), 0) <= iota((rows, rows), 1)
    for i in range(count):
        query = scr[i, 0]
        pieces = []
        for j in range(i + 1):
            score = contract(scr[j, 1], query, 1, 1) * scale
            pieces.append(jnp.where(causal, score, -jnp.inf) if j == i else score)
        top = pieces[0].max(axis=0, keepdims=True)
        for piece in pieces[1:]:
            top = jnp.maximum(top, piece.max(axis=0, keepdims=True))
        pieces = [jnp.exp(piece - top) for piece in pieces]
        total = pieces[0].sum(axis=0, keepdims=True)
        for piece in pieces[1:]:
            total = total + piece.sum(axis=0, keepdims=True)
        mixed = None
        for j, piece in enumerate(pieces):
            low = (piece / total).astype(BF16)
            prob_ref[i * (i + 1) // 2 + j] = low
            term = contract(low, scr[j, 2], 0, 0)
            mixed = term if mixed is None else mixed + term
        mixed_ref[i] = mixed
        att_scr[i] = mixed.astype(BF16)
    copies = scatter_blocks(place_ref, att_scr, outs, sem, 0)
    for copy in copies:
        copy.start()
    for copy in copies:
        copy.wait()


def attend_back_kernel(count, scale, place_ref, prob_ref, mixed_ref, *rest):
    ins, grads, outs = rest[:count], rest[count:2 * count], rest[2 * count:3 * count]
    scr, g_scr, out_scr, acc, sem = rest[3 * count:]
    copies = gather_blocks(place_ref, ins, scr, sem, 0) + gather_blocks(place_ref, grads, g_scr, sem, count)
    for copy in copies:
        copy.start()
    for copy in copies:
        copy.wait()
    rows = scr.shape[2]
    ones = jnp.ones((8, N), F32)
    for i in range(count):
        mixed = mixed_ref[i]
        low = mixed.astype(BF16).astype(F32)
        grad = g_scr[i].astype(F32)
        inv = lax.rsqrt(jnp.mean(low * low, axis=1, keepdims=True) + EPS)
        pull = inv * (grad - low * (inv * inv * jnp.mean(low * grad, axis=1, keepdims=True)))
        pull = pull.astype(BF16)
        dots = mm_nt(ones, pull.astype(F32) * mixed)[:1]
        query = scr[i, 0]
        gq = None
        for j in range(i + 1):
            prob = prob_ref[i * (i + 1) // 2 + j]
            gp = contract(scr[j, 2], pull, 1, 1)
            gs = (prob.astype(F32) * (gp - dots) * scale).astype(BF16)
            term = contract(gs, scr[j, 1], 0, 0)
            gq = term if gq is None else gq + term
            gk = contract(gs, query, 1, 0)
            gv = contract(prob, pull, 1, 0)
            if i == j:
                acc[j, 0] = gk
                acc[j, 1] = gv
            else:
                acc[j, 0] = acc[j, 0] + gk
                acc[j, 1] = acc[j, 1] + gv
        out_scr[i, 0] = gq.astype(BF16)
    for j in range(count):
        out_scr[j, 1] = acc[j, 0].astype(BF16)
        out_scr[j, 2] = acc[j, 1].astype(BF16)
    copies = scatter_blocks(place_ref, out_scr, outs, sem, 0)
    for copy in copies:
        copy.start()
    for copy in copies:
        copy.wait()


VM = pl.BlockSpec(memory_space=pltpu.VMEM)


def single(body, name, in_specs, outs, out_specs, scratch, flops):
    return pl.pallas_call(
        body,
        name=name,
        in_specs=in_specs,
        out_shape=outs,
        out_specs=out_specs,
        scratch_shapes=scratch,
        compiler_params=pltpu.CompilerParams(vmem_limit_bytes=LIMIT),
        cost_estimate=pl.CostEstimate(flops=flops, bytes_accessed=4 << 20, transcendentals=0),
    )


def send_heads(place, q, k, v, count):
    rows = q.shape[0] // count
    return single(
        functools.partial(send_kernel, count), "send_heads",
        [SCALAR, VM, VM, VM], [shaped((3, rows, N), BF16)] * count, [VM] * count,
        [pltpu.VMEM(q.shape, F32)], 1 << 28,
    )(place, q, k, v)


def take_heads(place, parts):
    count = len(parts)
    rows = parts[0].shape[1]
    wide = (rows * count, N)
    return single(
        functools.partial(take_kernel, count), "take_heads",
        [SCALAR] + [VM] * count, [shaped(wide, BF16)] * 3, [VM] * 3,
        [pltpu.VMEM(wide, F32)], 1 << 28,
    )(place, *parts)


def attend(place, parts, scale):
    count = len(parts)
    rows = parts[0].shape[1]
    tri = count * (count + 1) // 2
    return single(
        functools.partial(attend_kernel, count, scale), "attend",
        [SCALAR] + [ANY] * count,
        [shaped((tri, rows, rows), BF16), shaped((count, rows, N))] + [shaped((rows, N), BF16)] * count,
        [VM, VM] + [ANY] * count,
        [pltpu.VMEM((count, 3, rows, N), BF16), pltpu.VMEM((count, rows, N), BF16),
         pltpu.SemaphoreType.DMA((count,))], 2 << 30,
    )(place, *parts)


def attend_back(place, prob, mixed, parts, grads, scale):
    count = len(parts)
    rows = parts[0].shape[1]
    return single(
        functools.partial(attend_back_kernel, count, scale), "attend_back",
        [SCALAR, VM, VM] + [ANY] * (2 * count),
        [shaped((3, rows, N), BF16)] * count, [ANY] * count,
        [pltpu.VMEM((count, 3, rows, N), BF16), pltpu.VMEM((count, rows, N), BF16),
         pltpu.VMEM((count, 3, rows, N), BF16), pltpu.VMEM((count, 2, rows, N), F32),
         pltpu.SemaphoreType.DMA((2 * count,))], 4 << 30,
    )(place, prob, mixed, *parts, *grads)


PRECISE = lax.Precision.HIGHEST


def shifted(value, axis, steps):
    count = lax.axis_size(axis)
    initial, last = (max(0, -steps), min(count, count - steps))
    return lax.ppermute(value, axis, [(source, source + steps) for source in range(initial, last)])


def rotated(parts, axis):
    count = len(parts)
    moved = [parts[0]]
    for s in range(1, count):
        moved.append(lax.ppermute(parts[s], axis, [(d, (d + s) % count) for d in range(count)]))
    return moved


def apply_map(matrix, state):
    return jnp.einsum("hij,hjk->hik", matrix, state, precision=PRECISE)


def entering(matrix, offset, axis, step):
    count = lax.axis_size(axis)
    if count <= 4:
        state = shifted(offset.astype(BF16), axis, step)
        for hop in range(count - 2):
            state = shifted((apply_map(matrix, state.astype(F32)) + offset).astype(BF16), axis, step)
        return state
    place = lax.axis_index(axis)
    place = place if step > 0 else count - 1 - place
    eye = jnp.eye(matrix.shape[-1], dtype=F32)
    reach = 1
    while reach < count:
        before, start = (shifted(matrix, axis, step * reach), shifted(offset, axis, step * reach))
        before = before + jnp.where(place < reach, eye, 0.0)
        offset = apply_map(matrix, start) + offset
        matrix = apply_map(matrix, before)
        reach *= 2
    return shifted(offset, axis, step).astype(BF16)


def visible_pairs(rows, span):
    relative = jnp.arange((span + 1) * rows, dtype=jnp.int32) - span * rows
    local = jnp.arange(rows, dtype=jnp.int32)
    return (
        (relative[None, :] <= local[:, None])
        & (relative[None, :] > local[:, None] - WINDOW)
        & (lax.axis_index("seq") * rows + relative[None, :] >= 0)
    )


def window_forward(queries, keys, values, scale):
    rows = queries.shape[0]
    span = -(-WINDOW // rows)
    couple = jnp.stack([keys, values])
    earlier = [shifted(couple, "seq", step + 1) for step in range(min(span, lax.axis_size("seq") - 1))]
    span = len(earlier)
    ordered = earlier[::-1] + [couple]
    window_keys = jnp.concatenate([piece[0] for piece in ordered], axis=0)
    window_values = jnp.concatenate([piece[1] for piece in ordered], axis=0)
    visible = visible_pairs(rows, span)
    scores = jnp.einsum("qhe,khe->hqk", queries, window_keys, preferred_element_type=F32) * scale
    top = jnp.max(jnp.where(visible, scores, -jnp.inf), axis=-1)
    lifted = jnp.where(visible, jnp.exp(jnp.where(visible, scores - top[:, :, None], 0.0)), 0.0)
    attention = lifted / jnp.sum(lifted, axis=-1)[:, :, None]
    mixed = jnp.einsum(
        "hqk,khe->qhe", attention.astype(BF16), window_values, preferred_element_type=F32
    )
    return window_keys, window_values, attention, mixed, span


def window_backward(queries, window_keys, window_values, attention, mixed, span, unit_grad, scale):
    rows = queries.shape[0]
    low = mixed.astype(BF16).astype(F32)
    grad = unit_grad.astype(F32)
    inv = lax.rsqrt(jnp.mean(low * low, axis=-1, keepdims=True) + EPS)
    pull = inv * (grad - low * (inv * inv * jnp.mean(low * grad, axis=-1, keepdims=True)))
    pull = pull.astype(BF16)
    row_dots = jnp.sum(pull.astype(F32) * mixed, axis=-1).T
    grad_attention = jnp.einsum("qhe,khe->hqk", pull, window_values, preferred_element_type=F32)
    grad_scores = (attention * (grad_attention - row_dots[:, :, None]) * scale).astype(BF16)
    grad_queries = jnp.einsum(
        "hqk,khe->qhe", grad_scores, window_keys, preferred_element_type=F32
    ).astype(BF16)
    key_parts = jnp.einsum("hqk,qhe->khe", grad_scores, queries, preferred_element_type=F32)
    value_parts = jnp.einsum("hqk,qhe->khe", attention.astype(BF16), pull, preferred_element_type=F32)
    gathered = jnp.stack([key_parts[span * rows:], value_parts[span * rows:]])
    for later in range(1, span + 1):
        first = (span - later) * rows
        piece = jnp.stack([key_parts[first:first + rows], value_parts[first:first + rows]])
        gathered = gathered + shifted(piece, "seq", -later)
    return grad_queries, gathered[0].astype(BF16), gathered[1].astype(BF16)


def body(queries, keys, values, delta_keys, delta_values, betas, decays, grad_out):
    rows, heads, width = queries.shape
    scale = 1.0 / math.sqrt(width)
    count = lax.axis_size("seq")
    by_head = heads == count and WINDOW >= count * rows

    def flat(array):
        return array.reshape(-1, width)

    place = lax.axis_index("seq").astype(jnp.int32).reshape(1) if by_head else jnp.zeros((1,), jnp.int32)
    if by_head:
        parts = rotated(send_heads(place, flat(queries), flat(keys), flat(values), count), "seq")
    cot = flat(grad_out)
    k, inverse, p, y, t, o, aux, shard_map, shard_offset = delta_local(
        flat(delta_keys), flat(delta_values), betas, decays
    )
    entry = entering(shard_map, shard_offset, "seq", 1)
    if by_head:
        prob, mixed, *attended = attend(place, parts, scale)
        attended = rotated(attended, "seq")
    else:
        saved = window_forward(queries, keys, values, scale)
        low = saved[3].astype(BF16)
        attended = [low[:, (heads - s) % heads] for s in range(heads)]
    s, u, dw, dq, *pulls = delta_readout(place, cot, betas, decays, entry, k, p, y, t, o)
    if by_head:
        pulls = rotated(pulls, "seq")
        outs = rotated(attend_back(place, prob, mixed, parts, pulls, scale), "seq")
        grads = [array.reshape(rows, heads, width) for array in take_heads(place, outs)]
    else:
        grads = window_backward(queries, *saved, jnp.stack(pulls, axis=1), scale)
    q, z, b, shard_source = delta_source(place, cot, betas, decays, k, p, t, attended)
    leaving = entering(jnp.swapaxes(shard_map, 1, 2), shard_source, "seq", -1)
    grad_keys, grad_values, grad_betas, grad_decays = delta_final(
        betas, decays, leaving, k, inverse, t, aux, s, u, dw, dq, q, z, b
    )
    pair = (rows, 2, heads, width)
    return (*grads, grad_keys.reshape(pair), grad_values.reshape(pair), grad_betas, grad_decays)


def solution(mesh):
    row = P(("parts", "seq"), "head", None)
    pair = P(("parts", "seq"), None, "head", None)
    beta = P(None, "head", ("parts", "seq"))
    decay = P("head", ("parts", "seq"))
    return jax.shard_map(
        body,
        mesh=mesh,
        in_specs=(row, row, row, pair, pair, beta, decay, row),
        out_specs=(row, row, row, pair, pair, beta, decay),
        check_vma=False,
    )
```

time: 1260 us -> 138 us (0.11)
  the two profiles are of different devices: /device:TPU:0 before, /device:TPU:9 now
where the time goes in v1:
time: 138 us
  Pallas kernels  69.3 us (50%)
  waiting for transfers between devices  32.2 us (23%)
  starting transfers between devices  28.1 us (20%)
  local copies, waits for them, and re-layouts  3.93 us (3%)
  other arithmetic  2.01 us (1%)
    ppermute x12, waiting for transfers between devices, rotated(): lax.ppermute(parts[s], axis, [(d, (d + s) % count) for d in range(count)])  32.2 us
    ppermute x6, starting transfers between devices, shifted(): lax.ppermute(value, axis, [(source, source + steps) for source in range(i...  17.8 us
    pallas_call x1, Pallas kernels, delta_final(): call(functools.partial(final_kernel, heads, count), 'delta_final', heads,...  17.1 us
    pallas_call x1, Pallas kernels, delta_local(): call(functools.partial(local_kernel, heads, count), 'delta_local', heads,...  16.2 us
    ppermute x12, starting transfers between devices, rotated(): lax.ppermute(parts[s], axis, [(d, (d + s) % count) for d in range(count)])  10.3 us
    pallas_call x1, Pallas kernels, delta_source(): call(functools.partial(source_kernel, heads, count), 'delta_source', head...  10 us
    pallas_call x1, Pallas kernels, delta_readout(): call(functools.partial(readout_kernel, heads, count), 'delta_readout', he...  9.02 us
    pallas_call x1, Pallas kernels, attend_back(): single(functools.partial(attend_back_kernel, count, scale), 'attend_back'...  7.13 us
  transfers between devices with their start and end apart: 18, of which 5 were waited for; matrix products, arithmetic and copies ran while one was open for 2% of the time, Pallas kernels for 26%

profile of v1, /device:TPU:9, one launch (start us, length us, event | category | flops | bytes accessed | tf_op | source)
XLA Modules:
  0.0 137.9 jit_solution(14995861360678475360)
XLA Ops:
  0.6 16.2 %delta_local.1 = (f32[4,4,128,128]{3,2,1,0:T(8,128)}, f32[4,4,128,128]{3,2,1,0:T(8,128)}, f32[4,4,128,128]{3,2,1,0:T(8,128)}, f32[4,4,128,128]{3,2,1,0:T(8,128)}...) custom-call(bf16[2048,128]{1,0:T(8,128)(2,1)} %bitcast.20, ...), custom_call_target="tpu_custom_call" | custom-call | flops 10737418240 | bytes 8388608 | tf_op jit(solution)/shard_map/delta_local/pallas_call | solution.py:365
  17.9 3.2 %collective-permute-start.3 = (bf16[4,128,128]{2,1,0:T(8,128)(2,1)S(1)}, bf16[4,128,128]{2,1,0:T(8,128)(2,1)S(1)}, u32[]{:S(2)}, u32[]{:S(2)}) collective-permute-start(bf16[4,128,128]{2,1,0:T(8,128)(2,1)S(1)} %convert_element_type.22), channel_id=1, source_target_pairs={{0,4},{4,8},{8,12},{1,5},{5,9},{9,13},{2,6},{6,10},{10,14},{3,7},{... | collective-permute-start | bytes 393224 | tf_op jit(solution)/shard_map/ppermute | solution.py:618
  21.1 2.3 %send_heads.1 = (bf16[3,256,128]{2,1,0:T(8,128)(2,1)}, bf16[3,256,128]{2,1,0:T(8,128)(2,1)}, bf16[3,256,128]{2,1,0:T(8,128)(2,1)}, bf16[3,256,128]{2,1,0:T(8,128)(2,1)}) custom-call(s32[1]{0:T(128)} %bitcast.place_ref, bf16[1024,128]{1,0:T(8,128)(2,1)} %bitcast.22, bf16[1024,128]{1,0:T(8,128)(2,1)} %bitcast.23, bf16[1024,128]{1,0:T(8,128)(2,1)} %bitcast.24), custom_call_target="tpu_custom_call" | custom-call | flops 268435456 | bytes 4194304 | tf_op jit(solution)/shard_map/send_heads/pallas_call | solution.py:567
  23.4 1.3 collective-permute-start
  26.1 3.1 %collective-permute-start.4 = (bf16[4,128,128]{2,1,0:T(8,128)(2,1)S(1)}, bf16[4,128,128]{2,1,0:T(8,128)(2,1)S(1)}, u32[]{:S(2)}, u32[]{:S(2)}) collective-permute-start(bf16[4,128,128]{2,1,0:T(8,128)(2,1)S(1)} %fusion), channel_id=1, source_target_pairs={{0,4},{4,8},{8,12},{1,5},{5,9},{9,13},{2,6},{6,10},{10,14},{3,7},{... | collective-permute-start | bytes 393224 | tf_op jit(solution)/shard_map/ppermute | solution.py:618
  29.3 11.6 %collective-permute-done.1.rest_2_ = bf16[3,256,128]{2,1,0:T(8,128)(2,1)S(1)} collective-permute-done((bf16[3,256,128]{2,1,0:T(8,128)(2,1)}, bf16[3,256,128]{2,1,0:T(8,128)(2,1)S(1)}, u32[]{:S(2)}, u32[]{:S(2)}) %collective-permute-start.1) | collective-permute-done | bytes 196640 | tf_op jit(solution)/shard_map/ppermute | solution.py:625
  40.9 3.0 %collective-permute-done.2.rest_3_ = bf16[3,256,128]{2,1,0:T(8,128)(2,1)S(1)} collective-permute-done((bf16[3,256,128]{2,1,0:T(8,128)(2,1)}, bf16[3,256,128]{2,1,0:T(8,128)(2,1)S(1)}, u32[]{:S(2)}, u32[]{:S(2)}) %collective-permute-start.2) | collective-permute-done | bytes 196640 | tf_op jit(solution)/shard_map/ppermute | solution.py:625
  44.5 5.3 %attend.1 = (bf16[10,256,256]{2,1,0:T(8,128)(2,1)}, f32[4,256,128]{2,1,0:T(8,128)}, bf16[256,128]{1,0:T(8,128)(2,1)}, bf16[256,128]{1,0:T(8,128)(2,1)}, bf16[256...) custom-call(s32[1]{0:T(128)} %bitcast.place_ref, bf16[3,256,128]{2,1,0:T(8,128)(2,1)} %get-tuple-element.49.rest_0_, ...), custom_call_target="tpu_custom_call" | custom-call | flops 2147483648 | bytes 4194304 | tf_op jit(solution)/shard_map/attend/pallas_call | solution.py:589
  50.0 1.4 %collective-permute-start.14 = (bf16[256,128]{1,0:T(8,128)(2,1)}, bf16[256,128]{1,0:T(8,128)(2,1)S(1)}, u32[]{:S(2)}, u32[]{:S(2)}) collective-permute-start(bf16[256,128]{1,0:T(8,128)(2,1)} %get-tuple-element.76), channel_id=1, source_target_pairs={{0,12},{4,0},{8,4},{12,8},{1,13},{5,1},{9,5},{13,9},{2,14},{6,2},{... | collective-permute-start | bytes 196616 | tf_op jit(solution)/shard_map/ppermute | solution.py:625
  51.7 3.0 %collective-permute-start.5 = (bf16[4,128,128]{2,1,0:T(8,128)(2,1)S(1)}, bf16[4,128,128]{2,1,0:T(8,128)(2,1)S(1)}, u32[]{:S(2)}, u32[]{:S(2)}) collective-permute-start(bf16[4,128,128]{2,1,0:T(8,128)(2,1)S(1)} %fusion.1), channel_id=1, source_target_pairs={{0,4},{4,8},{8,12},{1,5},{5,9},{9,13},{2,6},{6,10},{10,14},{3,7},{... | collective-permute-start | bytes 393224 | tf_op jit(solution)/shard_map/ppermute | solution.py:618
  54.7 3.4 %collective-permute-done.14.rest_3_ = bf16[256,128]{1,0:T(8,128)(2,1)S(1)} collective-permute-done((bf16[256,128]{1,0:T(8,128)(2,1)}, bf16[256,128]{1,0:T(8,128)(2,1)S(1)}, u32[]{:S(2)}, u32[]{:S(2)}) %collective-permute-start.14) | collective-permute-done | bytes 65568 | tf_op jit(solution)/shard_map/ppermute | solution.py:625
  58.7 10.0 %delta_source.1 = (f32[4,4,64,128]{3,2,1,0:T(8,128)}, f32[4,4,128,128]{3,2,1,0:T(8,128)}, f32[4,4,128,128]{3,2,1,0:T(8,128)}, f32[4,128,128]{2,1,0:T(8,128)}) custom-call(s32[1]{0:T(128)} %bitcast.place_ref, bf16[1024,128]{1,0:T(8,128)(2,1)} %bitcast.25, f32[2,4,256]{2,1,0:T(4,128)} %betas_ref.7, f32[4,256]{1,0:T(4,128)} %decays_ref.7, ...), custom_call_target="tpu_custom_call" | custom-call | flops 3221225472 | bytes 8388608 | tf_op jit(solution)/shard_map/delta_source/pallas_call | solution.py:395
  69.8 1.9 %collective-permute-start.15 = (bf16[4,128,128]{2,1,0:T(8,128)(2,1)S(1)}, bf16[4,128,128]{2,1,0:T(8,128)(2,1)S(1)}, u32[]{:S(2)}, u32[]{:S(2)}) collective-permute-start(bf16[4,128,128]{2,1,0:T(8,128)(2,1)S(1)} %convert_element_type.25), channel_id=1, source_target_pairs={{4,0},{8,4},{12,8},{5,1},{9,5},{13,9},{6,2},{10,6},{14,10},{7,3},{... | collective-permute-start | bytes 393224 | tf_op jit(solution)/shard_map/ppermute | solution.py:618
  72.4 9.0 %delta_readout.1 = (f32[4,5,128,128]{3,2,1,0:T(8,128)}, f32[4,4,128,128]{3,2,1,0:T(8,128)}, f32[4,4,64,128]{3,2,1,0:T(8,128)}, f32[4,4,64,128]{3,2,1,0:T(8,128)}...) custom-call(s32[1]{0:T(128)} %bitcast.place_ref, ...), custom_call_target="tpu_custom_call" | custom-call | flops 3221225472 | bytes 8388608 | tf_op jit(solution)/shard_map/delta_readout/pallas_call | solution.py:380
  81.4 1.5 %collective-permute-start.6 = (bf16[256,128]{1,0:T(8,128)(2,1)}, bf16[256,128]{1,0:T(8,128)(2,1)S(1)}, u32[]{:S(2)}, u32[]{:S(2)}) collective-permute-start(bf16[256,128]{1,0:T(8,128)(2,1)} %get-tuple-element.63), channel_id=1, source_target_pairs={{0,4},{4,8},{8,12},{12,0},{1,5},{5,9},{9,13},{13,1},{2,6},{6,10},{... | collective-permute-start | bytes 196616 | tf_op jit(solution)/shard_map/ppermute | solution.py:625
  84.6 4.4 %collective-permute-start.16 = (bf16[4,128,128]{2,1,0:T(8,128)(2,1)S(1)}, bf16[4,128,128]{2,1,0:T(8,128)(2,1)S(1)}, u32[]{:S(2)}, u32[]{:S(2)}) collective-permute-start(bf16[4,128,128]{2,1,0:T(8,128)(2,1)S(1)} %fusion.2), channel_id=1, source_target_pairs={{4,0},{8,4},{12,8},{5,1},{9,5},{13,9},{6,2},{10,6},{14,10},{7,3},{... | collective-permute-start | bytes 393224 | tf_op jit(solution)/shard_map/ppermute | solution.py:618
  89.7 7.1 %attend_back.1 = (bf16[3,256,128]{2,1,0:T(8,128)(2,1)}, bf16[3,256,128]{2,1,0:T(8,128)(2,1)}, bf16[3,256,128]{2,1,0:T(8,128)(2,1)}, bf16[3,256,128]{2,1,0:T(8,128)(2,1)}) custom-call(s32[1]{0:T(128)} %bitcast.place_ref, bf16[10,256,256]{2,1,0:T(8,128)(2,1)} %get-tuple-element.53.prob_ref, f32[4,256,128]{2,1,0:T(8,128)} %get-tuple-element.54.mixed_ref, ...), custom_call_target="tpu_custom_call" | custom-call | flops 4294967296 | bytes 4194304 | tf_op jit(solution)/shard_map/attend_back/pallas_call | solution.py:602
  96.9 2.0 %collective-permute-start.10 = (bf16[3,256,128]{2,1,0:T(8,128)(2,1)}, bf16[3,256,128]{2,1,0:T(8,128)(2,1)S(1)}, u32[]{:S(2)}, u32[]{:S(2)}) collective-permute-start(bf16[3,256,128]{2,1,0:T(8,128)(2,1)} %get-tuple-element.68), channel_id=1, source_target_pairs={{0,8},{4,12},{8,0},{12,4},{1,9},{5,13},{9,1},{13,5},{2,10},{6,14},... | collective-permute-start | bytes 589832 | tf_op jit(solution)/shard_map/ppermute | solution.py:625
  98.8 1.4 %collective-permute-start.11 = (bf16[3,256,128]{2,1,0:T(8,128)(2,1)}, bf16[3,256,128]{2,1,0:T(8,128)(2,1)S(1)}, u32[]{:S(2)}, u32[]{:S(2)}) collective-permute-start(bf16[3,256,128]{2,1,0:T(8,128)(2,1)} %get-tuple-element.69), channel_id=1, source_target_pairs={{0,12},{4,0},{8,4},{12,8},{1,13},{5,1},{9,5},{13,9},{2,14},{6,2},{... | collective-permute-start | bytes 589832 | tf_op jit(solution)/shard_map/ppermute | solution.py:625
  100.6 2.1 %collective-permute-start.17 = (bf16[4,128,128]{2,1,0:T(8,128)(2,1)S(1)}, bf16[4,128,128]{2,1,0:T(8,128)(2,1)S(1)}, u32[]{:S(2)}, u32[]{:S(2)}) collective-permute-start(bf16[4,128,128]{2,1,0:T(8,128)(2,1)S(1)} %fusion.3), channel_id=1, source_target_pairs={{4,0},{8,4},{12,8},{5,1},{9,5},{13,9},{6,2},{10,6},{14,10},{7,3},{... | collective-permute-start | bytes 393224 | tf_op jit(solution)/shard_map/ppermute | solution.py:618
  102.8 2.4 %collective-permute-done.10.rest_2_ = bf16[3,256,128]{2,1,0:T(8,128)(2,1)S(1)} collective-permute-done((bf16[3,256,128]{2,1,0:T(8,128)(2,1)}, bf16[3,256,128]{2,1,0:T(8,128)(2,1)S(1)}, u32[]{:S(2)}, u32[]{:S(2)}) %collective-permute-start.10) | collective-permute-done | bytes 196640 | tf_op jit(solution)/shard_map/ppermute | solution.py:625
  105.2 11.8 %collective-permute-done.11.rest_3_ = bf16[3,256,128]{2,1,0:T(8,128)(2,1)S(1)} collective-permute-done((bf16[3,256,128]{2,1,0:T(8,128)(2,1)}, bf16[3,256,128]{2,1,0:T(8,128)(2,1)S(1)}, u32[]{:S(2)}, u32[]{:S(2)}) %collective-permute-start.11) | collective-permute-done | bytes 196640 | tf_op jit(solution)/shard_map/ppermute | solution.py:625
  117.7 2.3 %take_heads.1 = (bf16[1024,128]{1,0:T(8,128)(2,1)}, bf16[1024,128]{1,0:T(8,128)(2,1)}, bf16[1024,128]{1,0:T(8,128)(2,1)}) custom-call(s32[1]{0:T(128)} %bitcast.place_ref, bf16[3,256,128]{2,1,0:T(8,128)(2,1)} %get-tuple-element.66.rest_0_, bf16[3,256,128]{2,1,0:T(8,128)(2,1)} %copy-done.6, bf16[3,256,128]{2,1,0:T(8,128)(2,1)} %copy-done.7, ...), custom_call_target="tpu_custom_call" | custom-call | flops 268435456 | bytes 4194304 | tf_op jit(solution)/shard_map/take_heads/pallas_call | solution.py:578
  120.6 17.1 %delta_final.1 = (bf16[2048,128]{1,0:T(8,128)(2,1)}, bf16[2048,128]{1,0:T(8,128)(2,1)}, f32[2,4,256]{2,1,0:T(4,128)}, f32[4,256]{1,0:T(4,128)}) custom-call(f32[2,4,256]{2,1,0:T(4,128)} %betas_ref.7, f32[4,256]{1,0:T(4,128)} %decays_ref.7, bf16[4,128,128]{2,1,0:T(8,128)(2,1)} %copy-done.9, f32[4,4,128,128]{3,2,1,0:T(8,128)} %get-tuple-element.57.k_ref, ...), custom_call_target="tpu_custom_call" | custom-call | flops 8589934592 | bytes 8388608 | tf_op jit(solution)/shard_map/delta_final/pallas_call | solution.py:411
  (60 shorter events, 9.9 us)
Async XLA Ops:
  16.8 9.0 %copy-start = (f32[4,128,128]{2,1,0:T(8,128)S(1)}, f32[4,128,128]{2,1,0:T(8,128)}, u32[]{:S(2)}) copy-start(f32[4,128,128]{2,1,0:T(8,128)} %get-tuple-element.55) | copy-start | bytes 786436
  16.8 9.0 %copy-start.2 = (f32[4,128,128]{2,1,0:T(8,128)S(1)}, f32[4,128,128]{2,1,0:T(8,128)}, u32[]{:S(2)}) copy-start(f32[4,128,128]{2,1,0:T(8,128)} %get-tuple-element.56) | copy-start | bytes 786436
  17.9 8.0 %collective-permute-start.3 = (bf16[4,128,128]{2,1,0:T(8,128)(2,1)S(1)}, bf16[4,128,128]{2,1,0:T(8,128)(2,1)S(1)}, u32[]{:S(2)}, u32[]{:S(2)}) collective-permute-start(bf16[4,128,128]{2,1,0:T(8,128)(2,1)S(1)} %convert_element_type.22), channel_id=1, source_target_pairs={{0,4},{4,8},{8,12},{1,5},{5,9},{9,13},{2,6},{6,10},{10,14},{3,7},{... | collective-permute-start | bytes 393224 | tf_op jit(solution)/shard_map/ppermute | solution.py:618
  23.4 5.9 %collective-permute-start = (bf16[3,256,128]{2,1,0:T(8,128)(2,1)}, bf16[3,256,128]{2,1,0:T(8,128)(2,1)S(1)}, u32[]{:S(2)}, u32[]{:S(2)}) collective-permute-start(bf16[3,256,128]{2,1,0:T(8,128)(2,1)} %get-tuple-element.50), channel_id=1, source_target_pairs={{0,4},{4,8},{8,12},{12,0},{1,5},{5,9},{9,13},{13,1},{2,6},{6,10},{... | collective-permute-start | bytes 589832 | tf_op jit(solution)/shard_map/ppermute | solution.py:625
  24.7 16.2 %collective-permute-start.1 = (bf16[3,256,128]{2,1,0:T(8,128)(2,1)}, bf16[3,256,128]{2,1,0:T(8,128)(2,1)S(1)}, u32[]{:S(2)}, u32[]{:S(2)}) collective-permute-start(bf16[3,256,128]{2,1,0:T(8,128)(2,1)} %get-tuple-element.51), channel_id=1, source_target_pairs={{0,8},{4,12},{8,0},{12,4},{1,9},{5,13},{9,1},{13,5},{2,10},{6,14},... | collective-permute-start | bytes 589832 | tf_op jit(solution)/shard_map/ppermute | solution.py:625
  25.6 18.2 %collective-permute-start.2 = (bf16[3,256,128]{2,1,0:T(8,128)(2,1)}, bf16[3,256,128]{2,1,0:T(8,128)(2,1)S(1)}, u32[]{:S(2)}, u32[]{:S(2)}) collective-permute-start(bf16[3,256,128]{2,1,0:T(8,128)(2,1)} %get-tuple-element.52), channel_id=1, source_target_pairs={{0,12},{4,0},{8,4},{12,8},{1,13},{5,1},{9,5},{13,9},{2,14},{6,2},{... | collective-permute-start | bytes 589832 | tf_op jit(solution)/shard_map/ppermute | solution.py:625
  26.1 25.3 %collective-permute-start.4 = (bf16[4,128,128]{2,1,0:T(8,128)(2,1)S(1)}, bf16[4,128,128]{2,1,0:T(8,128)(2,1)S(1)}, u32[]{:S(2)}, u32[]{:S(2)}) collective-permute-start(bf16[4,128,128]{2,1,0:T(8,128)(2,1)S(1)} %fusion), channel_id=1, source_target_pairs={{0,4},{4,8},{8,12},{1,5},{5,9},{9,13},{2,6},{6,10},{10,14},{3,7},{... | collective-permute-start | bytes 393224 | tf_op jit(solution)/shard_map/ppermute | solution.py:618
  29.3 14.6 %copy-start.3 = (bf16[3,256,128]{2,1,0:T(8,128)(2,1)}, bf16[3,256,128]{2,1,0:T(8,128)(2,1)S(1)}, u32[]{:S(2)}) copy-start(bf16[3,256,128]{2,1,0:T(8,128)(2,1)S(1)} %collective-permute-done.rest_1_) | copy-start | bytes 589828
  49.8 4.9 %collective-permute-start.12 = (bf16[256,128]{1,0:T(8,128)(2,1)}, bf16[256,128]{1,0:T(8,128)(2,1)S(1)}, u32[]{:S(2)}, u32[]{:S(2)}) collective-permute-start(bf16[256,128]{1,0:T(8,128)(2,1)} %get-tuple-element.74), channel_id=1, source_target_pairs={{0,4},{4,8},{8,12},{12,0},{1,5},{5,9},{9,13},{13,1},{2,6},{6,10},{... | collective-permute-start | bytes 196616 | tf_op jit(solution)/shard_map/ppermute | solution.py:625
  49.9 4.8 %collective-permute-start.13 = (bf16[256,128]{1,0:T(8,128)(2,1)}, bf16[256,128]{1,0:T(8,128)(2,1)S(1)}, u32[]{:S(2)}, u32[]{:S(2)}) collective-permute-start(bf16[256,128]{1,0:T(8,128)(2,1)} %get-tuple-element.75), channel_id=1, source_target_pairs={{0,8},{4,12},{8,0},{12,4},{1,9},{5,13},{9,1},{13,5},{2,10},{6,14},... | collective-permute-start | bytes 196616 | tf_op jit(solution)/shard_map/ppermute | solution.py:625
  50.0 8.1 %collective-permute-start.14 = (bf16[256,128]{1,0:T(8,128)(2,1)}, bf16[256,128]{1,0:T(8,128)(2,1)S(1)}, u32[]{:S(2)}, u32[]{:S(2)}) collective-permute-start(bf16[256,128]{1,0:T(8,128)(2,1)} %get-tuple-element.76), channel_id=1, source_target_pairs={{0,12},{4,0},{8,4},{12,8},{1,13},{5,1},{9,5},{13,9},{2,14},{6,2},{... | collective-permute-start | bytes 196616 | tf_op jit(solution)/shard_map/ppermute | solution.py:625
  51.7 20.0 %collective-permute-start.5 = (bf16[4,128,128]{2,1,0:T(8,128)(2,1)S(1)}, bf16[4,128,128]{2,1,0:T(8,128)(2,1)S(1)}, u32[]{:S(2)}, u32[]{:S(2)}) collective-permute-start(bf16[4,128,128]{2,1,0:T(8,128)(2,1)S(1)} %fusion.1), channel_id=1, source_target_pairs={{0,4},{4,8},{8,12},{1,5},{5,9},{9,13},{2,6},{6,10},{10,14},{3,7},{... | collective-permute-start | bytes 393224 | tf_op jit(solution)/shard_map/ppermute | solution.py:618
  69.8 14.4 %collective-permute-start.15 = (bf16[4,128,128]{2,1,0:T(8,128)(2,1)S(1)}, bf16[4,128,128]{2,1,0:T(8,128)(2,1)S(1)}, u32[]{:S(2)}, u32[]{:S(2)}) collective-permute-start(bf16[4,128,128]{2,1,0:T(8,128)(2,1)S(1)} %convert_element_type.25), channel_id=1, source_target_pairs={{4,0},{8,4},{12,8},{5,1},{9,5},{13,9},{6,2},{10,6},{14,10},{7,3},{... | collective-permute-start | bytes 393224 | tf_op jit(solution)/shard_map/ppermute | solution.py:618
  72.4 11.8 %copy-start.1 = (f32[4,128,128]{2,1,0:T(8,128)S(1)}, f32[4,128,128]{2,1,0:T(8,128)}, u32[]{:S(2)}) copy-start(f32[4,128,128]{2,1,0:T(8,128)} %get-tuple-element.77) | copy-start | bytes 786436
  81.4 7.6 %collective-permute-start.6 = (bf16[256,128]{1,0:T(8,128)(2,1)}, bf16[256,128]{1,0:T(8,128)(2,1)S(1)}, u32[]{:S(2)}, u32[]{:S(2)}) collective-permute-start(bf16[256,128]{1,0:T(8,128)(2,1)} %get-tuple-element.63), channel_id=1, source_target_pairs={{0,4},{4,8},{8,12},{12,0},{1,5},{5,9},{9,13},{13,1},{2,6},{6,10},{... | collective-permute-start | bytes 196616 | tf_op jit(solution)/shard_map/ppermute | solution.py:625
  82.9 6.1 %collective-permute-start.7 = (bf16[256,128]{1,0:T(8,128)(2,1)}, bf16[256,128]{1,0:T(8,128)(2,1)S(1)}, u32[]{:S(2)}, u32[]{:S(2)}) collective-permute-start(bf16[256,128]{1,0:T(8,128)(2,1)} %get-tuple-element.64), channel_id=1, source_target_pairs={{0,8},{4,12},{8,0},{12,4},{1,9},{5,13},{9,1},{13,5},{2,10},{6,14},... | collective-permute-start | bytes 196616 | tf_op jit(solution)/shard_map/ppermute | solution.py:625
  82.9 6.1 %collective-permute-start.8 = (bf16[256,128]{1,0:T(8,128)(2,1)}, bf16[256,128]{1,0:T(8,128)(2,1)S(1)}, u32[]{:S(2)}, u32[]{:S(2)}) collective-permute-start(bf16[256,128]{1,0:T(8,128)(2,1)} %get-tuple-element.65), channel_id=1, source_target_pairs={{0,12},{4,0},{8,4},{12,8},{1,13},{5,1},{9,5},{13,9},{2,14},{6,2},{... | collective-permute-start | bytes 196616 | tf_op jit(solution)/shard_map/ppermute | solution.py:625
  84.6 15.7 %collective-permute-start.16 = (bf16[4,128,128]{2,1,0:T(8,128)(2,1)S(1)}, bf16[4,128,128]{2,1,0:T(8,128)(2,1)S(1)}, u32[]{:S(2)}, u32[]{:S(2)}) collective-permute-start(bf16[4,128,128]{2,1,0:T(8,128)(2,1)S(1)} %fusion.2), channel_id=1, source_target_pairs={{4,0},{8,4},{12,8},{5,1},{9,5},{13,9},{6,2},{10,6},{14,10},{7,3},{... | collective-permute-start | bytes 393224 | tf_op jit(solution)/shard_map/ppermute | solution.py:618
  96.8 6.0 %collective-permute-start.9 = (bf16[3,256,128]{2,1,0:T(8,128)(2,1)}, bf16[3,256,128]{2,1,0:T(8,128)(2,1)S(1)}, u32[]{:S(2)}, u32[]{:S(2)}) collective-permute-start(bf16[3,256,128]{2,1,0:T(8,128)(2,1)} %get-tuple-element.67), channel_id=1, source_target_pairs={{0,4},{4,8},{8,12},{12,0},{1,5},{5,9},{9,13},{13,1},{2,6},{6,10},{... | collective-permute-start | bytes 589832 | tf_op jit(solution)/shard_map/ppermute | solution.py:625
  96.9 8.4 %collective-permute-start.10 = (bf16[3,256,128]{2,1,0:T(8,128)(2,1)}, bf16[3,256,128]{2,1,0:T(8,128)(2,1)S(1)}, u32[]{:S(2)}, u32[]{:S(2)}) collective-permute-start(bf16[3,256,128]{2,1,0:T(8,128)(2,1)} %get-tuple-element.68), channel_id=1, source_target_pairs={{0,8},{4,12},{8,0},{12,4},{1,9},{5,13},{9,1},{13,5},{2,10},{6,14},... | collective-permute-start | bytes 589832 | tf_op jit(solution)/shard_map/ppermute | solution.py:625
  98.8 18.2 %collective-permute-start.11 = (bf16[3,256,128]{2,1,0:T(8,128)(2,1)}, bf16[3,256,128]{2,1,0:T(8,128)(2,1)S(1)}, u32[]{:S(2)}, u32[]{:S(2)}) collective-permute-start(bf16[3,256,128]{2,1,0:T(8,128)(2,1)} %get-tuple-element.69), channel_id=1, source_target_pairs={{0,12},{4,0},{8,4},{12,8},{1,13},{5,1},{9,5},{13,9},{2,14},{6,2},{... | collective-permute-start | bytes 589832 | tf_op jit(solution)/shard_map/ppermute | solution.py:625
  100.6 19.3 %collective-permute-start.17 = (bf16[4,128,128]{2,1,0:T(8,128)(2,1)S(1)}, bf16[4,128,128]{2,1,0:T(8,128)(2,1)S(1)}, u32[]{:S(2)}, u32[]{:S(2)}) collective-permute-start(bf16[4,128,128]{2,1,0:T(8,128)(2,1)S(1)} %fusion.3), channel_id=1, source_target_pairs={{4,0},{8,4},{12,8},{5,1},{9,5},{13,9},{6,2},{10,6},{14,10},{7,3},{... | collective-permute-start | bytes 393224 | tf_op jit(solution)/shard_map/ppermute | solution.py:618
  102.8 14.2 %copy-start.6 = (bf16[3,256,128]{2,1,0:T(8,128)(2,1)}, bf16[3,256,128]{2,1,0:T(8,128)(2,1)S(1)}, u32[]{:S(2)}) copy-start(bf16[3,256,128]{2,1,0:T(8,128)(2,1)S(1)} %collective-permute-done.9.rest_1_) | copy-start | bytes 589828
  105.2 11.8 %copy-start.7 = (bf16[3,256,128]{2,1,0:T(8,128)(2,1)}, bf16[3,256,128]{2,1,0:T(8,128)(2,1)S(1)}, u32[]{:S(2)}) copy-start(bf16[3,256,128]{2,1,0:T(8,128)(2,1)S(1)} %collective-permute-done.10.rest_2_) | copy-start | bytes 589828
  (11 other events, 15.0 us)

commit v2 on v1

v2 whole, which is shorter than its diff:
```python
import functools, math
import jax
import jax.numpy as jnp
from jax import lax
from jax.experimental import pallas as pl
from jax.experimental.pallas import tpu as pltpu
from jax.sharding import PartitionSpec as P

WINDOW = 1024

F32 = jnp.float32
BF16 = jnp.bfloat16
EPS = 1e-06
C = 64
N = 128
LIMIT = 16 * 1024 * 1024


def split(a):
    high = a.astype(BF16)
    return high, (a - high.astype(F32)).astype(BF16)


def contract(a, b, ca, cb):
    return lax.dot_general(a, b, (((ca,), (cb,)), ((), ())), preferred_element_type=F32)


def mm(a, b):
    ah, al = split(a)
    bh, bl = split(b)
    wide = jnp.concatenate([bh, bl], axis=1)
    both = contract(jnp.concatenate([ah, al], axis=1), jnp.concatenate([wide, wide], axis=0), 1, 0)
    half = b.shape[1]
    return both[:, :half] + both[:, half:]


def mm_nt(a, b):
    ah, al = split(a)
    bh, bl = split(b)
    tall = jnp.concatenate([bh, bl], axis=0)
    both = contract(jnp.concatenate([ah, al], axis=1), jnp.concatenate([tall, tall], axis=1), 1, 1)
    half = b.shape[0]
    return both[:, :half] + both[:, half:]


def mm_tn(a, b):
    ah, al = split(a)
    bh, bl = split(b)
    wide = jnp.concatenate([bh, bl], axis=1)
    both = contract(jnp.concatenate([ah, al], axis=0), jnp.concatenate([wide, wide], axis=0), 0, 0)
    half = b.shape[1]
    return both[:, :half] + both[:, half:]


def low_nt(low, b):
    bh, bl = split(b)
    both = contract(low, jnp.concatenate([bh, bl], axis=0), 1, 1)
    half = b.shape[0]
    return both[:, :half] + both[:, half:]


def low_tn(a, low):
    ah, al = split(a)
    return contract(jnp.concatenate([ah, al], axis=0), jnp.concatenate([low, low], axis=0), 0, 0)


def iota(shape, axis):
    return lax.broadcasted_iota(jnp.int32, shape, axis)


class Grid:
    def __init__(self):
        self.row = iota((N, N), 0)
        self.lane = iota((N, N), 1)
        self.row_pos = self.row & (C - 1)
        self.lane_pos = self.lane & (C - 1)
        key_row = 2 * self.row_pos + (self.row >> 6)
        key_lane = 2 * self.lane_pos + (self.lane >> 6)
        self.strict = key_row > key_lane
        self.differ = key_row ^ key_lane
        self.diag = self.row == self.lane

    def to_row(self, column):
        return jnp.sum(jnp.where(self.diag, column, 0.0), axis=0, keepdims=True)

    def to_column(self, line):
        return jnp.sum(jnp.where(self.diag, line, 0.0), axis=1, keepdims=True)


def gates(grid, betas_ref, decays_ref, h, c):
    pair, half = c // 2, C * (c % 2)
    lanes = pl.ds(pair * N, N)
    first = betas_ref[0, pl.ds(h, 1), lanes]
    second = betas_ref[1, pl.ds(h, 1), lanes]
    logs = jnp.log(decays_ref[pl.ds(h, 1), lanes])
    offset = grid.lane - half
    chosen = jnp.where(grid.row < C, first, second)
    beta = jnp.sum(jnp.where(offset == grid.row_pos, chosen, 0.0), axis=1, keepdims=True)
    seen = (offset >= 0) & (offset <= grid.row_pos)
    run = jnp.sum(jnp.where(seen, logs, 0.0), axis=1, keepdims=True)
    inside = (offset[:1] >= 0) & (offset[:1] < C)
    end = jnp.sum(jnp.where(inside, logs, 0.0), axis=1, keepdims=True)
    return beta, run, grid.to_row(run), end


def pair_rows(ref, heads, h, c):
    base = c * C * 2 * heads
    return jnp.concatenate(
        [
            ref[pl.ds(base + h, C, stride=2 * heads), :],
            ref[pl.ds(base + heads + h, C, stride=2 * heads), :],
        ],
        axis=0,
    )


BETA, READ, TAIL, SCALE = range(4)


def local_kernel(heads, count, dk_ref, dv_ref, betas_ref, decays_ref,
                 k_ref, kt_ref, inv_ref, p_ref, y_ref, t_ref, o_ref, fade_ref, see_ref, run_ref, col_ref,
                 tsh_ref, osh_ref, low_scr, keys_scr, values_scr, sys_scr, rhs_scr, sem):
    copies = [pltpu.make_async_copy(ref, low_scr.at[m], sem.at[m]) for m, ref in enumerate((dk_ref, dv_ref))]
    for copy in copies:
        copy.start()
    grid = Grid()
    for m, scr in enumerate((keys_scr, values_scr)):
        copies[m].wait()
        scr[...] = low_scr[m].astype(F32)
    eye = jnp.where(grid.diag, 1.0, 0.0)
    items = [(h, c) for h in range(heads) for c in range(count)]
    ends = {}
    for h, c in items:
        raw = pair_rows(keys_scr, heads, h, c)
        values = pair_rows(values_scr, heads, h, c)
        scale = lax.rsqrt(jnp.sum(raw * raw, axis=1, keepdims=True) + EPS)
        keys = raw * scale
        beta, run, line, end = gates(grid, betas_ref, decays_ref, h, c)
        tail = jnp.exp(end - run)
        read = beta * jnp.exp(run)
        fade = beta * jnp.where(grid.strict, jnp.exp(jnp.minimum(run - line, 0.0)), 0.0)
        seen = grid.lane_pos[:C] <= grid.row_pos[:C]
        see_ref[h, c] = jnp.where(seen, jnp.exp(jnp.minimum(run[:C] - line, 0.0)), 0.0)
        run_ref[h, c] = jnp.broadcast_to(jnp.exp(run[:C]), (C, N))
        col_ref[h, c] = jnp.where(
            grid.lane == BETA, beta,
            jnp.where(grid.lane == READ, read, jnp.where(grid.lane == TAIL, tail, scale)),
        )
        k_ref[h, c] = keys
        kt_ref[h, c] = keys * tail
        fade_ref[h, c] = fade
        system = fade * mm_nt(keys, keys)
        sys_scr[h, c] = system
        inv_ref[h, c] = eye - jnp.where(grid.differ == 1, system, 0.0)
        rhs_scr[h, c, :, :N] = read * keys
        rhs_scr[h, c, :, N:] = beta * values
        ends[h, c] = jnp.exp(end)
    for level in range(1, 7):
        near = (grid.differ >= (1 << level)) & (grid.differ < (2 << level))
        half = {}
        for i in items:
            half[i] = mm(jnp.where(near, sys_scr[i], 0.0), inv_ref[i])
        for i in items:
            inv_ref[i] = inv_ref[i] - mm(inv_ref[i], half[i])
    for i in items:
        both = mm(inv_ref[i], rhs_scr[i])
        p_ref[i] = both[:, :N]
        y_ref[i] = both[:, N:]
    for i in items:
        maps = mm_tn(kt_ref[i], jnp.concatenate([p_ref[i], y_ref[i]], axis=1))
        t_ref[i] = ends[i] * eye - maps[:, :N]
        o_ref[i] = maps[:, N:]
    for h in range(heads):
        tsh_ref[h] = t_ref[h, 0]
        osh_ref[h] = o_ref[h, 0]
    for c in range(1, count):
        for h in range(heads):
            both = mm(t_ref[h, c], jnp.concatenate([tsh_ref[h], osh_ref[h]], axis=1))
            tsh_ref[h] = both[:, :N]
            osh_ref[h] = both[:, N:] + o_ref[h, c]


def gather_blocks(place_ref, refs, scr, sem, first):
    copies = []
    count = len(refs)
    for s in range(count):
        source = lax.rem(place_ref[0] + count - s, count)
        copies.append(pltpu.make_async_copy(refs[s], scr.at[source], sem.at[first + s]))
    return copies


def scatter_blocks(place_ref, scr, refs, sem, first):
    copies = []
    count = len(refs)
    for s in range(count):
        target = lax.rem(place_ref[0] + s, count)
        copies.append(pltpu.make_async_copy(scr.at[target], refs[s], sem.at[first + s]))
    return copies


def head_rows(ref, heads, h, c):
    return ref[pl.ds(c * C * heads + h, C, stride=heads), :]


def readout_kernel(heads, count, place_ref, g_ref, s_in_ref, k_ref, p_ref, y_ref, t_ref, o_ref, see_ref, run_ref,
                   s_ref, u_ref, dw_ref, dq_ref, *rest):
    outs, (g_scr, dq_scr, sem) = rest[:heads], rest[heads:]
    g_scr[...] = g_ref[...].astype(F32)
    for h in range(heads):
        s_ref[h, 0] = s_in_ref[h].astype(F32)
    for c in range(count):
        for h in range(heads):
            both = mm(jnp.concatenate([t_ref[h, c], p_ref[h, c]], axis=0), s_ref[h, c])
            u_ref[h, c] = y_ref[h, c] - both[N:]
            s_ref[h, c + 1] = both[:N] + o_ref[h, c]
    items = [(h, c) for h in range(heads) for c in range(count)]
    for h, c in items:
        cot = head_rows(g_scr, heads, h, c).astype(BF16)
        both = low_nt(cot, jnp.concatenate([u_ref[h, c], s_ref[h, c]], axis=0))
        dw_ref[h, c] = both[:, :N] * see_ref[h, c]
        dq_ref[h, c] = run_ref[h, c] * both[:, N:]
    for h, c in items:
        grad = mm(dw_ref[h, c], k_ref[h, c]) + dq_ref[h, c]
        dq_ref[h, c] = grad
        dq_scr[h, pl.ds(c * C, C), :] = grad.astype(BF16)
    copies = scatter_blocks(place_ref, dq_scr, outs, sem, 0)
    for copy in copies:
        copy.start()
    for copy in copies:
        copy.wait()


def unit_queries(low):
    raw = low.astype(F32)
    return raw * lax.rsqrt(jnp.mean(raw * raw, axis=1, keepdims=True) + EPS)


def source_kernel(heads, count, place_ref, g_ref, k_ref, p_ref, t_ref, see_ref, run_ref, *rest):
    ins, (q_ref, z_ref, b_ref, bsh_ref, g_scr, q_scr, sem) = rest[:heads], rest[heads:]
    copies = gather_blocks(place_ref, ins, q_scr, sem, 0)
    for copy in copies:
        copy.start()
    g_scr[...] = g_ref[...].astype(F32)
    for copy in copies:
        copy.wait()
    items = [(h, c) for h in range(heads) for c in range(count)]
    weights = {}
    for h, c in items:
        query = unit_queries(q_scr[h, pl.ds(c * C, C), :])
        q_ref[h, c] = query
        weights[h, c] = mm_nt(query, k_ref[h, c]) * see_ref[h, c]
    for h, c in items:
        cot = head_rows(g_scr, heads, h, c).astype(BF16)
        z_ref[h, c] = low_tn(weights[h, c], cot)
        b_ref[h, c] = low_tn(q_ref[h, c] * run_ref[h, c], cot)
    for h, c in items:
        b_ref[h, c] = b_ref[h, c] - mm_tn(p_ref[h, c], z_ref[h, c])
    for h in range(heads):
        bsh_ref[h] = b_ref[h, count - 1]
    for c in range(count - 2, -1, -1):
        for h in range(heads):
            bsh_ref[h] = b_ref[h, c] + mm_tn(t_ref[h, c], bsh_ref[h])


def final_kernel(heads, count, decays_ref, lam_ref, k_ref, kt_ref, inv_ref, t_ref, fade_ref, col_ref,
                 s_ref, u_ref, dw_ref, dq_ref, q_ref, z_ref, b_ref,
                 gk_ref, gv_ref, gb_ref, gd_ref, gk_scr, gv_scr, lam_scr, r_scr, d_scr, rd_scr):
    grid = Grid()
    items = [(h, c) for h in range(heads) for c in range(count)]
    for h in range(heads):
        lam_scr[h, count - 1] = lam_ref[h].astype(F32)
    for c in range(count - 1, 0, -1):
        for h in range(heads):
            lam_scr[h, c - 1] = mm_tn(t_ref[h, c], lam_scr[h, c]) + b_ref[h, c]
    for i in items:
        d_scr[i] = z_ref[i] + mm(kt_ref[i], lam_scr[i])
    for i in items:
        r_scr[i] = mm_tn(inv_ref[i], d_scr[i])
    for h, c in items:
        both = mm_nt(r_scr[h, c], jnp.concatenate([u_ref[h, c], s_ref[h, c]], axis=0))
        d_scr[h, c] = -both[:, :N] * fade_ref[h, c]
        rd_scr[h, c] = -col_ref[h, c, :, READ:READ + 1] * both[:, N:]
    lines = {}
    for h, c in items:
        keys, r = k_ref[h, c], r_scr[h, c]
        cols = col_ref[h, c]
        beta, tail, scale = (cols[:, n:n + 1] for n in (BETA, TAIL, SCALE))
        gb = jnp.sum(r * u_ref[h, c], axis=1, keepdims=True) / beta
        read = mm(d_scr[h, c], keys) + rd_scr[h, c]
        query = q_ref[h, c]
        write = mm_tn(d_scr[h, c], keys) + tail * mm_nt(u_ref[h, c], lam_scr[h, c]) + mm_tn(dw_ref[h, c], query)
        grad = read + write
        gk = scale * (grad - keys * jnp.sum(keys * grad, axis=1, keepdims=True))
        gv = beta * r
        base = c * C * 2 * heads
        for m in range(2):
            rows = pl.ds(base + m * heads + h, C, stride=2 * heads)
            gk_scr[rows, :] = gk[m * C:(m + 1) * C]
            gv_scr[rows, :] = gv[m * C:(m + 1) * C]
        pulls = keys * (read - write)
        pulls = jnp.sum(pulls[:C] + pulls[C:] + query * dq_ref[h, c], axis=1, keepdims=True)
        after = grid.row_pos[:C] >= grid.lane_pos[:C]
        total = jnp.sum(
            jnp.sum(s_ref[h, c + 1] * lam_scr[h, c], axis=0, keepdims=True), axis=1, keepdims=True
        )
        gd = jnp.sum(jnp.where(after, pulls, 0.0), axis=0, keepdims=True) + total
        half = C * (c % 2)
        mine = (grid.lane[:1] >= half) & (grid.lane[:1] < half + C)
        lines[h, c, 2] = jnp.where(mine, gd, 0.0)
        for m in range(2):
            pick = (grid.lane - half == grid.row - m * C) & (grid.row >= m * C) & (grid.row < (m + 1) * C)
            lines[h, c, m] = jnp.sum(jnp.where(pick, gb, 0.0), axis=0, keepdims=True)
    for h in range(heads):
        for p in range(count // 2):
            lanes = pl.ds(p * N, N)
            for m in range(2):
                gb_ref[m, pl.ds(h, 1), lanes] = lines[h, 2 * p, m] + lines[h, 2 * p + 1, m]
            gd_ref[pl.ds(h, 1), lanes] = (lines[h, 2 * p, 2] + lines[h, 2 * p + 1, 2]) / decays_ref[pl.ds(h, 1), lanes]
    gk_ref[...] = gk_scr[...].astype(BF16)
    gv_ref[...] = gv_scr[...].astype(BF16)


ANY = pl.BlockSpec(memory_space=pl.ANY)
SCALAR = pl.BlockSpec(memory_space=pltpu.SMEM)
VM = pl.BlockSpec(memory_space=pltpu.VMEM)


def shaped(shape, dtype=F32):
    return jax.ShapeDtypeStruct(shape, dtype)


def single(body, name, in_specs, outs, out_specs, scratch, flops):
    return pl.pallas_call(
        body,
        name=name,
        in_specs=in_specs,
        out_shape=outs,
        out_specs=out_specs,
        scratch_shapes=scratch,
        compiler_params=pltpu.CompilerParams(vmem_limit_bytes=LIMIT),
        cost_estimate=pl.CostEstimate(flops=flops, bytes_accessed=4 << 20, transcendentals=0),
    )


def delta_local(dk, dv, betas, decays):
    heads, rows = decays.shape
    count = rows // C
    square, thin, one = (shaped((heads,) + tail) for tail in ((count, N, N), (count, C, N), (N, N)))
    outs = [square] * 8 + [thin] * 2 + [square] + [one] * 2
    return single(
        functools.partial(local_kernel, heads, count), "delta_local",
        [ANY, ANY, VM, VM], outs, [VM] * len(outs),
        [pltpu.VMEM((2,) + dk.shape, BF16)] + [pltpu.VMEM(dk.shape, F32)] * 2
        + [pltpu.VMEM((heads, count, N, N), F32), pltpu.VMEM((heads, count, N, 2 * N), F32),
           pltpu.SemaphoreType.DMA((2,))],
        10 << 30,
    )(dk, dv, betas, decays)


def delta_readout(place, g, entry, k, p, y, t, o, see, run):
    heads, count = k.shape[:2]
    rows = count * C
    square, thin = (shaped((heads,) + tail) for tail in ((count, N, N), (count, C, N)))
    outs = [shaped((heads, count + 1, N, N)), square, thin, thin]
    return single(
        functools.partial(readout_kernel, heads, count), "delta_readout",
        [SCALAR] + [VM] * 9, outs + [shaped((rows, N), BF16)] * heads, [VM] * 4 + [ANY] * heads,
        [pltpu.VMEM(g.shape, F32), pltpu.VMEM((heads, rows, N), BF16), pltpu.SemaphoreType.DMA((heads,))],
        3 << 30,
    )(place, g, entry, k, p, y, t, o, see, run)


def delta_source(place, g, k, p, t, see, run, attended):
    heads, count = k.shape[:2]
    rows = count * C
    square, thin = (shaped((heads,) + tail) for tail in ((count, N, N), (count, C, N)))
    return single(
        functools.partial(source_kernel, heads, count), "delta_source",
        [SCALAR] + [VM] * 6 + [ANY] * heads,
        [thin, square, square, shaped((heads, N, N))], [VM] * 4,
        [pltpu.VMEM(g.shape, F32), pltpu.VMEM((heads, rows, N), BF16), pltpu.SemaphoreType.DMA((heads,))],
        3 << 30,
    )(place, g, k, p, t, see, run, *attended)


def delta_final(betas, decays, lam, k, kt, inv, t, fade, col, s, u, dw, dq, q, z, b):
    heads, count = k.shape[:2]
    wide = (2 * count * C * heads, N)
    return single(
        functools.partial(final_kernel, heads, count), "delta_final",
        [VM] * 15,
        [shaped(wide, BF16), shaped(wide, BF16), shaped(betas.shape), shaped(decays.shape)], [VM] * 4,
        [pltpu.VMEM(wide, F32)] * 2 + [pltpu.VMEM((heads, count, N, N), F32)] * 4,
        8 << 30,
    )(decays, lam, k, kt, inv, t, fade, col, s, u, dw, dq, q, z, b)


def rounds(refs, index, count, sign):
    return [lax.rem(index + (s if sign > 0 else count - s), count) for s in range(count)]


def send_kernel(count, place_ref, q_ref, k_ref, v_ref, *rest):
    outs, (low, scr, sem) = rest[:count], rest[count:]
    heads = count
    rows = q_ref.shape[0] // heads
    copies = [pltpu.make_async_copy(ref, low.at[m], sem.at[m]) for m, ref in enumerate((q_ref, k_ref, v_ref))]
    for copy in copies:
        copy.start()
    for m in range(3):
        copies[m].wait()
        scr[m] = low[m].astype(F32)
        for s in range(count):
            head = lax.rem(place_ref[0] + s, count)
            outs[s][m] = scr[m, pl.ds(head, rows, stride=heads), :].astype(BF16)


def take_kernel(count, place_ref, *rest):
    ins, outs, (scr,) = rest[:count], rest[count:count + 3], rest[count + 3:]
    heads = count
    rows = outs[0].shape[0] // heads
    for m in range(3):
        for s in range(count):
            head = lax.rem(place_ref[0] + count - s, count)
            scr[pl.ds(head, rows, stride=heads), :] = ins[s][m].astype(F32)
        outs[m][...] = scr[...].astype(BF16)


def attend_kernel(count, scale, place_ref, *rest):
    ins, (prob_ref, mixed_ref), outs = rest[:count], rest[count:count + 2], rest[count + 2:2 * count + 2]
    scr, att_scr, sem = rest[2 * count + 2:]
    copies = gather_blocks(place_ref, ins, scr, sem, 0)
    for copy in copies:
        copy.start()
    for copy in copies:
        copy.wait()
    rows = scr.shape[2]
    causal = iota((rows, rows), 0) <= iota((rows, rows), 1)
    for i in range(count):
        query = scr[i, 0]
        pieces = []
        for j in range(i + 1):
            score = contract(scr[j, 1], query, 1, 1) * scale
            pieces.append(jnp.where(causal, score, -jnp.inf) if j == i else score)
        top = pieces[0].max(axis=0, keepdims=True)
        for piece in pieces[1:]:
            top = jnp.maximum(top, piece.max(axis=0, keepdims=True))
        pieces = [jnp.exp(piece - top) for piece in pieces]
        total = pieces[0].sum(axis=0, keepdims=True)
        for piece in pieces[1:]:
            total = total + piece.sum(axis=0, keepdims=True)
        mixed = None
        for j, piece in enumerate(pieces):
            low = (piece / total).astype(BF16)
            prob_ref[i * (i + 1) // 2 + j] = low
            term = contract(low, scr[j, 2], 0, 0)
            mixed = term if mixed is None else mixed + term
        mixed_ref[i] = mixed
        att_scr[i] = mixed.astype(BF16)
    copies = scatter_blocks(place_ref, att_scr, outs, sem, 0)
    for copy in copies:
        copy.start()
    for copy in copies:
        copy.wait()


def attend_back_kernel(count, scale, place_ref, prob_ref, mixed_ref, *rest):
    ins, grads, outs = rest[:count], rest[count:2 * count], rest[2 * count:3 * count]
    scr, g_scr, out_scr, acc, sem = rest[3 * count:]
    copies = gather_blocks(place_ref, ins, scr, sem, 0) + gather_blocks(place_ref, grads, g_scr, sem, count)
    for copy in copies:
        copy.start()
    for copy in copies:
        copy.wait()
    rows = scr.shape[2]
    ones = jnp.ones((8, N), F32)
    for i in range(count):
        mixed = mixed_ref[i]
        low = mixed.astype(BF16).astype(F32)
        grad = g_scr[i].astype(F32)
        inv = lax.rsqrt(jnp.mean(low * low, axis=1, keepdims=True) + EPS)
        pull = inv * (grad - low * (inv * inv * jnp.mean(low * grad, axis=1, keepdims=True)))
        pull = pull.astype(BF16)
        dots = mm_nt(ones, pull.astype(F32) * mixed)[:1]
        query = scr[i, 0]
        gq = None
        for j in range(i + 1):
            prob = prob_ref[i * (i + 1) // 2 + j]
            gp = contract(scr[j, 2], pull, 1, 1)
            gs = (prob.astype(F32) * (gp - dots) * scale).astype(BF16)
            term = contract(gs, scr[j, 1], 0, 0)
            gq = term if gq is None else gq + term
            gk = contract(gs, query, 1, 0)
            gv = contract(prob, pull, 1, 0)
            if i == j:
                acc[j, 0] = gk
                acc[j, 1] = gv
            else:
                acc[j, 0] = acc[j, 0] + gk
                acc[j, 1] = acc[j, 1] + gv
        out_scr[i, 0] = gq.astype(BF16)
    for j in range(count):
        out_scr[j, 1] = acc[j, 0].astype(BF16)
        out_scr[j, 2] = acc[j, 1].astype(BF16)
    copies = scatter_blocks(place_ref, out_scr, outs, sem, 0)
    for copy in copies:
        copy.start()
    for copy in copies:
        copy.wait()


def send_heads(place, q, k, v, count):
    rows = q.shape[0] // count
    return single(
        functools.partial(send_kernel, count), "send_heads",
        [SCALAR, ANY, ANY, ANY], [shaped((3, rows, N), BF16)] * count, [VM] * count,
        [pltpu.VMEM((3,) + q.shape, BF16), pltpu.VMEM((3,) + q.shape, F32), pltpu.SemaphoreType.DMA((3,))],
        1 << 28,
    )(place, q, k, v)


def take_heads(place, parts):
    count = len(parts)
    rows = parts[0].shape[1]
    wide = (rows * count, N)
    return single(
        functools.partial(take_kernel, count), "take_heads",
        [SCALAR] + [VM] * count, [shaped(wide, BF16)] * 3, [VM] * 3,
        [pltpu.VMEM(wide, F32)], 1 << 28,
    )(place, *parts)


def attend(place, parts, scale):
    count = len(parts)
    rows = parts[0].shape[1]
    tri = count * (count + 1) // 2
    return single(
        functools.partial(attend_kernel, count, scale), "attend",
        [SCALAR] + [ANY] * count,
        [shaped((tri, rows, rows), BF16), shaped((count, rows, N))] + [shaped((rows, N), BF16)] * count,
        [VM, VM] + [ANY] * count,
        [pltpu.VMEM((count, 3, rows, N), BF16), pltpu.VMEM((count, rows, N), BF16),
         pltpu.SemaphoreType.DMA((count,))], 2 << 30,
    )(place, *parts)


def attend_back(place, prob, mixed, parts, grads, scale):
    count = len(parts)
    rows = parts[0].shape[1]
    return single(
        functools.partial(attend_back_kernel, count, scale), "attend_back",
        [SCALAR, VM, VM] + [ANY] * (2 * count),
        [shaped((3, rows, N), BF16)] * count, [ANY] * count,
        [pltpu.VMEM((count, 3, rows, N), BF16), pltpu.VMEM((count, rows, N), BF16),
         pltpu.VMEM((count, 3, rows, N), BF16), pltpu.VMEM((count, 2, rows, N), F32),
         pltpu.SemaphoreType.DMA((2 * count,))], 4 << 30,
    )(place, prob, mixed, *parts, *grads)


PRECISE = lax.Precision.HIGHEST


def shifted(value, axis, steps):
    count = lax.axis_size(axis)
    initial, last = (max(0, -steps), min(count, count - steps))
    return lax.ppermute(value, axis, [(source, source + steps) for source in range(initial, last)])


def rotated(parts, axis):
    count = len(parts)
    moved = [parts[0]]
    for s in range(1, count):
        moved.append(lax.ppermute(parts[s], axis, [(d, (d + s) % count) for d in range(count)]))
    return moved


def apply_map(matrix, state):
    return jnp.einsum("hij,hjk->hik", matrix, state, precision=PRECISE)


def entering(matrix, offset, axis, step):
    count = lax.axis_size(axis)
    if count <= 4:
        state = shifted(offset.astype(BF16), axis, step)
        for hop in range(count - 2):
            state = shifted((apply_map(matrix, state.astype(F32)) + offset).astype(BF16), axis, step)
        return state
    place = lax.axis_index(axis)
    place = place if step > 0 else count - 1 - place
    eye = jnp.eye(matrix.shape[-1], dtype=F32)
    reach = 1
    while reach < count:
        before, start = (shifted(matrix, axis, step * reach), shifted(offset, axis, step * reach))
        before = before + jnp.where(place < reach, eye, 0.0)
        offset = apply_map(matrix, start) + offset
        matrix = apply_map(matrix, before)
        reach *= 2
    return shifted(offset, axis, step).astype(BF16)


def visible_pairs(rows, span):
    relative = jnp.arange((span + 1) * rows, dtype=jnp.int32) - span * rows
    local = jnp.arange(rows, dtype=jnp.int32)
    return (
        (relative[None, :] <= local[:, None])
        & (relative[None, :] > local[:, None] - WINDOW)
        & (lax.axis_index("seq") * rows + relative[None, :] >= 0)
    )


def window_forward(queries, keys, values, scale):
    rows = queries.shape[0]
    span = -(-WINDOW // rows)
    couple = jnp.stack([keys, values])
    earlier = [shifted(couple, "seq", step + 1) for step in range(min(span, lax.axis_size("seq") - 1))]
    span = len(earlier)
    ordered = earlier[::-1] + [couple]
    window_keys = jnp.concatenate([piece[0] for piece in ordered], axis=0)
    window_values = jnp.concatenate([piece[1] for piece in ordered], axis=0)
    visible = visible_pairs(rows, span)
    scores = jnp.einsum("qhe,khe->hqk", queries, window_keys, preferred_element_type=F32) * scale
    top = jnp.max(jnp.where(visible, scores, -jnp.inf), axis=-1)
    lifted = jnp.where(visible, jnp.exp(jnp.where(visible, scores - top[:, :, None], 0.0)), 0.0)
    attention = lifted / jnp.sum(lifted, axis=-1)[:, :, None]
    mixed = jnp.einsum(
        "hqk,khe->qhe", attention.astype(BF16), window_values, preferred_element_type=F32
    )
    return window_keys, window_values, attention, mixed, span


def window_backward(queries, window_keys, window_values, attention, mixed, span, unit_grad, scale):
    rows = queries.shape[0]
    low = mixed.astype(BF16).astype(F32)
    grad = unit_grad.astype(F32)
    inv = lax.rsqrt(jnp.mean(low * low, axis=-1, keepdims=True) + EPS)
    pull = inv * (grad - low * (inv * inv * jnp.mean(low * grad, axis=-1, keepdims=True)))
    pull = pull.astype(BF16)
    row_dots = jnp.sum(pull.astype(F32) * mixed, axis=-1).T
    grad_attention = jnp.einsum("qhe,khe->hqk", pull, window_values, preferred_element_type=F32)
    grad_scores = (attention * (grad_attention - row_dots[:, :, None]) * scale).astype(BF16)
    grad_queries = jnp.einsum(
        "hqk,khe->qhe", grad_scores, window_keys, preferred_element_type=F32
    ).astype(BF16)
    key_parts = jnp.einsum("hqk,qhe->khe", grad_scores, queries, preferred_element_type=F32)
    value_parts = jnp.einsum("hqk,qhe->khe", attention.astype(BF16), pull, preferred_element_type=F32)
    gathered = jnp.stack([key_parts[span * rows:], value_parts[span * rows:]])
    for later in range(1, span + 1):
        first = (span - later) * rows
        piece = jnp.stack([key_parts[first:first + rows], value_parts[first:first + rows]])
        gathered = gathered + shifted(piece, "seq", -later)
    return grad_queries, gathered[0].astype(BF16), gathered[1].astype(BF16)


def body(queries, keys, values, delta_keys, delta_values, betas, decays, grad_out):
    rows, heads, width = queries.shape
    scale = 1.0 / math.sqrt(width)
    count = lax.axis_size("seq")
    by_head = heads == count and WINDOW >= count * rows

    def flat(array):
        return array.reshape(-1, width)

    place = lax.axis_index("seq").astype(jnp.int32).reshape(1) if by_head else jnp.zeros((1,), jnp.int32)
    pairs = flat(delta_keys)
    if by_head:
        parts = send_heads(place, flat(queries), flat(keys), flat(values), count)
        pairs, parts = lax.optimization_barrier((pairs, parts))
        parts = rotated(parts, "seq")
    cot = flat(grad_out)
    k, kt, inverse, p, y, t, o, fade, see, run, col, shard_t, shard_o = delta_local(
        pairs, flat(delta_values), betas, decays
    )
    entry = entering(shard_t, shard_o, "seq", 1)
    if by_head:
        prob, mixed, *attended = attend(place, parts, scale)
        attended = rotated(attended, "seq")
    else:
        saved = window_forward(queries, keys, values, scale)
        low = saved[3].astype(BF16)
        attended = [low[:, (heads - s) % heads] for s in range(heads)]
    s, u, dw, dq, *pulls = delta_readout(place, cot, entry, k, p, y, t, o, see, run)
    if by_head:
        pulls = rotated(pulls, "seq")
        outs = rotated(attend_back(place, prob, mixed, parts, pulls, scale), "seq")
    else:
        grads = window_backward(queries, *saved, jnp.stack(pulls, axis=1), scale)
    q, z, b, shard_source = delta_source(place, cot, k, p, t, see, run, attended)
    leaving = entering(jnp.swapaxes(shard_t, 1, 2), shard_source, "seq", -1)
    grad_keys, grad_values, grad_betas, grad_decays = delta_final(
        betas, decays, leaving, k, kt, inverse, t, fade, col, s, u, dw, dq, q, z, b
    )
    if by_head:
        outs, grad_keys = lax.optimization_barrier((outs, grad_keys))
        grads = [array.reshape(rows, heads, width) for array in take_heads(place, outs)]
    pair = (rows, 2, heads, width)
    return (*grads, grad_keys.reshape(pair), grad_values.reshape(pair), grad_betas, grad_decays)


def solution(mesh):
    row = P(("parts", "seq"), "head", None)
    pair = P(("parts", "seq"), None, "head", None)
    beta = P(None, "head", ("parts", "seq"))
    decay = P("head", ("parts", "seq"))
    return jax.shard_map(
        body,
        mesh=mesh,
        in_specs=(row, row, row, pair, pair, beta, decay, row),
        out_specs=(row, row, row, pair, pair, beta, decay),
        check_vma=False,
    )
```

time: 138 us -> 85.1 us (0.62)
  Pallas kernels: 69.3 us -> 30.2 us
  waiting for transfers between devices: 32.2 us -> 17.4 us
  local copies, waits for them, and re-layouts: 3.93 us -> 6.32 us
  other arithmetic: 2.01 us -> 0.04 us
    pallas_call x5, Pallas kernels: 54.6 us -> 19.6 us  [the longest x1 8.19 us: delta_local(): single(functools.partial(local_kernel, heads, count), 'delta_local', [ANY...]
    ppermute x12, waiting for transfers between devices: 32.2 us -> 16.6 us  [rotated(): lax.ppermute(parts[s], axis, [(d, (d + s) % count) for d in range(count)])]
    unnamed x34 -> x18, local copies, waits for them, and re-layouts: 3.93 us -> 6.32 us
    convert_element_type x2, other arithmetic: 2.01 us -> 0.04 us  [entering(): state = shifted(offset.astype(BF16), axis, step)]
    pallas_call x1, Pallas kernels: 5.27 us -> 3.48 us  [attend(): single(functools.partial(attend_kernel, count, scale), 'attend', [SCALAR]...]
    ppermute x12, starting transfers between devices: 10.3 us -> 11.8 us  [rotated(): lax.ppermute(parts[s], axis, [(d, (d + s) % count) for d in range(count)])]
  transfers between devices with their start and end apart: 18 -> 18, of which waited for: 5 -> 4; matrix products, arithmetic and copies ran while one was open for 2% -> 2% of each run, Pallas kernels for 26% -> 34%
where the time goes in v2:
time: 85.1 us; the launch traced here: 84.6 us
  Pallas kernels  30.2 us (35%)
  starting transfers between devices  28.3 us (33%)
  waiting for transfers between devices  17.4 us (20%)
  local copies, waits for them, and re-layouts  6.32 us (7%)
  matrix products  1.31 us (2%)
  between operations  0.91 us (1%)
    ppermute x12, waiting for transfers between devices, rotated(): lax.ppermute(parts[s], axis, [(d, (d + s) % count) for d in range(count)])  16.6 us
    ppermute x6, starting transfers between devices, shifted(): lax.ppermute(value, axis, [(source, source + steps) for source in range(i...  16.5 us
    ppermute x12, starting transfers between devices, rotated(): lax.ppermute(parts[s], axis, [(d, (d + s) % count) for d in range(count)])  11.8 us
    pallas_call x1, Pallas kernels, delta_local(): single(functools.partial(local_kernel, heads, count), 'delta_local', [ANY...  8.19 us
    unnamed x18, local copies, waits for them, and re-layouts  6.32 us
    pallas_call x1, Pallas kernels, delta_final(): single(functools.partial(final_kernel, heads, count), 'delta_final', [VM]...  6.2 us
    pallas_call x1, Pallas kernels, attend_back(): single(functools.partial(attend_back_kernel, count, scale), 'attend_back'...  6.09 us
    pallas_call x1, Pallas kernels, attend(): single(functools.partial(attend_kernel, count, scale), 'attend', [SCALAR]...  3.48 us
  transfers between devices with their start and end apart: 18, of which 4 were waited for; matrix products, arithmetic and copies ran while one was open for 2% of the time, Pallas kernels for 34%

profile of v2, /device:TPU:9, one launch (start us, length us, event | category | flops | bytes accessed | tf_op | source)
XLA Modules:
  0.0 84.6 jit_solution(11038702408655469460)
XLA Ops:
  3.9 1.3 %collective-permute-start = (bf16[3,256,128]{2,1,0:T(8,128)(2,1)S(1)}, bf16[3,256,128]{2,1,0:T(8,128)(2,1)S(1)}, u32[]{:S(2)}, u32[]{:S(2)}) collective-permute-start(bf16[3,256,128]{2,1,0:T(8,128)(2,1)S(1)} %get-tuple-element.68), channel_id=1, source_target_pairs={{0,4},{4,8},{8,12},{12,0},{1,5},{5,9},{9,13},{13,1},{2,6},{6,10},{... | collective-permute-start | bytes 589832 | tf_op jit(solution)/shard_map/ppermute | solution.py:572
  5.3 1.1 %collective-permute-start.1 = (bf16[3,256,128]{2,1,0:T(8,128)(2,1)S(1)}, bf16[3,256,128]{2,1,0:T(8,128)(2,1)S(1)}, u32[]{:S(2)}, u32[]{:S(2)}) collective-permute-start(bf16[3,256,128]{2,1,0:T(8,128)(2,1)S(1)} %get-tuple-element.69), channel_id=1, source_target_pairs={{0,8},{4,12},{8,0},{12,4},{1,9},{5,13},{9,1},{13,5},{2,10},{6,14},... | collective-permute-start | bytes 589832 | tf_op jit(solution)/shard_map/ppermute | solution.py:572
  6.3 1.4 %collective-permute-start.2 = (bf16[3,256,128]{2,1,0:T(8,128)(2,1)S(1)}, bf16[3,256,128]{2,1,0:T(8,128)(2,1)S(1)}, u32[]{:S(2)}, u32[]{:S(2)}) collective-permute-start(bf16[3,256,128]{2,1,0:T(8,128)(2,1)S(1)} %get-tuple-element.70), channel_id=1, source_target_pairs={{0,12},{4,0},{8,4},{12,8},{1,13},{5,1},{9,5},{13,9},{2,14},{6,2},{... | collective-permute-start | bytes 589832 | tf_op jit(solution)/shard_map/ppermute | solution.py:572
  8.8 1.0 %copy-done.1 = bf16[256,2,4,128]{3,2,1,0:T(4,128)(2,1)S(1)} copy-done((bf16[256,2,4,128]{3,2,1,0:T(4,128)(2,1)S(1)}, bf16[256,2,4,128]{3,2,1,0:T(4,128)(2,1)}, u32[]{:S(2)}) %copy-start.1) | copy-done | bytes 524312
  11.2 8.2 %delta_local.1 = (f32[4,4,128,128]{3,2,1,0:T(8,128)S(1)}, f32[4,4,128,128]{3,2,1,0:T(8,128)S(1)}, f32[4,4,128,128]{3,2,1,0:T(8,128)S(1)}, f32[4,4,128,128]{3,2,1...) custom-call(bf16[2048,128]{1,0:T(8,128)(2,1)S(1)} %bitcast.20, ...), custom_call_target="tpu_custom_call" | custom-call | flops 10737418240 | bytes 4194304 | tf_op jit(solution)/shard_map/delta_local/pallas_call | solution.py:350
  19.4 2.1 %collective-permute-start.3 = (bf16[4,128,128]{2,1,0:T(8,128)(2,1)S(1)}, bf16[4,128,128]{2,1,0:T(8,128)(2,1)S(1)}, u32[]{:S(2)}, u32[]{:S(2)}) collective-permute-start(bf16[4,128,128]{2,1,0:T(8,128)(2,1)S(1)} %convert_element_type.22), channel_id=1, source_target_pairs={{0,4},{4,8},{8,12},{1,5},{5,9},{9,13},{2,6},{6,10},{10,14},{3,7},{... | collective-permute-start | bytes 393224 | tf_op jit(solution)/shard_map/ppermute | solution.py:565
  21.6 2.7 %collective-permute-done.2.rest_3_ = bf16[3,256,128]{2,1,0:T(8,128)(2,1)S(1)} collective-permute-done((bf16[3,256,128]{2,1,0:T(8,128)(2,1)S(1)}, bf16[3,256,128]{2,1,0:T(8,128)(2,1)S(1)}, u32[]{:S(2)}, u32[]{:S(2)}) %collective-permute-start.2) | collective-permute-done | bytes 196640 | tf_op jit(solution)/shard_map/ppermute | solution.py:572
  24.3 3.5 %attend.1 = (bf16[10,256,256]{2,1,0:T(8,128)(2,1)S(1)}, f32[4,256,128]{2,1,0:T(8,128)S(1)}, bf16[256,128]{1,0:T(8,128)(2,1)S(1)}, bf16[256,128]{1,0:T(8,128)(2,1...) custom-call(s32[1]{0:T(128)} %bitcast.place_ref, bf16[3,256,128]{2,1,0:T(8,128)(2,1)S(1)} %get-tuple-element.67.rest_0_, ...), custom_call_target="tpu_custom_call" | custom-call | flops 2147483648 | bytes 4194304 | tf_op jit(solution)/shard_map/attend/pallas_call | solution.py:536
  29.9 3.0 %collective-permute-start.4 = (bf16[4,128,128]{2,1,0:T(8,128)(2,1)S(1)}, bf16[4,128,128]{2,1,0:T(8,128)(2,1)S(1)}, u32[]{:S(2)}, u32[]{:S(2)}) collective-permute-start(bf16[4,128,128]{2,1,0:T(8,128)(2,1)S(1)} %fusion), channel_id=1, source_target_pairs={{0,4},{4,8},{8,12},{1,5},{5,9},{9,13},{2,6},{6,10},{10,14},{3,7},{... | collective-permute-start | bytes 393224 | tf_op jit(solution)/shard_map/ppermute | solution.py:565
  32.9 3.5 %collective-permute-done.14.rest_3_ = bf16[256,128]{1,0:T(8,128)(2,1)S(1)} collective-permute-done((bf16[256,128]{1,0:T(8,128)(2,1)S(1)}, bf16[256,128]{1,0:T(8,128)(2,1)S(1)}, u32[]{:S(2)}, u32[]{:S(2)}) %collective-permute-start.14) | collective-permute-done | bytes 65568 | tf_op jit(solution)/shard_map/ppermute | solution.py:572
  36.3 2.4 %delta_source.1 = (f32[4,4,64,128]{3,2,1,0:T(8,128)S(1)}, f32[4,4,128,128]{3,2,1,0:T(8,128)S(1)}, f32[4,4,128,128]{3,2,1,0:T(8,128)S(1)}, f32[4,128,128]{2,1,0:T(8,128)S(1)}) custom-call(s32[1]{0:T(128)} %bitcast.place_ref, bf16[1024,128]{1,0:T(8,128)(2,1)S(1)} %bitcast.25, f32[4,4,128,128]{3,2,1,0:T(8,128)S(1)} %get-tuple-element.76.k_ref, ...), custom_call_target="tpu_custom_call" | custom-call | flops 3221225472 | bytes 4194304 | tf_op jit(solution)/shard_map/delta_source/pallas_call | solution.py:377
  38.7 1.9 %collective-permute-start.15 = (bf16[4,128,128]{2,1,0:T(8,128)(2,1)S(1)}, bf16[4,128,128]{2,1,0:T(8,128)(2,1)S(1)}, u32[]{:S(2)}, u32[]{:S(2)}) collective-permute-start(bf16[4,128,128]{2,1,0:T(8,128)(2,1)S(1)} %convert_element_type.25), channel_id=1, source_target_pairs={{4,0},{8,4},{12,8},{5,1},{9,5},{13,9},{6,2},{10,6},{14,10},{7,3},{... | collective-permute-start | bytes 393224 | tf_op jit(solution)/shard_map/ppermute | solution.py:565
  40.9 3.4 %collective-permute-start.5 = (bf16[4,128,128]{2,1,0:T(8,128)(2,1)S(1)}, bf16[4,128,128]{2,1,0:T(8,128)(2,1)S(1)}, u32[]{:S(2)}, u32[]{:S(2)}) collective-permute-start(bf16[4,128,128]{2,1,0:T(8,128)(2,1)S(1)} %fusion.1), channel_id=1, source_target_pairs={{0,4},{4,8},{8,12},{1,5},{5,9},{9,13},{2,6},{6,10},{10,14},{3,7},{... | collective-permute-start | bytes 393224 | tf_op jit(solution)/shard_map/ppermute | solution.py:565
  45.6 1.9 %collective-permute-start.16 = (bf16[4,128,128]{2,1,0:T(8,128)(2,1)S(1)}, bf16[4,128,128]{2,1,0:T(8,128)(2,1)S(1)}, u32[]{:S(2)}, u32[]{:S(2)}) collective-permute-start(bf16[4,128,128]{2,1,0:T(8,128)(2,1)S(1)} %fusion.2), channel_id=1, source_target_pairs={{4,0},{8,4},{12,8},{5,1},{9,5},{13,9},{6,2},{10,6},{14,10},{7,3},{... | collective-permute-start | bytes 393224 | tf_op jit(solution)/shard_map/ppermute | solution.py:565
  47.5 2.5 %delta_readout.1 = (f32[4,5,128,128]{3,2,1,0:T(8,128)S(1)}, f32[4,4,128,128]{3,2,1,0:T(8,128)S(1)}, f32[4,4,64,128]{3,2,1,0:T(8,128)S(1)}, f32[4,4,64,128]{3,2,1...) custom-call(s32[1]{0:T(128)} %bitcast.place_ref, ...), custom_call_target="tpu_custom_call" | custom-call | flops 3221225472 | bytes 4194304 | tf_op jit(solution)/shard_map/delta_readout/pallas_call | solution.py:365
  50.0 1.5 %collective-permute-start.6 = (bf16[256,128]{1,0:T(8,128)(2,1)S(1)}, bf16[256,128]{1,0:T(8,128)(2,1)S(1)}, u32[]{:S(2)}, u32[]{:S(2)}) collective-permute-start(bf16[256,128]{1,0:T(8,128)(2,1)S(1)} %get-tuple-element.84), channel_id=1, source_target_pairs={{0,4},{4,8},{8,12},{12,0},{1,5},{5,9},{9,13},{13,1},{2,6},{6,10},{... | collective-permute-start | bytes 196616 | tf_op jit(solution)/shard_map/ppermute | solution.py:572
  51.5 1.3 %collective-permute-start.8 = (bf16[256,128]{1,0:T(8,128)(2,1)S(1)}, bf16[256,128]{1,0:T(8,128)(2,1)S(1)}, u32[]{:S(2)}, u32[]{:S(2)}) collective-permute-start(bf16[256,128]{1,0:T(8,128)(2,1)S(1)} %get-tuple-element.86), channel_id=1, source_target_pairs={{0,12},{4,0},{8,4},{12,8},{1,13},{5,1},{9,5},{13,9},{2,14},{6,2},{... | collective-permute-start | bytes 196616 | tf_op jit(solution)/shard_map/ppermute | solution.py:572
  53.2 4.2 %collective-permute-start.17 = (bf16[4,128,128]{2,1,0:T(8,128)(2,1)S(1)}, bf16[4,128,128]{2,1,0:T(8,128)(2,1)S(1)}, u32[]{:S(2)}, u32[]{:S(2)}) collective-permute-start(bf16[4,128,128]{2,1,0:T(8,128)(2,1)S(1)} %fusion.3), channel_id=1, source_target_pairs={{4,0},{8,4},{12,8},{5,1},{9,5},{13,9},{6,2},{10,6},{14,10},{7,3},{... | collective-permute-start | bytes 393224 | tf_op jit(solution)/shard_map/ppermute | solution.py:565
  57.4 6.1 %attend_back.1 = (bf16[3,256,128]{2,1,0:T(8,128)(2,1)S(1)}, bf16[3,256,128]{2,1,0:T(8,128)(2,1)S(1)}, bf16[3,256,128]{2,1,0:T(8,128)(2,1)S(1)}, bf16[3,256,128]{2,1,0:T(8,128)(2,1)S(1)}) custom-call(s32[1]{0:T(128)} %bitcast.place_ref, bf16[10,256,256]{2,1,0:T(8,128)(2,1)S(1)} %get-tuple-element.71.prob_ref, f32[4,256,128]{2,1,0:T(8,128)S(1)} %get-tuple-element.72.mixed_ref, ...), custom_call_target="tpu_custom_call" | custom-call | flops 4294967296 | bytes 4194304 | tf_op jit(solution)/shard_map/attend_back/pallas_call | solution.py:549
  63.6 2.0 %collective-permute-start.10 = (bf16[3,256,128]{2,1,0:T(8,128)(2,1)S(1)}, bf16[3,256,128]{2,1,0:T(8,128)(2,1)S(1)}, u32[]{:S(2)}, u32[]{:S(2)}) collective-permute-start(bf16[3,256,128]{2,1,0:T(8,128)(2,1)S(1)} %get-tuple-element.89), channel_id=1, source_target_pairs={{0,8},{4,12},{8,0},{12,4},{1,9},{5,13},{9,1},{13,5},{2,10},{6,14},... | collective-permute-start | bytes 589832 | tf_op jit(solution)/shard_map/ppermute | solution.py:572
  65.6 1.4 %collective-permute-start.11 = (bf16[3,256,128]{2,1,0:T(8,128)(2,1)S(1)}, bf16[3,256,128]{2,1,0:T(8,128)(2,1)S(1)}, u32[]{:S(2)}, u32[]{:S(2)}) collective-permute-start(bf16[3,256,128]{2,1,0:T(8,128)(2,1)S(1)} %get-tuple-element.90), channel_id=1, source_target_pairs={{0,12},{4,0},{8,4},{12,8},{1,13},{5,1},{9,5},{13,9},{2,14},{6,2},{... | collective-permute-start | bytes 589832 | tf_op jit(solution)/shard_map/ppermute | solution.py:572
  67.0 6.2 %delta_final.1 = (bf16[2048,128]{1,0:T(8,128)(2,1)}, bf16[2048,128]{1,0:T(8,128)(2,1)}, f32[2,4,256]{2,1,0:T(4,128)}, f32[4,256]{1,0:T(4,128)}) custom-call(f32[4,256]{1,0:T(4,128)S(1)} %copy-done.8, bf16[4,128,128]{2,1,0:T(8,128)(2,1)S(1)} %collective-permute-done.17.lam_ref, f32[4,4,128,128]{3,2,1,0:T(8,128)S(1)} %get-tuple-element.76.k_ref, ...), custom_call_target="tpu_custom_call" | custom-call | flops 8589934592 | bytes 4194304 | tf_op jit(solution)/shard_map/delta_final/pallas_call | solution.py:389
  73.2 10.3 %collective-permute-done.11.rest_3_ = bf16[3,256,128]{2,1,0:T(8,128)(2,1)S(1)} collective-permute-done((bf16[3,256,128]{2,1,0:T(8,128)(2,1)S(1)}, bf16[3,256,128]{2,1,0:T(8,128)(2,1)S(1)}, u32[]{:S(2)}, u32[]{:S(2)}) %collective-permute-start.11) | collective-permute-done | bytes 196640 | tf_op jit(solution)/shard_map/ppermute | solution.py:572
  83.5 1.1 %take_heads.1 = (bf16[1024,128]{1,0:T(8,128)(2,1)}, bf16[1024,128]{1,0:T(8,128)(2,1)}, bf16[1024,128]{1,0:T(8,128)(2,1)}) custom-call(s32[1]{0:T(128)} %bitcast.place_ref, bf16[3,256,128]{2,1,0:T(8,128)(2,1)S(1)} %get-tuple-element.108.rest_0_, bf16[3,256,128]{2,1,0:T(8,128)(2,1)S(1)} %collective-permute-done.9.rest_1_, ...), custom_call_target="tpu_custom_call" | custom-call | flops 268435456 | bytes 4194304 | tf_op jit(solution)/shard_map/take_heads/pallas_call | solution.py:525
  (44 shorter events, 9.8 us)
Async XLA Ops:
  0.6 1.0 %copy-start.2 = (bf16[256,4,128]{2,1,0:T(4,128)(2,1)S(1)}, bf16[256,4,128]{2,1,0:T(4,128)(2,1)}, u32[]{:S(2)}) copy-start(bf16[256,4,128]{2,1,0:T(4,128)(2,1)} %param.8) | copy-start | bytes 786436
  1.6 0.9 %copy-start.3 = (bf16[256,4,128]{2,1,0:T(4,128)(2,1)S(1)}, bf16[256,4,128]{2,1,0:T(4,128)(2,1)}, u32[]{:S(2)}) copy-start(bf16[256,4,128]{2,1,0:T(4,128)(2,1)} %param.9) | copy-start | bytes 786436
  3.9 17.6 %collective-permute-start = (bf16[3,256,128]{2,1,0:T(8,128)(2,1)S(1)}, bf16[3,256,128]{2,1,0:T(8,128)(2,1)S(1)}, u32[]{:S(2)}, u32[]{:S(2)}) collective-permute-start(bf16[3,256,128]{2,1,0:T(8,128)(2,1)S(1)} %get-tuple-element.68), channel_id=1, source_target_pairs={{0,4},{4,8},{8,12},{12,0},{1,5},{5,9},{9,13},{13,1},{2,6},{6,10},{... | collective-permute-start | bytes 589832 | tf_op jit(solution)/shard_map/ppermute | solution.py:572
  5.3 16.3 %collective-permute-start.1 = (bf16[3,256,128]{2,1,0:T(8,128)(2,1)S(1)}, bf16[3,256,128]{2,1,0:T(8,128)(2,1)S(1)}, u32[]{:S(2)}, u32[]{:S(2)}) collective-permute-start(bf16[3,256,128]{2,1,0:T(8,128)(2,1)S(1)} %get-tuple-element.69), channel_id=1, source_target_pairs={{0,8},{4,12},{8,0},{12,4},{1,9},{5,13},{9,1},{13,5},{2,10},{6,14},... | collective-permute-start | bytes 589832 | tf_op jit(solution)/shard_map/ppermute | solution.py:572
  6.3 17.9 %collective-permute-start.2 = (bf16[3,256,128]{2,1,0:T(8,128)(2,1)S(1)}, bf16[3,256,128]{2,1,0:T(8,128)(2,1)S(1)}, u32[]{:S(2)}, u32[]{:S(2)}) collective-permute-start(bf16[3,256,128]{2,1,0:T(8,128)(2,1)S(1)} %get-tuple-element.70), channel_id=1, source_target_pairs={{0,12},{4,0},{8,4},{12,8},{1,13},{5,1},{9,5},{13,9},{2,14},{6,2},{... | collective-permute-start | bytes 589832 | tf_op jit(solution)/shard_map/ppermute | solution.py:572
  7.7 1.0 %copy-start = (bf16[256,2,4,128]{3,2,1,0:T(4,128)(2,1)S(1)}, bf16[256,2,4,128]{3,2,1,0:T(4,128)(2,1)}, u32[]{:S(2)}) copy-start(bf16[256,2,4,128]{3,2,1,0:T(4,128)(2,1)} %param.11) | copy-start | bytes 1572868
  8.8 1.0 %copy-start.1 = (bf16[256,2,4,128]{3,2,1,0:T(4,128)(2,1)S(1)}, bf16[256,2,4,128]{3,2,1,0:T(4,128)(2,1)}, u32[]{:S(2)}) copy-start(bf16[256,2,4,128]{3,2,1,0:T(4,128)(2,1)} %param.12) | copy-start | bytes 1572868
  19.4 16.9 %copy-start.5 = (bf16[256,4,128]{2,1,0:T(4,128)(2,1)S(1)}, bf16[256,4,128]{2,1,0:T(4,128)(2,1)}, u32[]{:S(2)}) copy-start(bf16[256,4,128]{2,1,0:T(4,128)(2,1)} %param.15) | copy-start | bytes 786436
  19.4 10.1 %collective-permute-start.3 = (bf16[4,128,128]{2,1,0:T(8,128)(2,1)S(1)}, bf16[4,128,128]{2,1,0:T(8,128)(2,1)S(1)}, u32[]{:S(2)}, u32[]{:S(2)}) collective-permute-start(bf16[4,128,128]{2,1,0:T(8,128)(2,1)S(1)} %convert_element_type.22), channel_id=1, source_target_pairs={{0,4},{4,8},{8,12},{1,5},{5,9},{9,13},{2,6},{6,10},{10,14},{3,7},{... | collective-permute-start | bytes 393224 | tf_op jit(solution)/shard_map/ppermute | solution.py:565
  27.8 5.1 %collective-permute-start.12 = (bf16[256,128]{1,0:T(8,128)(2,1)S(1)}, bf16[256,128]{1,0:T(8,128)(2,1)S(1)}, u32[]{:S(2)}, u32[]{:S(2)}) collective-permute-start(bf16[256,128]{1,0:T(8,128)(2,1)S(1)} %get-tuple-element.92), channel_id=1, source_target_pairs={{0,4},{4,8},{8,12},{12,0},{1,5},{5,9},{9,13},{13,1},{2,6},{6,10},{... | collective-permute-start | bytes 196616 | tf_op jit(solution)/shard_map/ppermute | solution.py:572
  27.9 5.0 %collective-permute-start.13 = (bf16[256,128]{1,0:T(8,128)(2,1)S(1)}, bf16[256,128]{1,0:T(8,128)(2,1)S(1)}, u32[]{:S(2)}, u32[]{:S(2)}) collective-permute-start(bf16[256,128]{1,0:T(8,128)(2,1)S(1)} %get-tuple-element.93), channel_id=1, source_target_pairs={{0,8},{4,12},{8,0},{12,4},{1,9},{5,13},{9,1},{13,5},{2,10},{6,14},... | collective-permute-start | bytes 196616 | tf_op jit(solution)/shard_map/ppermute | solution.py:572
  28.7 7.7 %collective-permute-start.14 = (bf16[256,128]{1,0:T(8,128)(2,1)S(1)}, bf16[256,128]{1,0:T(8,128)(2,1)S(1)}, u32[]{:S(2)}, u32[]{:S(2)}) collective-permute-start(bf16[256,128]{1,0:T(8,128)(2,1)S(1)} %get-tuple-element.94), channel_id=1, source_target_pairs={{0,12},{4,0},{8,4},{12,8},{1,13},{5,1},{9,5},{13,9},{2,14},{6,2},{... | collective-permute-start | bytes 196616 | tf_op jit(solution)/shard_map/ppermute | solution.py:572
  29.9 10.8 %collective-permute-start.4 = (bf16[4,128,128]{2,1,0:T(8,128)(2,1)S(1)}, bf16[4,128,128]{2,1,0:T(8,128)(2,1)S(1)}, u32[]{:S(2)}, u32[]{:S(2)}) collective-permute-start(bf16[4,128,128]{2,1,0:T(8,128)(2,1)S(1)} %fusion), channel_id=1, source_target_pairs={{0,4},{4,8},{8,12},{1,5},{5,9},{9,13},{2,6},{6,10},{10,14},{3,7},{... | collective-permute-start | bytes 393224 | tf_op jit(solution)/shard_map/ppermute | solution.py:565
  38.7 6.5 %collective-permute-start.15 = (bf16[4,128,128]{2,1,0:T(8,128)(2,1)S(1)}, bf16[4,128,128]{2,1,0:T(8,128)(2,1)S(1)}, u32[]{:S(2)}, u32[]{:S(2)}) collective-permute-start(bf16[4,128,128]{2,1,0:T(8,128)(2,1)S(1)} %convert_element_type.25), channel_id=1, source_target_pairs={{4,0},{8,4},{12,8},{5,1},{9,5},{13,9},{6,2},{10,6},{14,10},{7,3},{... | collective-permute-start | bytes 393224 | tf_op jit(solution)/shard_map/ppermute | solution.py:565
  40.9 6.6 %collective-permute-start.5 = (bf16[4,128,128]{2,1,0:T(8,128)(2,1)S(1)}, bf16[4,128,128]{2,1,0:T(8,128)(2,1)S(1)}, u32[]{:S(2)}, u32[]{:S(2)}) collective-permute-start(bf16[4,128,128]{2,1,0:T(8,128)(2,1)S(1)} %fusion.1), channel_id=1, source_target_pairs={{0,4},{4,8},{8,12},{1,5},{5,9},{9,13},{2,6},{6,10},{10,14},{3,7},{... | collective-permute-start | bytes 393224 | tf_op jit(solution)/shard_map/ppermute | solution.py:565
  45.6 7.2 %collective-permute-start.16 = (bf16[4,128,128]{2,1,0:T(8,128)(2,1)S(1)}, bf16[4,128,128]{2,1,0:T(8,128)(2,1)S(1)}, u32[]{:S(2)}, u32[]{:S(2)}) collective-permute-start(bf16[4,128,128]{2,1,0:T(8,128)(2,1)S(1)} %fusion.2), channel_id=1, source_target_pairs={{4,0},{8,4},{12,8},{5,1},{9,5},{13,9},{6,2},{10,6},{14,10},{7,3},{... | collective-permute-start | bytes 393224 | tf_op jit(solution)/shard_map/ppermute | solution.py:565
  50.0 7.4 %collective-permute-start.6 = (bf16[256,128]{1,0:T(8,128)(2,1)S(1)}, bf16[256,128]{1,0:T(8,128)(2,1)S(1)}, u32[]{:S(2)}, u32[]{:S(2)}) collective-permute-start(bf16[256,128]{1,0:T(8,128)(2,1)S(1)} %get-tuple-element.84), channel_id=1, source_target_pairs={{0,4},{4,8},{8,12},{12,0},{1,5},{5,9},{9,13},{13,1},{2,6},{6,10},{... | collective-permute-start | bytes 196616 | tf_op jit(solution)/shard_map/ppermute | solution.py:572
  51.5 5.9 %collective-permute-start.7 = (bf16[256,128]{1,0:T(8,128)(2,1)S(1)}, bf16[256,128]{1,0:T(8,128)(2,1)S(1)}, u32[]{:S(2)}, u32[]{:S(2)}) collective-permute-start(bf16[256,128]{1,0:T(8,128)(2,1)S(1)} %get-tuple-element.85), channel_id=1, source_target_pairs={{0,8},{4,12},{8,0},{12,4},{1,9},{5,13},{9,1},{13,5},{2,10},{6,14},... | collective-permute-start | bytes 196616 | tf_op jit(solution)/shard_map/ppermute | solution.py:572
  51.5 5.9 %collective-permute-start.8 = (bf16[256,128]{1,0:T(8,128)(2,1)S(1)}, bf16[256,128]{1,0:T(8,128)(2,1)S(1)}, u32[]{:S(2)}, u32[]{:S(2)}) collective-permute-start(bf16[256,128]{1,0:T(8,128)(2,1)S(1)} %get-tuple-element.86), channel_id=1, source_target_pairs={{0,12},{4,0},{8,4},{12,8},{1,13},{5,1},{9,5},{13,9},{2,14},{6,2},{... | collective-permute-start | bytes 196616 | tf_op jit(solution)/shard_map/ppermute | solution.py:572
  53.2 13.8 %collective-permute-start.17 = (bf16[4,128,128]{2,1,0:T(8,128)(2,1)S(1)}, bf16[4,128,128]{2,1,0:T(8,128)(2,1)S(1)}, u32[]{:S(2)}, u32[]{:S(2)}) collective-permute-start(bf16[4,128,128]{2,1,0:T(8,128)(2,1)S(1)} %fusion.3), channel_id=1, source_target_pairs={{4,0},{8,4},{12,8},{5,1},{9,5},{13,9},{6,2},{10,6},{14,10},{7,3},{... | collective-permute-start | bytes 393224 | tf_op jit(solution)/shard_map/ppermute | solution.py:565
  57.4 9.6 %copy-start.8 = (f32[4,256]{1,0:T(4,128)S(1)}, f32[4,256]{1,0:T(4,128)}, u32[]{:S(2)}) copy-start(f32[4,256]{1,0:T(4,128)} %decays_ref.3) | copy-start | bytes 12292
  63.5 9.7 %collective-permute-start.9 = (bf16[3,256,128]{2,1,0:T(8,128)(2,1)S(1)}, bf16[3,256,128]{2,1,0:T(8,128)(2,1)S(1)}, u32[]{:S(2)}, u32[]{:S(2)}) collective-permute-start(bf16[3,256,128]{2,1,0:T(8,128)(2,1)S(1)} %get-tuple-element.88), channel_id=1, source_target_pairs={{0,4},{4,8},{8,12},{12,0},{1,5},{5,9},{9,13},{13,1},{2,6},{6,10},{... | collective-permute-start | bytes 589832 | tf_op jit(solution)/shard_map/ppermute | solution.py:572
  63.6 9.6 %collective-permute-start.10 = (bf16[3,256,128]{2,1,0:T(8,128)(2,1)S(1)}, bf16[3,256,128]{2,1,0:T(8,128)(2,1)S(1)}, u32[]{:S(2)}, u32[]{:S(2)}) collective-permute-start(bf16[3,256,128]{2,1,0:T(8,128)(2,1)S(1)} %get-tuple-element.89), channel_id=1, source_target_pairs={{0,8},{4,12},{8,0},{12,4},{1,9},{5,13},{9,1},{13,5},{2,10},{6,14},... | collective-permute-start | bytes 589832 | tf_op jit(solution)/shard_map/ppermute | solution.py:572
  65.6 17.9 %collective-permute-start.11 = (bf16[3,256,128]{2,1,0:T(8,128)(2,1)S(1)}, bf16[3,256,128]{2,1,0:T(8,128)(2,1)S(1)}, u32[]{:S(2)}, u32[]{:S(2)}) collective-permute-start(bf16[3,256,128]{2,1,0:T(8,128)(2,1)S(1)} %get-tuple-element.90), channel_id=1, source_target_pairs={{0,12},{4,0},{8,4},{12,8},{1,13},{5,1},{9,5},{13,9},{2,14},{6,2},{... | collective-permute-start | bytes 589832 | tf_op jit(solution)/shard_map/ppermute | solution.py:572
  (3 other events, 2.3 us)

commit v3 on v2

--- a/solution.py
+++ b/solution.py
@@ -14,6 +14,8 @@
 C = 64
 N = 128
 LIMIT = 16 * 1024 * 1024
+SENDLIMIT = 58 * 1024 * 1024
+SENDFLOPS = 20 << 30
 
 
 def split(a):
@@ -117,18 +119,22 @@
 BETA, READ, TAIL, SCALE = range(4)
 
 
+def pair_product(ah, al, bh, bl):
+    wide = jnp.concatenate([bh, bl], axis=1)
+    both = contract(jnp.concatenate([ah, al], axis=1), jnp.concatenate([wide, wide], axis=0), 1, 0)
+    half = bh.shape[1]
+    return both[:, :half] + both[:, half:]
+
+
 def local_kernel(heads, count, dk_ref, dv_ref, betas_ref, decays_ref,
                  k_ref, kt_ref, inv_ref, p_ref, y_ref, t_ref, o_ref, fade_ref, see_ref, run_ref, col_ref,
-                 tsh_ref, osh_ref, low_scr, keys_scr, values_scr, sys_scr, rhs_scr, sem):
-    copies = [pltpu.make_async_copy(ref, low_scr.at[m], sem.at[m]) for m, ref in enumerate((dk_ref, dv_ref))]
-    for copy in copies:
-        copy.start()
+                 tsh_ref, osh_ref, low_ref,
+                 keys_scr, values_scr, sys_scr, full_scr, split_scr, half_scr, rhs_scr):
     grid = Grid()
-    for m, scr in enumerate((keys_scr, values_scr)):
-        copies[m].wait()
-        scr[...] = low_scr[m].astype(F32)
     eye = jnp.where(grid.diag, 1.0, 0.0)
     items = [(h, c) for h in range(heads) for c in range(count)]
+    keys_scr[...] = dk_ref[...].astype(F32)
+    values_scr[...] = dv_ref[...].astype(F32)
     ends = {}
     for h, c in items:
         raw = pair_rows(keys_scr, heads, h, c)
@@ -150,22 +156,31 @@
         kt_ref[h, c] = keys * tail
         fade_ref[h, c] = fade
         system = fade * mm_nt(keys, keys)
-        sys_scr[h, c] = system
-        inv_ref[h, c] = eye - jnp.where(grid.differ == 1, system, 0.0)
+        sys_scr[0, h, c], sys_scr[1, h, c] = split(system)
+        inverse = eye - jnp.where(grid.differ == 1, system, 0.0)
+        inv_ref[h, c] = inverse
+        split_scr[0, h, c], split_scr[1, h, c] = split(inverse)
         rhs_scr[h, c, :, :N] = read * keys
         rhs_scr[h, c, :, N:] = beta * values
         ends[h, c] = jnp.exp(end)
     for level in range(1, 7):
         near = (grid.differ >= (1 << level)) & (grid.differ < (2 << level))
-        half = {}
-        for i in items:
-            half[i] = mm(jnp.where(near, sys_scr[i], 0.0), inv_ref[i])
-        for i in items:
-            inv_ref[i] = inv_ref[i] - mm(inv_ref[i], half[i])
-    for i in items:
-        both = mm(inv_ref[i], rhs_scr[i])
-        p_ref[i] = both[:, :N]
-        y_ref[i] = both[:, N:]
+        near = jnp.where(near, 1.0, 0.0).astype(BF16)
+        for h, c in items:
+            half = pair_product(
+                sys_scr[0, h, c] * near, sys_scr[1, h, c] * near, split_scr[0, h, c], split_scr[1, h, c]
+            )
+            half_scr[0, h, c], half_scr[1, h, c] = split(half)
+        for h, c in items:
+            inverse = inv_ref[h, c] - pair_product(
+                split_scr[0, h, c], split_scr[1, h, c], half_scr[0, h, c], half_scr[1, h, c]
+            )
+            inv_ref[h, c] = inverse
+            split_scr[0, h, c], split_scr[1, h, c] = split(inverse)
+    for h, c in items:
+        both = pair_product(split_scr[0, h, c], split_scr[1, h, c], *split(rhs_scr[h, c]))
+        p_ref[h, c] = both[:, :N]
+        y_ref[h, c] = both[:, N:]
     for i in items:
         maps = mm_tn(kt_ref[i], jnp.concatenate([p_ref[i], y_ref[i]], axis=1))
         t_ref[i] = ends[i] * eye - maps[:, :N]
@@ -178,6 +193,9 @@
             both = mm(t_ref[h, c], jnp.concatenate([tsh_ref[h], osh_ref[h]], axis=1))
             tsh_ref[h] = both[:, :N]
             osh_ref[h] = both[:, N:] + o_ref[h, c]
+    for h in range(heads):
+        low_ref[0, h] = osh_ref[h].astype(BF16)
+        low_ref[1, h] = tsh_ref[h].astype(BF16)
 
 
 def gather_blocks(place_ref, refs, scr, sem, first):
@@ -202,12 +220,12 @@
     return ref[pl.ds(c * C * heads + h, C, stride=heads), :]
 
 
-def readout_kernel(heads, count, place_ref, g_ref, s_in_ref, k_ref, p_ref, y_ref, t_ref, o_ref, see_ref, run_ref,
+def readout_kernel(heads, count, place_ref, g_ref, near_ref, far_ref, k_ref, p_ref, y_ref, t_ref, o_ref, see_ref, run_ref,
                    s_ref, u_ref, dw_ref, dq_ref, *rest):
     outs, (g_scr, dq_scr, sem) = rest[:heads], rest[heads:]
     g_scr[...] = g_ref[...].astype(F32)
     for h in range(heads):
-        s_ref[h, 0] = s_in_ref[h].astype(F32)
+        s_ref[h, 0] = near_ref[0, h].astype(F32) + contract(near_ref[1, h], far_ref[h], 1, 0)
     for c in range(count):
         for h in range(heads):
             both = mm(jnp.concatenate([t_ref[h, c], p_ref[h, c]], axis=0), s_ref[h, c])
@@ -235,8 +253,8 @@
     return raw * lax.rsqrt(jnp.mean(raw * raw, axis=1, keepdims=True) + EPS)
 
 
-def source_kernel(heads, count, place_ref, g_ref, k_ref, p_ref, t_ref, see_ref, run_ref, *rest):
-    ins, (q_ref, z_ref, b_ref, bsh_ref, g_scr, q_scr, sem) = rest[:heads], rest[heads:]
+def source_kernel(heads, count, place_ref, g_ref, k_ref, p_ref, t_ref, see_ref, run_ref, map_ref, *rest):
+    ins, (q_ref, z_ref, b_ref, bsh_ref, low_ref, g_scr, q_scr, sem) = rest[:heads], rest[heads:]
     copies = gather_blocks(place_ref, ins, q_scr, sem, 0)
     for copy in copies:
         copy.start()
@@ -260,15 +278,18 @@
     for c in range(count - 2, -1, -1):
         for h in range(heads):
             bsh_ref[h] = b_ref[h, c] + mm_tn(t_ref[h, c], bsh_ref[h])
-
-
-def final_kernel(heads, count, decays_ref, lam_ref, k_ref, kt_ref, inv_ref, t_ref, fade_ref, col_ref,
+    for h in range(heads):
+        low_ref[0, h] = bsh_ref[h].astype(BF16)
+        low_ref[1, h] = map_ref[1, h]
+
+
+def final_kernel(heads, count, decays_ref, near_ref, far_ref, k_ref, kt_ref, inv_ref, t_ref, fade_ref, col_ref,
                  s_ref, u_ref, dw_ref, dq_ref, q_ref, z_ref, b_ref,
                  gk_ref, gv_ref, gb_ref, gd_ref, gk_scr, gv_scr, lam_scr, r_scr, d_scr, rd_scr):
     grid = Grid()
     items = [(h, c) for h in range(heads) for c in range(count)]
     for h in range(heads):
-        lam_scr[h, count - 1] = lam_ref[h].astype(F32)
+        lam_scr[h, count - 1] = near_ref[0, h].astype(F32) + contract(near_ref[1, h], far_ref[h], 0, 0)
     for c in range(count - 1, 0, -1):
         for h in range(heads):
             lam_scr[h, c - 1] = mm_tn(t_ref[h, c], lam_scr[h, c]) + b_ref[h, c]
@@ -321,6 +342,7 @@
 
 
 ANY = pl.BlockSpec(memory_space=pl.ANY)
+HBM = pl.BlockSpec(memory_space=pltpu.HBM)
 SCALAR = pl.BlockSpec(memory_space=pltpu.SMEM)
 VM = pl.BlockSpec(memory_space=pltpu.VMEM)
 
@@ -329,7 +351,7 @@
     return jax.ShapeDtypeStruct(shape, dtype)
 
 
-def single(body, name, in_specs, outs, out_specs, scratch, flops):
+def single(body, name, in_specs, outs, out_specs, scratch, flops, limit=LIMIT):
     return pl.pallas_call(
         body,
         name=name,
@@ -337,7 +359,7 @@
         out_shape=outs,
         out_specs=out_specs,
         scratch_shapes=scratch,
-        compiler_params=pltpu.CompilerParams(vmem_limit_bytes=LIMIT),
+        compiler_params=pltpu.CompilerParams(vmem_limit_bytes=limit),
         cost_estimate=pl.CostEstimate(flops=flops, bytes_accessed=4 << 20, transcendentals=0),
     )
 
@@ -346,53 +368,53 @@
     heads, rows = decays.shape
     count = rows // C
     square, thin, one = (shaped((heads,) + tail) for tail in ((count, N, N), (count, C, N), (N, N)))
-    outs = [square] * 8 + [thin] * 2 + [square] + [one] * 2
+    outs = [square] * 8 + [thin] * 2 + [square] + [one] * 2 + [shaped((2, heads, N, N), BF16)]
+    halves = pltpu.VMEM((2, heads, count, N, N), BF16)
     return single(
         functools.partial(local_kernel, heads, count), "delta_local",
-        [ANY, ANY, VM, VM], outs, [VM] * len(outs),
-        [pltpu.VMEM((2,) + dk.shape, BF16)] + [pltpu.VMEM(dk.shape, F32)] * 2
-        + [pltpu.VMEM((heads, count, N, N), F32), pltpu.VMEM((heads, count, N, 2 * N), F32),
-           pltpu.SemaphoreType.DMA((2,))],
+        [VM] * 4, outs, [VM] * len(outs),
+        [pltpu.VMEM(dk.shape, F32)] * 2 + [halves, pltpu.VMEM(square.shape, F32), halves, halves]
+        + [pltpu.VMEM((heads, count, N, 2 * N), F32)],
         10 << 30,
     )(dk, dv, betas, decays)
 
 
-def delta_readout(place, g, entry, k, p, y, t, o, see, run):
+def delta_readout(place, g, near, far, k, p, y, t, o, see, run):
     heads, count = k.shape[:2]
     rows = count * C
     square, thin = (shaped((heads,) + tail) for tail in ((count, N, N), (count, C, N)))
     outs = [shaped((heads, count + 1, N, N)), square, thin, thin]
     return single(
         functools.partial(readout_kernel, heads, count), "delta_readout",
-        [SCALAR] + [VM] * 9, outs + [shaped((rows, N), BF16)] * heads, [VM] * 4 + [ANY] * heads,
+        [SCALAR] + [VM] * 10, outs + [shaped((rows, N), BF16)] * heads, [VM] * 4 + [ANY] * heads,
         [pltpu.VMEM(g.shape, F32), pltpu.VMEM((heads, rows, N), BF16), pltpu.SemaphoreType.DMA((heads,))],
         3 << 30,
-    )(place, g, entry, k, p, y, t, o, see, run)
-
-
-def delta_source(place, g, k, p, t, see, run, attended):
+    )(place, g, near, far, k, p, y, t, o, see, run)
+
+
+def delta_source(place, g, k, p, t, see, run, low, attended):
     heads, count = k.shape[:2]
     rows = count * C
     square, thin = (shaped((heads,) + tail) for tail in ((count, N, N), (count, C, N)))
     return single(
         functools.partial(source_kernel, heads, count), "delta_source",
-        [SCALAR] + [VM] * 6 + [ANY] * heads,
-        [thin, square, square, shaped((heads, N, N))], [VM] * 4,
+        [SCALAR] + [VM] * 7 + [ANY] * heads,
+        [thin, square, square, shaped((heads, N, N)), shaped(low.shape, BF16)], [VM] * 5,
         [pltpu.VMEM(g.shape, F32), pltpu.VMEM((heads, rows, N), BF16), pltpu.SemaphoreType.DMA((heads,))],
         3 << 30,
-    )(place, g, k, p, t, see, run, *attended)
-
-
-def delta_final(betas, decays, lam, k, kt, inv, t, fade, col, s, u, dw, dq, q, z, b):
+    )(place, g, k, p, t, see, run, low, *attended)
+
+
+def delta_final(betas, decays, near, far, k, kt, inv, t, fade, col, s, u, dw, dq, q, z, b):
     heads, count = k.shape[:2]
     wide = (2 * count * C * heads, N)
     return single(
         functools.partial(final_kernel, heads, count), "delta_final",
-        [VM] * 15,
+        [VM] * 16,
         [shaped(wide, BF16), shaped(wide, BF16), shaped(betas.shape), shaped(decays.shape)], [VM] * 4,
         [pltpu.VMEM(wide, F32)] * 2 + [pltpu.VMEM((heads, count, N, N), F32)] * 4,
         8 << 30,
-    )(decays, lam, k, kt, inv, t, fade, col, s, u, dw, dq, q, z, b)
+    )(decays, near, far, k, kt, inv, t, fade, col, s, u, dw, dq, q, z, b)
 
 
 def rounds(refs, index, count, sign):
@@ -426,20 +448,20 @@
 
 
 def attend_kernel(count, scale, place_ref, *rest):
-    ins, (prob_ref, mixed_ref), outs = rest[:count], rest[count:count + 2], rest[count + 2:2 * count + 2]
-    scr, att_scr, sem = rest[2 * count + 2:]
-    copies = gather_blocks(place_ref, ins, scr, sem, 0)
+    ins, (whole_ref, prob_ref, mixed_ref), outs = rest[:count], rest[count:count + 3], rest[count + 3:2 * count + 3]
+    att_scr, sem = rest[2 * count + 3:]
+    copies = gather_blocks(place_ref, ins, whole_ref, sem, 0)
     for copy in copies:
         copy.start()
     for copy in copies:
         copy.wait()
-    rows = scr.shape[2]
+    rows = whole_ref.shape[2]
     causal = iota((rows, rows), 0) <= iota((rows, rows), 1)
     for i in range(count):
-        query = scr[i, 0]
+        query = whole_ref[i, 0]
         pieces = []
         for j in range(i + 1):
-            score = contract(scr[j, 1], query, 1, 1) * scale
+            score = contract(whole_ref[j, 1], query, 1, 1) * scale
             pieces.append(jnp.where(causal, score, -jnp.inf) if j == i else score)
         top = pieces[0].max(axis=0, keepdims=True)
         for piece in pieces[1:]:
@@ -448,32 +470,33 @@
         total = pieces[0].sum(axis=0, keepdims=True)
         for piece in pieces[1:]:
             total = total + piece.sum(axis=0, keepdims=True)
+        share = 1.0 / total
         mixed = None
         for j, piece in enumerate(pieces):
-            low = (piece / total).astype(BF16)
+            low = (piece * share).astype(BF16)
             prob_ref[i * (i + 1) // 2 + j] = low
-            term = contract(low, scr[j, 2], 0, 0)
+            term = contract(low, whole_ref[j, 2], 0, 0)
             mixed = term if mixed is None else mixed + term
         mixed_ref[i] = mixed
         att_scr[i] = mixed.astype(BF16)
-    copies = scatter_blocks(place_ref, att_scr, outs, sem, 0)
+    copies = scatter_blocks(place_ref, att_scr, outs, sem, count)
     for copy in copies:
         copy.start()
     for copy in copies:
         copy.wait()
 
 
-def attend_back_kernel(count, scale, place_ref, prob_ref, mixed_ref, *rest):
-    ins, grads, outs = rest[:count], rest[count:2 * count], rest[2 * count:3 * count]
-    scr, g_scr, out_scr, acc, sem = rest[3 * count:]
-    copies = gather_blocks(place_ref, ins, scr, sem, 0) + gather_blocks(place_ref, grads, g_scr, sem, count)
+def attend_back_kernel(count, scale, place_ref, prob_ref, mixed_ref, whole_ref, *rest):
+    grads, outs = rest[:count], rest[count:2 * count]
+    g_scr, out_scr, acc, sem = rest[2 * count:]
+    copies = gather_blocks(place_ref, grads, g_scr, sem, 0)
     for copy in copies:
         copy.start()
     for copy in copies:
         copy.wait()
-    rows = scr.shape[2]
+    rows = whole_ref.shape[2]
     ones = jnp.ones((8, N), F32)
-    for i in range(count):
+    for i in range(count - 1, -1, -1):
         mixed = mixed_ref[i]
         low = mixed.astype(BF16).astype(F32)
         grad = g_scr[i].astype(F32)
@@ -481,27 +504,26 @@
         pull = inv * (grad - low * (inv * inv * jnp.mean(low * grad, axis=1, keepdims=True)))
         pull = pull.astype(BF16)
         dots = mm_nt(ones, pull.astype(F32) * mixed)[:1]
-        query = scr[i, 0]
+        query = whole_ref[i, 0]
         gq = None
         for j in range(i + 1):
             prob = prob_ref[i * (i + 1) // 2 + j]
-            gp = contract(scr[j, 2], pull, 1, 1)
+            gp = contract(whole_ref[j, 2], pull, 1, 1)
             gs = (prob.astype(F32) * (gp - dots) * scale).astype(BF16)
-            term = contract(gs, scr[j, 1], 0, 0)
+            term = contract(gs, whole_ref[j, 1], 0, 0)
             gq = term if gq is None else gq + term
             gk = contract(gs, query, 1, 0)
             gv = contract(prob, pull, 1, 0)
+            if i < count - 1:
+                gk, gv = gk + acc[j, 0], gv + acc[j, 1]
             if i == j:
+                out_scr[j, 1] = gk.astype(BF16)
+                out_scr[j, 2] = gv.astype(BF16)
+            else:
                 acc[j, 0] = gk
                 acc[j, 1] = gv
-            else:
-                acc[j, 0] = acc[j, 0] + gk
-                acc[j, 1] = acc[j, 1] + gv
         out_scr[i, 0] = gq.astype(BF16)
-    for j in range(count):
-        out_scr[j, 1] = acc[j, 0].astype(BF16)
-        out_scr[j, 2] = acc[j, 1].astype(BF16)
-    copies = scatter_blocks(place_ref, out_scr, outs, sem, 0)
+    copies = scatter_blocks(place_ref, out_scr, outs, sem, count)
     for copy in copies:
         copy.start()
     for copy in copies:
@@ -512,9 +534,9 @@
     rows = q.shape[0] // count
     return single(
         functools.partial(send_kernel, count), "send_heads",
-        [SCALAR, ANY, ANY, ANY], [shaped((3, rows, N), BF16)] * count, [VM] * count,
+        [SCALAR, HBM, HBM, HBM], [shaped((3, rows, N), BF16)] * count, [VM] * count,
         [pltpu.VMEM((3,) + q.shape, BF16), pltpu.VMEM((3,) + q.shape, F32), pltpu.SemaphoreType.DMA((3,))],
-        1 << 28,
+        SENDFLOPS, SENDLIMIT,
     )(place, q, k, v)
 
 
@@ -536,24 +558,22 @@
     return single(
         functools.partial(attend_kernel, count, scale), "attend",
         [SCALAR] + [ANY] * count,
-        [shaped((tri, rows, rows), BF16), shaped((count, rows, N))] + [shaped((rows, N), BF16)] * count,
-        [VM, VM] + [ANY] * count,
-        [pltpu.VMEM((count, 3, rows, N), BF16), pltpu.VMEM((count, rows, N), BF16),
-         pltpu.SemaphoreType.DMA((count,))], 2 << 30,
+        [shaped((count, 3, rows, N), BF16), shaped((tri, rows, rows), BF16), shaped((count, rows, N))]
+        + [shaped((rows, N), BF16)] * count,
+        [VM] * 3 + [ANY] * count,
+        [pltpu.VMEM((count, rows, N), BF16), pltpu.SemaphoreType.DMA((2 * count,))], 2 << 30,
     )(place, *parts)
 
 
-def attend_back(place, prob, mixed, parts, grads, scale):
-    count = len(parts)
-    rows = parts[0].shape[1]
+def attend_back(place, prob, mixed, whole, grads, scale):
+    count, _, rows, _ = whole.shape
     return single(
         functools.partial(attend_back_kernel, count, scale), "attend_back",
-        [SCALAR, VM, VM] + [ANY] * (2 * count),
+        [SCALAR, VM, VM, VM] + [ANY] * count,
         [shaped((3, rows, N), BF16)] * count, [ANY] * count,
-        [pltpu.VMEM((count, 3, rows, N), BF16), pltpu.VMEM((count, rows, N), BF16),
-         pltpu.VMEM((count, 3, rows, N), BF16), pltpu.VMEM((count, 2, rows, N), F32),
-         pltpu.SemaphoreType.DMA((2 * count,))], 4 << 30,
-    )(place, prob, mixed, *parts, *grads)
+        [pltpu.VMEM((count, rows, N), BF16), pltpu.VMEM((count, 3, rows, N), BF16),
+         pltpu.VMEM((count, 2, rows, N), F32), pltpu.SemaphoreType.DMA((2 * count,))], 4 << 30,
+    )(place, prob, mixed, whole, *grads)
 
 
 PRECISE = lax.Precision.HIGHEST
@@ -577,13 +597,12 @@
     return jnp.einsum("hij,hjk->hik", matrix, state, precision=PRECISE)
 
 
-def entering(matrix, offset, axis, step):
+def entering(low, matrix, offset, axis, step):
     count = lax.axis_size(axis)
     if count <= 4:
-        state = shifted(offset.astype(BF16), axis, step)
-        for hop in range(count - 2):
-            state = shifted((apply_map(matrix, state.astype(F32)) + offset).astype(BF16), axis, step)
-        return state
+        near = shifted(low, axis, step)
+        middle = (apply_map(matrix, near[0].astype(F32)) + offset).astype(BF16)
+        return near, shifted(middle, axis, 2 * step), middle
     place = lax.axis_index(axis)
     place = place if step > 0 else count - 1 - place
     eye = jnp.eye(matrix.shape[-1], dtype=F32)
@@ -594,7 +613,8 @@
         offset = apply_map(matrix, start) + offset
         matrix = apply_map(matrix, before)
         reach *= 2
-    return shifted(offset, axis, step).astype(BF16)
+    state = shifted(offset, axis, step).astype(BF16)
+    return jnp.stack([state, jnp.zeros_like(state)]), jnp.zeros_like(state), state
 
 
 def visible_pairs(rows, span):
@@ -660,33 +680,33 @@
         return array.reshape(-1, width)
 
     place = lax.axis_index("seq").astype(jnp.int32).reshape(1) if by_head else jnp.zeros((1,), jnp.int32)
-    pairs = flat(delta_keys)
+    extra = (flat(delta_keys), flat(delta_values), betas, decays)
     if by_head:
         parts = send_heads(place, flat(queries), flat(keys), flat(values), count)
-        pairs, parts = lax.optimization_barrier((pairs, parts))
+        first, parts = lax.optimization_barrier((extra[0], parts))
+        extra = (first,) + extra[1:]
         parts = rotated(parts, "seq")
     cot = flat(grad_out)
-    k, kt, inverse, p, y, t, o, fade, see, run, col, shard_t, shard_o = delta_local(
-        pairs, flat(delta_values), betas, decays
-    )
-    entry = entering(shard_t, shard_o, "seq", 1)
+    k, kt, inverse, p, y, t, o, fade, see, run, col, shard_t, shard_o, low = delta_local(*extra)
+    near, far, middle = entering(low, shard_t, shard_o, "seq", 1)
     if by_head:
-        prob, mixed, *attended = attend(place, parts, scale)
+        whole, prob, mixed, *attended = attend(place, parts, scale)
         attended = rotated(attended, "seq")
     else:
         saved = window_forward(queries, keys, values, scale)
-        low = saved[3].astype(BF16)
-        attended = [low[:, (heads - s) % heads] for s in range(heads)]
-    s, u, dw, dq, *pulls = delta_readout(place, cot, entry, k, p, y, t, o, see, run)
+        rounded = saved[3].astype(BF16)
+        attended = [rounded[:, (heads - s) % heads] for s in range(heads)]
+    s, u, dw, dq, *pulls = delta_readout(place, cot, near, far, k, p, y, t, o, see, run)
     if by_head:
         pulls = rotated(pulls, "seq")
-        outs = rotated(attend_back(place, prob, mixed, parts, pulls, scale), "seq")
+        outs = rotated(attend_back(place, prob, mixed, whole, pulls, scale), "seq")
     else:
         grads = window_backward(queries, *saved, jnp.stack(pulls, axis=1), scale)
-    q, z, b, shard_source = delta_source(place, cot, k, p, t, see, run, attended)
-    leaving = entering(jnp.swapaxes(shard_t, 1, 2), shard_source, "seq", -1)
+    attended, _ = lax.optimization_barrier((attended, middle))
+    q, z, b, shard_source, low = delta_source(place, cot, k, p, t, see, run, low, attended)
+    near, far, _ = entering(low, jnp.swapaxes(shard_t, 1, 2), shard_source, "seq", -1)
     grad_keys, grad_values, grad_betas, grad_decays = delta_final(
-        betas, decays, leaving, k, kt, inverse, t, fade, col, s, u, dw, dq, q, z, b
+        betas, decays, near, far, k, kt, inverse, t, fade, col, s, u, dw, dq, q, z, b
     )
     if by_head:
         outs, grad_keys = lax.optimization_barrier((outs, grad_keys))

time: 85.1 us -> 78.9 us (0.927)
  waiting for transfers between devices: 17.4 us -> 24.8 us
  starting transfers between devices: 28.3 us -> 21.2 us
  local copies, waits for them, and re-layouts: 6.32 us -> 0.03 us
  Pallas kernels: 30.2 us -> 31.1 us
    ppermute x6 -> x4, starting transfers between devices: 16.5 us -> 9.5 us  [shifted(): lax.ppermute(value, axis, [(source, source + steps) for source in range(i...]
    ppermute x12, waiting for transfers between devices: 16.6 us -> 23.5 us  [rotated(): lax.ppermute(parts[s], axis, [(d, (d + s) % count) for d in range(count)])]
    unnamed x18 -> x12, local copies, waits for them, and re-layouts: 6.32 us -> 0.03 us
    pallas_call x2, Pallas kernels: 8.6 us -> 10.3 us  [the longest x1 8.08 us: delta_local(): single(functools.partial(local_kernel, heads, count), 'delta_local', [VM]...]
    pallas_call x1, Pallas kernels: 6.09 us -> 4.97 us  [attend_back(): single(functools.partial(attend_back_kernel, count, scale), 'attend_back'...]
  transfers between devices with their start and end apart: 18 -> 16, of which waited for: 4 -> 7; matrix products, arithmetic and copies ran while one was open for 2% -> 1% of each run, Pallas kernels for 34% -> 35%
where the time goes in v3:
time: 78.9 us; the launch traced here: 78.7 us
  Pallas kernels  31.1 us (39%)
  waiting for transfers between devices  24.8 us (31%)
  starting transfers between devices  21.2 us (27%)
  between operations  0.86 us (1%)
    ppermute x12, waiting for transfers between devices, rotated(): lax.ppermute(parts[s], axis, [(d, (d + s) % count) for d in range(count)])  23.5 us
    ppermute x12, starting transfers between devices, rotated(): lax.ppermute(parts[s], axis, [(d, (d + s) % count) for d in range(count)])  11.7 us
    ppermute x4, starting transfers between devices, shifted(): lax.ppermute(value, axis, [(source, source + steps) for source in range(i...  9.5 us
    pallas_call x1, Pallas kernels, delta_local(): single(functools.partial(local_kernel, heads, count), 'delta_local', [VM]...  8.08 us
    pallas_call x1, Pallas kernels, delta_final(): single(functools.partial(final_kernel, heads, count), 'delta_final', [VM]...  6.28 us
    pallas_call x1, Pallas kernels, attend_back(): single(functools.partial(attend_back_kernel, count, scale), 'attend_back'...  4.97 us
    pallas_call x1, Pallas kernels, attend(): single(functools.partial(attend_kernel, count, scale), 'attend', [SCALAR]...  3.54 us
    pallas_call x1, Pallas kernels, delta_readout(): single(functools.partial(readout_kernel, heads, count), 'delta_readout',...  2.6 us
  transfers between devices with their start and end apart: 16, of which 7 were waited for; matrix products, arithmetic and copies ran while one was open for 1% of the time, Pallas kernels for 35%

profile of v3, /device:TPU:9, one launch (start us, length us, event | category | flops | bytes accessed | tf_op | source)
XLA Modules:
  0.0 78.7 jit_solution(1647903042872989440)
XLA Ops:
  0.7 2.2 %send_heads.1 = (bf16[3,256,128]{2,1,0:T(8,128)(2,1)}, bf16[3,256,128]{2,1,0:T(8,128)(2,1)}, bf16[3,256,128]{2,1,0:T(8,128)(2,1)}, bf16[3,256,128]{2,1,0:T(8,128)(2,1)}) custom-call(s32[1]{0:T(128)} %bitcast.place_ref, bf16[1024,128]{1,0:T(8,128)(2,1)} %bitcast.24, bf16[1024,128]{1,0:T(8,128)(2,1)} %bitcast.25, bf16[1024,128]{1,0:T(8,128)(2,1)} %bitcast.26), custom_call_target="tpu_custom_call" | custom-call | flops 21474836480 | bytes 4194304 | tf_op jit(solution)/shard_map/send_heads/pallas_call | solution.py:535
  2.9 1.3 %collective-permute-start = (bf16[3,256,128]{2,1,0:T(8,128)(2,1)}, bf16[3,256,128]{2,1,0:T(8,128)(2,1)S(1)}, u32[]{:S(2)}, u32[]{:S(2)}) collective-permute-start(bf16[3,256,128]{2,1,0:T(8,128)(2,1)} %get-tuple-element.75), channel_id=1, source_target_pairs={{0,4},{4,8},{8,12},{12,0},{1,5},{5,9},{9,13},{13,1},{2,6},{6,10},{... | collective-permute-start | bytes 589832 | tf_op jit(solution)/shard_map/ppermute | solution.py:592
  5.4 1.4 %collective-permute-start.2 = (bf16[3,256,128]{2,1,0:T(8,128)(2,1)}, bf16[3,256,128]{2,1,0:T(8,128)(2,1)S(1)}, u32[]{:S(2)}, u32[]{:S(2)}) collective-permute-start(bf16[3,256,128]{2,1,0:T(8,128)(2,1)} %get-tuple-element.77), channel_id=1, source_target_pairs={{0,12},{4,0},{8,4},{12,8},{1,13},{5,1},{9,5},{13,9},{2,14},{6,2},{... | collective-permute-start | bytes 589832 | tf_op jit(solution)/shard_map/ppermute | solution.py:592
  6.8 8.1 %delta_local.1 = (f32[4,4,128,128]{3,2,1,0:T(8,128)S(1)}, f32[4,4,128,128]{3,2,1,0:T(8,128)S(1)}, f32[4,4,128,128]{3,2,1,0:T(8,128)S(1)}, f32[4,4,128,128]{3,2,1...) custom-call(bf16[2048,128]{1,0:T(8,128)(2,1)S(1)} %bitcast.20, ...), custom_call_target="tpu_custom_call" | custom-call | flops 10737418240 | bytes 4194304 | tf_op jit(solution)/shard_map/delta_local/pallas_call | solution.py:373
  14.9 2.1 %collective-permute-start.3 = (bf16[2,4,128,128]{3,2,1,0:T(8,128)(2,1)S(1)}, bf16[2,4,128,128]{3,2,1,0:T(8,128)(2,1)S(1)}, u32[]{:S(2)}, u32[]{:S(2)}) collective-permute-start(bf16[2,4,128,128]{3,2,1,0:T(8,128)(2,1)S(1)} %get-tuple-element.82.map_ref), channel_id=1, source_target_pairs={{0,4},{4,8},{8,12},{1,5},{5,9},{9,13},{2,6},{6,10},{10,14},{3,7},{... | collective-permute-start | bytes 786440 | tf_op jit(solution)/shard_map/ppermute | solution.py:585
  17.0 3.8 %collective-permute-done.1.rest_2_ = bf16[3,256,128]{2,1,0:T(8,128)(2,1)S(1)} collective-permute-done((bf16[3,256,128]{2,1,0:T(8,128)(2,1)}, bf16[3,256,128]{2,1,0:T(8,128)(2,1)S(1)}, u32[]{:S(2)}, u32[]{:S(2)}) %collective-permute-start.1) | collective-permute-done | bytes 196640 | tf_op jit(solution)/shard_map/ppermute | solution.py:592
  20.8 2.7 %collective-permute-done.2.rest_3_ = bf16[3,256,128]{2,1,0:T(8,128)(2,1)S(1)} collective-permute-done((bf16[3,256,128]{2,1,0:T(8,128)(2,1)}, bf16[3,256,128]{2,1,0:T(8,128)(2,1)S(1)}, u32[]{:S(2)}, u32[]{:S(2)}) %collective-permute-start.2) | collective-permute-done | bytes 196640 | tf_op jit(solution)/shard_map/ppermute | solution.py:592
  23.5 3.5 %attend.1 = (bf16[4,3,256,128]{3,2,1,0:T(8,128)(2,1)S(1)}, bf16[10,256,256]{2,1,0:T(8,128)(2,1)S(1)}, f32[4,256,128]{2,1,0:T(8,128)S(1)}, bf16[256,128]{1,0:T(8,...) custom-call(s32[1]{0:T(128)} %bitcast.place_ref, ...), custom_call_target="tpu_custom_call" | custom-call | flops 2147483648 | bytes 4194304 | tf_op jit(solution)/shard_map/attend/pallas_call | solution.py:558
  27.5 1.4 %collective-permute-start.13 = (bf16[256,128]{1,0:T(8,128)(2,1)S(1)}, bf16[256,128]{1,0:T(8,128)(2,1)S(1)}, u32[]{:S(2)}, u32[]{:S(2)}) collective-permute-start(bf16[256,128]{1,0:T(8,128)(2,1)S(1)} %get-tuple-element.103), channel_id=1, source_target_pairs={{0,12},{4,0},{8,4},{12,8},{1,13},{5,1},{9,5},{13,9},{2,14},{6,2},{... | collective-permute-start | bytes 196616 | tf_op jit(solution)/shard_map/ppermute | solution.py:592
  29.1 4.2 %collective-permute-start.4 = (bf16[4,128,128]{2,1,0:T(8,128)(2,1)S(1)}, bf16[4,128,128]{2,1,0:T(8,128)(2,1)S(1)}, u32[]{:S(2)}, u32[]{:S(2)}) collective-permute-start(bf16[4,128,128]{2,1,0:T(8,128)(2,1)S(1)} %fusion), channel_id=1, source_target_pairs={{0,8},{4,12},{1,9},{5,13},{2,10},{6,14},{3,11},{7,15},{16,24},{20,... | collective-permute-start | bytes 393224 | tf_op jit(solution)/shard_map/ppermute | solution.py:585
  33.3 2.3 %collective-permute-done.13.rest_3_ = bf16[256,128]{1,0:T(8,128)(2,1)S(1)} collective-permute-done((bf16[256,128]{1,0:T(8,128)(2,1)S(1)}, bf16[256,128]{1,0:T(8,128)(2,1)S(1)}, u32[]{:S(2)}, u32[]{:S(2)}) %collective-permute-start.13) | collective-permute-done | bytes 65568 | tf_op jit(solution)/shard_map/ppermute | solution.py:592
  35.6 2.4 %delta_source.1 = (f32[4,4,64,128]{3,2,1,0:T(8,128)S(1)}, f32[4,4,128,128]{3,2,1,0:T(8,128)S(1)}, f32[4,4,128,128]{3,2,1,0:T(8,128)S(1)}, f32[4,128,128]{2,1,0:T(8,128)S(1)}, bf16[2,4,128,128]{3,2,1,0:T(8,128)(2,1)S(1)}) custom-call(s32[1]{0:T(128)} %bitcast.place_ref, bf16[1024,128]{1,0:T(8,128)(2,1)S(1)} %bitcast.22, ...), custom_call_target="tpu_custom_call" | custom-call | flops 3221225472 | bytes 4194304 | tf_op jit(solution)/shard_map/delta_source/pallas_call | solution.py:399
  38.0 1.9 %collective-permute-start.14 = (bf16[2,4,128,128]{3,2,1,0:T(8,128)(2,1)S(1)}, bf16[2,4,128,128]{3,2,1,0:T(8,128)(2,1)S(1)}, u32[]{:S(2)}, u32[]{:S(2)}) collective-permute-start(bf16[2,4,128,128]{3,2,1,0:T(8,128)(2,1)S(1)} %get-tuple-element.108), channel_id=1, source_target_pairs={{4,0},{8,4},{12,8},{5,1},{9,5},{13,9},{6,2},{10,6},{14,10},{7,3},{... | collective-permute-start | bytes 786440 | tf_op jit(solution)/shard_map/ppermute | solution.py:585
  40.0 2.6 %delta_readout.1 = (f32[4,5,128,128]{3,2,1,0:T(8,128)S(1)}, f32[4,4,128,128]{3,2,1,0:T(8,128)S(1)}, f32[4,4,64,128]{3,2,1,0:T(8,128)S(1)}, f32[4,4,64,128]{3,2,1...) custom-call(s32[1]{0:T(128)} %bitcast.place_ref, ...), custom_call_target="tpu_custom_call" | custom-call | flops 3221225472 | bytes 4194304 | tf_op jit(solution)/shard_map/delta_readout/pallas_call | solution.py:387
  42.6 1.5 %collective-permute-start.5 = (bf16[256,128]{1,0:T(8,128)(2,1)S(1)}, bf16[256,128]{1,0:T(8,128)(2,1)S(1)}, u32[]{:S(2)}, u32[]{:S(2)}) collective-permute-start(bf16[256,128]{1,0:T(8,128)(2,1)S(1)} %get-tuple-element.93), channel_id=1, source_target_pairs={{0,4},{4,8},{8,12},{12,0},{1,5},{5,9},{9,13},{13,1},{2,6},{6,10},{... | collective-permute-start | bytes 196616 | tf_op jit(solution)/shard_map/ppermute | solution.py:592
  44.1 1.2 %collective-permute-start.6 = (bf16[256,128]{1,0:T(8,128)(2,1)S(1)}, bf16[256,128]{1,0:T(8,128)(2,1)S(1)}, u32[]{:S(2)}, u32[]{:S(2)}) collective-permute-start(bf16[256,128]{1,0:T(8,128)(2,1)S(1)} %get-tuple-element.94), channel_id=1, source_target_pairs={{0,8},{4,12},{8,0},{12,4},{1,9},{5,13},{9,1},{13,5},{2,10},{6,14},... | collective-permute-start | bytes 196616 | tf_op jit(solution)/shard_map/ppermute | solution.py:592
  45.3 1.4 %collective-permute-start.7 = (bf16[256,128]{1,0:T(8,128)(2,1)S(1)}, bf16[256,128]{1,0:T(8,128)(2,1)S(1)}, u32[]{:S(2)}, u32[]{:S(2)}) collective-permute-start(bf16[256,128]{1,0:T(8,128)(2,1)S(1)} %get-tuple-element.95), channel_id=1, source_target_pairs={{0,12},{4,0},{8,4},{12,8},{1,13},{5,1},{9,5},{13,9},{2,14},{6,2},{... | collective-permute-start | bytes 196616 | tf_op jit(solution)/shard_map/ppermute | solution.py:592
  46.7 1.4 %collective-permute-done.14.near_ref = bf16[2,4,128,128]{3,2,1,0:T(8,128)(2,1)S(1)} collective-permute-done((bf16[2,4,128,128]{3,2,1,0:T(8,128)(2,1)S(1)}, bf16[2,4,128,128]{3,2,1,0:T(8,128)(2,1)S(1)}, u32[]{:S(2)}, u32[]{:S(2)}) %collective-permute-start.14) | collective-permute-done | bytes 262176 | tf_op jit(solution)/shard_map/ppermute | solution.py:585
  48.4 1.3 %collective-permute-start.15 = (bf16[4,128,128]{2,1,0:T(8,128)(2,1)S(1)}, bf16[4,128,128]{2,1,0:T(8,128)(2,1)S(1)}, u32[]{:S(2)}, u32[]{:S(2)}) collective-permute-start(bf16[4,128,128]{2,1,0:T(8,128)(2,1)S(1)} %fusion.1), channel_id=1, source_target_pairs={{8,0},{12,4},{9,1},{13,5},{10,2},{14,6},{11,3},{15,7},{24,16},{28,... | collective-permute-start | bytes 393224 | tf_op jit(solution)/shard_map/ppermute | solution.py:585
  49.7 2.9 %collective-permute-done.7.rest_3_ = bf16[256,128]{1,0:T(8,128)(2,1)S(1)} collective-permute-done((bf16[256,128]{1,0:T(8,128)(2,1)S(1)}, bf16[256,128]{1,0:T(8,128)(2,1)S(1)}, u32[]{:S(2)}, u32[]{:S(2)}) %collective-permute-start.7) | collective-permute-done | bytes 65568 | tf_op jit(solution)/shard_map/ppermute | solution.py:592
  52.6 5.0 %attend_back.1 = (bf16[3,256,128]{2,1,0:T(8,128)(2,1)S(1)}, bf16[3,256,128]{2,1,0:T(8,128)(2,1)S(1)}, bf16[3,256,128]{2,1,0:T(8,128)(2,1)S(1)}, bf16[3,256,128]{2,1,0:T(8,128)(2,1)S(1)}) custom-call(s32[1]{0:T(128)} %bitcast.place_ref, bf16[10,256,256]{2,1,0:T(8,128)(2,1)S(1)} %get-tuple-element.78.prob_ref, f32[4,256,128]{2,1,0:T(8,128)S(1)} %get-tuple-element.79.mixed_ref, ...), custom_call_target="tpu_custom_call" | custom-call | flops 4294967296 | bytes 4194304 | tf_op jit(solution)/shard_map/attend_back/pallas_call | solution.py:570
  57.7 1.9 %collective-permute-start.9 = (bf16[3,256,128]{2,1,0:T(8,128)(2,1)S(1)}, bf16[3,256,128]{2,1,0:T(8,128)(2,1)S(1)}, u32[]{:S(2)}, u32[]{:S(2)}) collective-permute-start(bf16[3,256,128]{2,1,0:T(8,128)(2,1)S(1)} %get-tuple-element.98), channel_id=1, source_target_pairs={{0,8},{4,12},{8,0},{12,4},{1,9},{5,13},{9,1},{13,5},{2,10},{6,14},... | collective-permute-start | bytes 589832 | tf_op jit(solution)/shard_map/ppermute | solution.py:592
  59.5 6.3 %delta_final.1 = (bf16[2048,128]{1,0:T(8,128)(2,1)}, bf16[2048,128]{1,0:T(8,128)(2,1)}, f32[2,4,256]{2,1,0:T(4,128)}, f32[4,256]{1,0:T(4,128)}) custom-call(f32[4,256]{1,0:T(4,128)S(1)} %copy-done.4, bf16[2,4,128,128]{3,2,1,0:T(8,128)(2,1)S(1)} %collective-permute-done.14.near_ref, bf16[4,128,128]{2,1,0:T(8,128)(2,1)S(1)} %collective-permute-done.15.far_ref, ...), custom_call_target="tpu_custom_call" | custom-call | flops 8589934592 | bytes 4194304 | tf_op jit(solution)/shard_map/delta_final/pallas_call | solution.py:411
  66.6 11.0 %collective-permute-done.10.rest_3_ = bf16[3,256,128]{2,1,0:T(8,128)(2,1)S(1)} collective-permute-done((bf16[3,256,128]{2,1,0:T(8,128)(2,1)S(1)}, bf16[3,256,128]{2,1,0:T(8,128)(2,1)S(1)}, u32[]{:S(2)}, u32[]{:S(2)}) %collective-permute-start.10) | collective-permute-done | bytes 196640 | tf_op jit(solution)/shard_map/ppermute | solution.py:592
  (30 shorter events, 4.1 us)
Async XLA Ops:
  0.6 6.1 %copy-start = (bf16[256,2,4,128]{3,2,1,0:T(4,128)(2,1)S(1)}, bf16[256,2,4,128]{3,2,1,0:T(4,128)(2,1)}, u32[]{:S(2)}) copy-start(bf16[256,2,4,128]{3,2,1,0:T(4,128)(2,1)} %param.11) | copy-start | bytes 1572868
  0.6 6.1 %copy-start.1 = (bf16[256,2,4,128]{3,2,1,0:T(4,128)(2,1)S(1)}, bf16[256,2,4,128]{3,2,1,0:T(4,128)(2,1)}, u32[]{:S(2)}) copy-start(bf16[256,2,4,128]{3,2,1,0:T(4,128)(2,1)} %param.12) | copy-start | bytes 1572868
  0.7 6.1 %copy-start.3 = (f32[2,4,256]{2,1,0:T(4,128)S(1)}, f32[2,4,256]{2,1,0:T(4,128)}, u32[]{:S(2)}) copy-start(f32[2,4,256]{2,1,0:T(4,128)} %betas_ref.1) | copy-start | bytes 24580
  0.7 6.1 %copy-start.4 = (f32[4,256]{1,0:T(4,128)S(1)}, f32[4,256]{1,0:T(4,128)}, u32[]{:S(2)}) copy-start(f32[4,256]{1,0:T(4,128)} %decays_ref.3) | copy-start | bytes 12292
  2.9 14.1 %collective-permute-start = (bf16[3,256,128]{2,1,0:T(8,128)(2,1)}, bf16[3,256,128]{2,1,0:T(8,128)(2,1)S(1)}, u32[]{:S(2)}, u32[]{:S(2)}) collective-permute-start(bf16[3,256,128]{2,1,0:T(8,128)(2,1)} %get-tuple-element.75), channel_id=1, source_target_pairs={{0,4},{4,8},{8,12},{12,0},{1,5},{5,9},{9,13},{13,1},{2,6},{6,10},{... | collective-permute-start | bytes 589832 | tf_op jit(solution)/shard_map/ppermute | solution.py:592
  4.3 16.5 %collective-permute-start.1 = (bf16[3,256,128]{2,1,0:T(8,128)(2,1)}, bf16[3,256,128]{2,1,0:T(8,128)(2,1)S(1)}, u32[]{:S(2)}, u32[]{:S(2)}) collective-permute-start(bf16[3,256,128]{2,1,0:T(8,128)(2,1)} %get-tuple-element.76), channel_id=1, source_target_pairs={{0,8},{4,12},{8,0},{12,4},{1,9},{5,13},{9,1},{13,5},{2,10},{6,14},... | collective-permute-start | bytes 589832 | tf_op jit(solution)/shard_map/ppermute | solution.py:592
  5.4 18.2 %collective-permute-start.2 = (bf16[3,256,128]{2,1,0:T(8,128)(2,1)}, bf16[3,256,128]{2,1,0:T(8,128)(2,1)S(1)}, u32[]{:S(2)}, u32[]{:S(2)}) collective-permute-start(bf16[3,256,128]{2,1,0:T(8,128)(2,1)} %get-tuple-element.77), channel_id=1, source_target_pairs={{0,12},{4,0},{8,4},{12,8},{1,13},{5,1},{9,5},{13,9},{2,14},{6,2},{... | collective-permute-start | bytes 589832 | tf_op jit(solution)/shard_map/ppermute | solution.py:592
  6.8 16.8 %copy-start.5 = (bf16[3,256,128]{2,1,0:T(8,128)(2,1)S(1)}, bf16[3,256,128]{2,1,0:T(8,128)(2,1)}, u32[]{:S(2)}) copy-start(bf16[3,256,128]{2,1,0:T(8,128)(2,1)} %get-tuple-element.74.rest_0_) | copy-start | bytes 589828
  14.9 20.8 %copy-start.2 = (bf16[256,4,128]{2,1,0:T(4,128)(2,1)S(1)}, bf16[256,4,128]{2,1,0:T(4,128)(2,1)}, u32[]{:S(2)}) copy-start(bf16[256,4,128]{2,1,0:T(4,128)(2,1)} %param.15) | copy-start | bytes 786436
  14.9 14.0 %collective-permute-start.3 = (bf16[2,4,128,128]{3,2,1,0:T(8,128)(2,1)S(1)}, bf16[2,4,128,128]{3,2,1,0:T(8,128)(2,1)S(1)}, u32[]{:S(2)}, u32[]{:S(2)}) collective-permute-start(bf16[2,4,128,128]{3,2,1,0:T(8,128)(2,1)S(1)} %get-tuple-element.82.map_ref), channel_id=1, source_target_pairs={{0,4},{4,8},{8,12},{1,5},{5,9},{9,13},{2,6},{6,10},{10,14},{3,7},{... | collective-permute-start | bytes 786440 | tf_op jit(solution)/shard_map/ppermute | solution.py:585
  27.1 6.3 %collective-permute-start.11 = (bf16[256,128]{1,0:T(8,128)(2,1)S(1)}, bf16[256,128]{1,0:T(8,128)(2,1)S(1)}, u32[]{:S(2)}, u32[]{:S(2)}) collective-permute-start(bf16[256,128]{1,0:T(8,128)(2,1)S(1)} %get-tuple-element.101), channel_id=1, source_target_pairs={{0,4},{4,8},{8,12},{12,0},{1,5},{5,9},{9,13},{13,1},{2,6},{6,10},{... | collective-permute-start | bytes 196616 | tf_op jit(solution)/shard_map/ppermute | solution.py:592
  27.1 6.2 %collective-permute-start.12 = (bf16[256,128]{1,0:T(8,128)(2,1)S(1)}, bf16[256,128]{1,0:T(8,128)(2,1)S(1)}, u32[]{:S(2)}, u32[]{:S(2)}) collective-permute-start(bf16[256,128]{1,0:T(8,128)(2,1)S(1)} %get-tuple-element.102), channel_id=1, source_target_pairs={{0,8},{4,12},{8,0},{12,4},{1,9},{5,13},{9,1},{13,5},{2,10},{6,14},... | collective-permute-start | bytes 196616 | tf_op jit(solution)/shard_map/ppermute | solution.py:592
  27.5 8.1 %collective-permute-start.13 = (bf16[256,128]{1,0:T(8,128)(2,1)S(1)}, bf16[256,128]{1,0:T(8,128)(2,1)S(1)}, u32[]{:S(2)}, u32[]{:S(2)}) collective-permute-start(bf16[256,128]{1,0:T(8,128)(2,1)S(1)} %get-tuple-element.103), channel_id=1, source_target_pairs={{0,12},{4,0},{8,4},{12,8},{1,13},{5,1},{9,5},{13,9},{2,14},{6,2},{... | collective-permute-start | bytes 196616 | tf_op jit(solution)/shard_map/ppermute | solution.py:592
  29.1 10.8 %collective-permute-start.4 = (bf16[4,128,128]{2,1,0:T(8,128)(2,1)S(1)}, bf16[4,128,128]{2,1,0:T(8,128)(2,1)S(1)}, u32[]{:S(2)}, u32[]{:S(2)}) collective-permute-start(bf16[4,128,128]{2,1,0:T(8,128)(2,1)S(1)} %fusion), channel_id=1, source_target_pairs={{0,8},{4,12},{1,9},{5,13},{2,10},{6,14},{3,11},{7,15},{16,24},{20,... | collective-permute-start | bytes 393224 | tf_op jit(solution)/shard_map/ppermute | solution.py:585
  38.0 10.0 %collective-permute-start.14 = (bf16[2,4,128,128]{3,2,1,0:T(8,128)(2,1)S(1)}, bf16[2,4,128,128]{3,2,1,0:T(8,128)(2,1)S(1)}, u32[]{:S(2)}, u32[]{:S(2)}) collective-permute-start(bf16[2,4,128,128]{3,2,1,0:T(8,128)(2,1)S(1)} %get-tuple-element.108), channel_id=1, source_target_pairs={{4,0},{8,4},{12,8},{5,1},{9,5},{13,9},{6,2},{10,6},{14,10},{7,3},{... | collective-permute-start | bytes 786440 | tf_op jit(solution)/shard_map/ppermute | solution.py:585
  42.6 7.2 %collective-permute-start.5 = (bf16[256,128]{1,0:T(8,128)(2,1)S(1)}, bf16[256,128]{1,0:T(8,128)(2,1)S(1)}, u32[]{:S(2)}, u32[]{:S(2)}) collective-permute-start(bf16[256,128]{1,0:T(8,128)(2,1)S(1)} %get-tuple-element.93), channel_id=1, source_target_pairs={{0,4},{4,8},{8,12},{12,0},{1,5},{5,9},{9,13},{13,1},{2,6},{6,10},{... | collective-permute-start | bytes 196616 | tf_op jit(solution)/shard_map/ppermute | solution.py:592
  44.1 5.7 %collective-permute-start.6 = (bf16[256,128]{1,0:T(8,128)(2,1)S(1)}, bf16[256,128]{1,0:T(8,128)(2,1)S(1)}, u32[]{:S(2)}, u32[]{:S(2)}) collective-permute-start(bf16[256,128]{1,0:T(8,128)(2,1)S(1)} %get-tuple-element.94), channel_id=1, source_target_pairs={{0,8},{4,12},{8,0},{12,4},{1,9},{5,13},{9,1},{13,5},{2,10},{6,14},... | collective-permute-start | bytes 196616 | tf_op jit(solution)/shard_map/ppermute | solution.py:592
  45.3 7.3 %collective-permute-start.7 = (bf16[256,128]{1,0:T(8,128)(2,1)S(1)}, bf16[256,128]{1,0:T(8,128)(2,1)S(1)}, u32[]{:S(2)}, u32[]{:S(2)}) collective-permute-start(bf16[256,128]{1,0:T(8,128)(2,1)S(1)} %get-tuple-element.95), channel_id=1, source_target_pairs={{0,12},{4,0},{8,4},{12,8},{1,13},{5,1},{9,5},{13,9},{2,14},{6,2},{... | collective-permute-start | bytes 196616 | tf_op jit(solution)/shard_map/ppermute | solution.py:592
  48.4 11.1 %collective-permute-start.15 = (bf16[4,128,128]{2,1,0:T(8,128)(2,1)S(1)}, bf16[4,128,128]{2,1,0:T(8,128)(2,1)S(1)}, u32[]{:S(2)}, u32[]{:S(2)}) collective-permute-start(bf16[4,128,128]{2,1,0:T(8,128)(2,1)S(1)} %fusion.1), channel_id=1, source_target_pairs={{8,0},{12,4},{9,1},{13,5},{10,2},{14,6},{11,3},{15,7},{24,16},{28,... | collective-permute-start | bytes 393224 | tf_op jit(solution)/shard_map/ppermute | solution.py:585
  57.6 8.2 %collective-permute-start.8 = (bf16[3,256,128]{2,1,0:T(8,128)(2,1)S(1)}, bf16[3,256,128]{2,1,0:T(8,128)(2,1)S(1)}, u32[]{:S(2)}, u32[]{:S(2)}) collective-permute-start(bf16[3,256,128]{2,1,0:T(8,128)(2,1)S(1)} %get-tuple-element.97), channel_id=1, source_target_pairs={{0,4},{4,8},{8,12},{12,0},{1,5},{5,9},{9,13},{13,1},{2,6},{6,10},{... | collective-permute-start | bytes 589832 | tf_op jit(solution)/shard_map/ppermute | solution.py:592
  57.7 9.0 %collective-permute-start.9 = (bf16[3,256,128]{2,1,0:T(8,128)(2,1)S(1)}, bf16[3,256,128]{2,1,0:T(8,128)(2,1)S(1)}, u32[]{:S(2)}, u32[]{:S(2)}) collective-permute-start(bf16[3,256,128]{2,1,0:T(8,128)(2,1)S(1)} %get-tuple-element.98), channel_id=1, source_target_pairs={{0,8},{4,12},{8,0},{12,4},{1,9},{5,13},{9,1},{13,5},{2,10},{6,14},... | collective-permute-start | bytes 589832 | tf_op jit(solution)/shard_map/ppermute | solution.py:592
  59.5 18.1 %collective-permute-start.10 = (bf16[3,256,128]{2,1,0:T(8,128)(2,1)S(1)}, bf16[3,256,128]{2,1,0:T(8,128)(2,1)S(1)}, u32[]{:S(2)}, u32[]{:S(2)}) collective-permute-start(bf16[3,256,128]{2,1,0:T(8,128)(2,1)S(1)} %get-tuple-element.99), channel_id=1, source_target_pairs={{0,12},{4,0},{8,4},{12,8},{1,13},{5,1},{9,5},{13,9},{2,14},{6,2},{... | collective-permute-start | bytes 589832 | tf_op jit(solution)/shard_map/ppermute | solution.py:592

commit v4 on v3

--- a/solution.py
+++ b/solution.py
@@ -129,7 +129,7 @@
 def local_kernel(heads, count, dk_ref, dv_ref, betas_ref, decays_ref,
                  k_ref, kt_ref, inv_ref, p_ref, y_ref, t_ref, o_ref, fade_ref, see_ref, run_ref, col_ref,
                  tsh_ref, osh_ref, low_ref,
-                 keys_scr, values_scr, sys_scr, full_scr, split_scr, half_scr, rhs_scr):
+                 keys_scr, values_scr, sys_scr, split_scr, half_scr, rhs_scr):
     grid = Grid()
     eye = jnp.where(grid.diag, 1.0, 0.0)
     items = [(h, c) for h in range(heads) for c in range(count)]
@@ -198,22 +198,16 @@
         low_ref[1, h] = tsh_ref[h].astype(BF16)
 
 
-def gather_blocks(place_ref, refs, scr, sem, first):
-    copies = []
+def gather_blocks(place_ref, refs, scr):
     count = len(refs)
     for s in range(count):
-        source = lax.rem(place_ref[0] + count - s, count)
-        copies.append(pltpu.make_async_copy(refs[s], scr.at[source], sem.at[first + s]))
-    return copies
-
-
-def scatter_blocks(place_ref, scr, refs, sem, first):
-    copies = []
+        scr[lax.rem(place_ref[0] + count - s, count)] = refs[s][...]
+
+
+def scatter_blocks(place_ref, scr, refs):
     count = len(refs)
     for s in range(count):
-        target = lax.rem(place_ref[0] + s, count)
-        copies.append(pltpu.make_async_copy(scr.at[target], refs[s], sem.at[first + s]))
-    return copies
+        refs[s][...] = scr[lax.rem(place_ref[0] + s, count)]
 
 
 def head_rows(ref, heads, h, c):
@@ -222,7 +216,7 @@
 
 def readout_kernel(heads, count, place_ref, g_ref, near_ref, far_ref, k_ref, p_ref, y_ref, t_ref, o_ref, see_ref, run_ref,
                    s_ref, u_ref, dw_ref, dq_ref, *rest):
-    outs, (g_scr, dq_scr, sem) = rest[:heads], rest[heads:]
+    outs, (g_scr, dq_scr) = rest[:heads], rest[heads:]
     g_scr[...] = g_ref[...].astype(F32)
     for h in range(heads):
         s_ref[h, 0] = near_ref[0, h].astype(F32) + contract(near_ref[1, h], far_ref[h], 1, 0)
@@ -241,11 +235,7 @@
         grad = mm(dw_ref[h, c], k_ref[h, c]) + dq_ref[h, c]
         dq_ref[h, c] = grad
         dq_scr[h, pl.ds(c * C, C), :] = grad.astype(BF16)
-    copies = scatter_blocks(place_ref, dq_scr, outs, sem, 0)
-    for copy in copies:
-        copy.start()
-    for copy in copies:
-        copy.wait()
+    scatter_blocks(place_ref, dq_scr, outs)
 
 
 def unit_queries(low):
@@ -254,13 +244,9 @@
 
 
 def source_kernel(heads, count, place_ref, g_ref, k_ref, p_ref, t_ref, see_ref, run_ref, map_ref, *rest):
-    ins, (q_ref, z_ref, b_ref, bsh_ref, low_ref, g_scr, q_scr, sem) = rest[:heads], rest[heads:]
-    copies = gather_blocks(place_ref, ins, q_scr, sem, 0)
-    for copy in copies:
-        copy.start()
+    ins, (q_ref, z_ref, b_ref, bsh_ref, low_ref, g_scr, q_scr) = rest[:heads], rest[heads:]
+    gather_blocks(place_ref, ins, q_scr)
     g_scr[...] = g_ref[...].astype(F32)
-    for copy in copies:
-        copy.wait()
     items = [(h, c) for h in range(heads) for c in range(count)]
     weights = {}
     for h, c in items:
@@ -341,7 +327,6 @@
     gv_ref[...] = gv_scr[...].astype(BF16)
 
 
-ANY = pl.BlockSpec(memory_space=pl.ANY)
 HBM = pl.BlockSpec(memory_space=pltpu.HBM)
 SCALAR = pl.BlockSpec(memory_space=pltpu.SMEM)
 VM = pl.BlockSpec(memory_space=pltpu.VMEM)
@@ -373,7 +358,7 @@
     return single(
         functools.partial(local_kernel, heads, count), "delta_local",
         [VM] * 4, outs, [VM] * len(outs),
-        [pltpu.VMEM(dk.shape, F32)] * 2 + [halves, pltpu.VMEM(square.shape, F32), halves, halves]
+        [pltpu.VMEM(dk.shape, F32)] * 2 + [halves] * 3
         + [pltpu.VMEM((heads, count, N, 2 * N), F32)],
         10 << 30,
     )(dk, dv, betas, decays)
@@ -386,8 +371,8 @@
     outs = [shaped((heads, count + 1, N, N)), square, thin, thin]
     return single(
         functools.partial(readout_kernel, heads, count), "delta_readout",
-        [SCALAR] + [VM] * 10, outs + [shaped((rows, N), BF16)] * heads, [VM] * 4 + [ANY] * heads,
-        [pltpu.VMEM(g.shape, F32), pltpu.VMEM((heads, rows, N), BF16), pltpu.SemaphoreType.DMA((heads,))],
+        [SCALAR] + [VM] * 10, outs + [shaped((rows, N), BF16)] * heads, [VM] * (4 + heads),
+        [pltpu.VMEM(g.shape, F32), pltpu.VMEM((heads, rows, N), BF16)],
         3 << 30,
     )(place, g, near, far, k, p, y, t, o, see, run)
 
@@ -398,9 +383,9 @@
     square, thin = (shaped((heads,) + tail) for tail in ((count, N, N), (count, C, N)))
     return single(
         functools.partial(source_kernel, heads, count), "delta_source",
-        [SCALAR] + [VM] * 7 + [ANY] * heads,
+        [SCALAR] + [VM] * (7 + heads),
         [thin, square, square, shaped((heads, N, N)), shaped(low.shape, BF16)], [VM] * 5,
-        [pltpu.VMEM(g.shape, F32), pltpu.VMEM((heads, rows, N), BF16), pltpu.SemaphoreType.DMA((heads,))],
+        [pltpu.VMEM(g.shape, F32), pltpu.VMEM((heads, rows, N), BF16)],
         3 << 30,
     )(place, g, k, p, t, see, run, low, *attended)
 
@@ -449,12 +434,8 @@
 
 def attend_kernel(count, scale, place_ref, *rest):
     ins, (whole_ref, prob_ref, mixed_ref), outs = rest[:count], rest[count:count + 3], rest[count + 3:2 * count + 3]
-    att_scr, sem = rest[2 * count + 3:]
-    copies = gather_blocks(place_ref, ins, whole_ref, sem, 0)
-    for copy in copies:
-        copy.start()
-    for copy in copies:
-        copy.wait()
+    (att_scr,) = rest[2 * count + 3:]
+    gather_blocks(place_ref, ins, whole_ref)
     rows = whole_ref.shape[2]
     causal = iota((rows, rows), 0) <= iota((rows, rows), 1)
     for i in range(count):
@@ -479,21 +460,13 @@
             mixed = term if mixed is None else mixed + term
         mixed_ref[i] = mixed
         att_scr[i] = mixed.astype(BF16)
-    copies = scatter_blocks(place_ref, att_scr, outs, sem, count)
-    for copy in copies:
-        copy.start()
-    for copy in copies:
-        copy.wait()
+    scatter_blocks(place_ref, att_scr, outs)
 
 
 def attend_back_kernel(count, scale, place_ref, prob_ref, mixed_ref, whole_ref, *rest):
     grads, outs = rest[:count], rest[count:2 * count]
-    g_scr, out_scr, acc, sem = rest[2 * count:]
-    copies = gather_blocks(place_ref, grads, g_scr, sem, 0)
-    for copy in copies:
-        copy.start()
-    for copy in copies:
-        copy.wait()
+    g_scr, out_scr, acc = rest[2 * count:]
+    gather_blocks(place_ref, grads, g_scr)
     rows = whole_ref.shape[2]
     ones = jnp.ones((8, N), F32)
     for i in range(count - 1, -1, -1):
@@ -523,11 +496,7 @@
                 acc[j, 0] = gk
                 acc[j, 1] = gv
         out_scr[i, 0] = gq.astype(BF16)
-    copies = scatter_blocks(place_ref, out_scr, outs, sem, count)
-    for copy in copies:
-        copy.start()
-    for copy in copies:
-        copy.wait()
+    scatter_blocks(place_ref, out_scr, outs)
 
 
 def send_heads(place, q, k, v, count):
@@ -557,11 +526,11 @@
     tri = count * (count + 1) // 2
     return single(
         functools.partial(attend_kernel, count, scale), "attend",
-        [SCALAR] + [ANY] * count,
+        [SCALAR] + [VM] * count,
         [shaped((count, 3, rows, N), BF16), shaped((tri, rows, rows), BF16), shaped((count, rows, N))]
         + [shaped((rows, N), BF16)] * count,
-        [VM] * 3 + [ANY] * count,
-        [pltpu.VMEM((count, rows, N), BF16), pltpu.SemaphoreType.DMA((2 * count,))], 2 << 30,
+        [VM] * (3 + count),
+        [pltpu.VMEM((count, rows, N), BF16)], 2 << 30,
     )(place, *parts)
 
 
@@ -569,10 +538,10 @@
     count, _, rows, _ = whole.shape
     return single(
         functools.partial(attend_back_kernel, count, scale), "attend_back",
-        [SCALAR, VM, VM, VM] + [ANY] * count,
-        [shaped((3, rows, N), BF16)] * count, [ANY] * count,
+        [SCALAR] + [VM] * (3 + count),
+        [shaped((3, rows, N), BF16)] * count, [VM] * count,
         [pltpu.VMEM((count, rows, N), BF16), pltpu.VMEM((count, 3, rows, N), BF16),
-         pltpu.VMEM((count, 2, rows, N), F32), pltpu.SemaphoreType.DMA((2 * count,))], 4 << 30,
+         pltpu.VMEM((count, 2, rows, N), F32)], 4 << 30,
     )(place, prob, mixed, whole, *grads)
 
 

time: 78.9 us -> 76.7 us (0.972)
  Pallas kernels: 31.1 us -> 27.8 us
    pallas_call x1, Pallas kernels: 3.54 us -> 2.27 us  [attend(): single(functools.partial(attend_kernel, count, scale), 'attend', [SCALAR]...]
    ppermute x12, waiting for transfers between devices: 23.5 us -> 24.7 us  [rotated(): lax.ppermute(parts[s], axis, [(d, (d + s) % count) for d in range(count)])]
    pallas_call x1, Pallas kernels: 4.97 us -> 3.71 us  [attend_back(): single(functools.partial(attend_back_kernel, count, scale), 'attend_back'...]
  transfers between devices with their start and end apart: 16 -> 16, of which waited for: 7 -> 9; matrix products, arithmetic and copies ran while one was open for 1% -> 1% of each run, Pallas kernels for 35% -> 32%
where the time goes in v4:
time: 76.7 us; the launch traced here: 76.5 us
  Pallas kernels  27.8 us (36%)
  waiting for transfers between devices  25.5 us (33%)
  starting transfers between devices  21.7 us (28%)
  between operations  0.83 us (1%)
    ppermute x12, waiting for transfers between devices, rotated(): lax.ppermute(parts[s], axis, [(d, (d + s) % count) for d in range(count)])  24.7 us
    ppermute x12, starting transfers between devices, rotated(): lax.ppermute(parts[s], axis, [(d, (d + s) % count) for d in range(count)])  12.2 us
    ppermute x4, starting transfers between devices, shifted(): lax.ppermute(value, axis, [(source, source + steps) for source in range(i...  9.51 us
    pallas_call x1, Pallas kernels, delta_local(): single(functools.partial(local_kernel, heads, count), 'delta_local', [VM]...  8.08 us
    pallas_call x1, Pallas kernels, delta_final(): single(functools.partial(final_kernel, heads, count), 'delta_final', [VM]...  6.28 us
    pallas_call x1, Pallas kernels, attend_back(): single(functools.partial(attend_back_kernel, count, scale), 'attend_back'...  3.71 us
    pallas_call x1, Pallas kernels, attend(): single(functools.partial(attend_kernel, count, scale), 'attend', [SCALAR]...  2.27 us
    pallas_call x1, Pallas kernels, send_heads(): single(functools.partial(send_kernel, count), 'send_heads', [SCALAR, HBM,...  2.23 us
  transfers between devices with their start and end apart: 16, of which 9 were waited for; matrix products, arithmetic and copies ran while one was open for 1% of the time, Pallas kernels for 32%

profile of v4, /device:TPU:9, one launch (start us, length us, event | category | flops | bytes accessed | tf_op | source)
XLA Modules:
  0.0 76.5 jit_solution(16418645059631812319)
XLA Ops:
  0.7 2.2 %send_heads.1 = (bf16[3,256,128]{2,1,0:T(8,128)(2,1)}, bf16[3,256,128]{2,1,0:T(8,128)(2,1)}, bf16[3,256,128]{2,1,0:T(8,128)(2,1)}, bf16[3,256,128]{2,1,0:T(8,128)(2,1)}) custom-call(s32[1]{0:T(128)} %bitcast.place_ref, bf16[1024,128]{1,0:T(8,128)(2,1)} %bitcast.24, bf16[1024,128]{1,0:T(8,128)(2,1)} %bitcast.25, bf16[1024,128]{1,0:T(8,128)(2,1)} %bitcast.26), custom_call_target="tpu_custom_call" | custom-call | flops 21474836480 | bytes 4194304 | tf_op jit(solution)/shard_map/send_heads/pallas_call | solution.py:504
  2.9 1.3 %collective-permute-start = (bf16[3,256,128]{2,1,0:T(8,128)(2,1)}, bf16[3,256,128]{2,1,0:T(8,128)(2,1)S(1)}, u32[]{:S(2)}, u32[]{:S(2)}) collective-permute-start(bf16[3,256,128]{2,1,0:T(8,128)(2,1)} %get-tuple-element.75), channel_id=1, source_target_pairs={{0,4},{4,8},{8,12},{12,0},{1,5},{5,9},{9,13},{13,1},{2,6},{6,10},{... | collective-permute-start | bytes 589832 | tf_op jit(solution)/shard_map/ppermute | solution.py:561
  5.4 1.4 %collective-permute-start.2 = (bf16[3,256,128]{2,1,0:T(8,128)(2,1)}, bf16[3,256,128]{2,1,0:T(8,128)(2,1)S(1)}, u32[]{:S(2)}, u32[]{:S(2)}) collective-permute-start(bf16[3,256,128]{2,1,0:T(8,128)(2,1)} %get-tuple-element.77), channel_id=1, source_target_pairs={{0,12},{4,0},{8,4},{12,8},{1,13},{5,1},{9,5},{13,9},{2,14},{6,2},{... | collective-permute-start | bytes 589832 | tf_op jit(solution)/shard_map/ppermute | solution.py:561
  6.8 8.1 %delta_local.1 = (f32[4,4,128,128]{3,2,1,0:T(8,128)S(1)}, f32[4,4,128,128]{3,2,1,0:T(8,128)S(1)}, f32[4,4,128,128]{3,2,1,0:T(8,128)S(1)}, f32[4,4,128,128]{3,2,1...) custom-call(bf16[2048,128]{1,0:T(8,128)(2,1)S(1)} %bitcast.20, ...), custom_call_target="tpu_custom_call" | custom-call | flops 10737418240 | bytes 4194304 | tf_op jit(solution)/shard_map/delta_local/pallas_call | solution.py:358
  14.9 2.1 %collective-permute-start.3 = (bf16[2,4,128,128]{3,2,1,0:T(8,128)(2,1)S(1)}, bf16[2,4,128,128]{3,2,1,0:T(8,128)(2,1)S(1)}, u32[]{:S(2)}, u32[]{:S(2)}) collective-permute-start(bf16[2,4,128,128]{3,2,1,0:T(8,128)(2,1)S(1)} %get-tuple-element.82.map_ref), channel_id=1, source_target_pairs={{0,4},{4,8},{8,12},{1,5},{5,9},{9,13},{2,6},{6,10},{10,14},{3,7},{... | collective-permute-start | bytes 786440 | tf_op jit(solution)/shard_map/ppermute | solution.py:554
  17.0 3.8 %collective-permute-done.1.rest_2_ = bf16[3,256,128]{2,1,0:T(8,128)(2,1)S(1)} collective-permute-done((bf16[3,256,128]{2,1,0:T(8,128)(2,1)}, bf16[3,256,128]{2,1,0:T(8,128)(2,1)S(1)}, u32[]{:S(2)}, u32[]{:S(2)}) %collective-permute-start.1) | collective-permute-done | bytes 196640 | tf_op jit(solution)/shard_map/ppermute | solution.py:561
  20.8 2.7 %collective-permute-done.2.rest_3_ = bf16[3,256,128]{2,1,0:T(8,128)(2,1)S(1)} collective-permute-done((bf16[3,256,128]{2,1,0:T(8,128)(2,1)}, bf16[3,256,128]{2,1,0:T(8,128)(2,1)S(1)}, u32[]{:S(2)}, u32[]{:S(2)}) %collective-permute-start.2) | collective-permute-done | bytes 196640 | tf_op jit(solution)/shard_map/ppermute | solution.py:561
  23.5 2.3 %attend.1 = (bf16[4,3,256,128]{3,2,1,0:T(8,128)(2,1)S(1)}, bf16[10,256,256]{2,1,0:T(8,128)(2,1)S(1)}, f32[4,256,128]{2,1,0:T(8,128)S(1)}, bf16[256,128]{1,0:T(8,...) custom-call(s32[1]{0:T(128)} %bitcast.place_ref, ...), custom_call_target="tpu_custom_call" | custom-call | flops 2147483648 | bytes 4194304 | tf_op jit(solution)/shard_map/attend/pallas_call | solution.py:527
  26.2 1.4 %collective-permute-start.13 = (bf16[256,128]{1,0:T(8,128)(2,1)S(1)}, bf16[256,128]{1,0:T(8,128)(2,1)S(1)}, u32[]{:S(2)}, u32[]{:S(2)}) collective-permute-start(bf16[256,128]{1,0:T(8,128)(2,1)S(1)} %get-tuple-element.103), channel_id=1, source_target_pairs={{0,12},{4,0},{8,4},{12,8},{1,13},{5,1},{9,5},{13,9},{2,14},{6,2},{... | collective-permute-start | bytes 196616 | tf_op jit(solution)/shard_map/ppermute | solution.py:561
  27.9 4.2 %collective-permute-start.4 = (bf16[4,128,128]{2,1,0:T(8,128)(2,1)S(1)}, bf16[4,128,128]{2,1,0:T(8,128)(2,1)S(1)}, u32[]{:S(2)}, u32[]{:S(2)}) collective-permute-start(bf16[4,128,128]{2,1,0:T(8,128)(2,1)S(1)} %fusion), channel_id=1, source_target_pairs={{0,8},{4,12},{1,9},{5,13},{2,10},{6,14},{3,11},{7,15},{16,24},{20,... | collective-permute-start | bytes 393224 | tf_op jit(solution)/shard_map/ppermute | solution.py:554
  32.1 2.3 %collective-permute-done.13.rest_3_ = bf16[256,128]{1,0:T(8,128)(2,1)S(1)} collective-permute-done((bf16[256,128]{1,0:T(8,128)(2,1)S(1)}, bf16[256,128]{1,0:T(8,128)(2,1)S(1)}, u32[]{:S(2)}, u32[]{:S(2)}) %collective-permute-start.13) | collective-permute-done | bytes 65568 | tf_op jit(solution)/shard_map/ppermute | solution.py:561
  34.3 2.0 %delta_source.1 = (f32[4,4,64,128]{3,2,1,0:T(8,128)S(1)}, f32[4,4,128,128]{3,2,1,0:T(8,128)S(1)}, f32[4,4,128,128]{3,2,1,0:T(8,128)S(1)}, f32[4,128,128]{2,1,0:T(8,128)S(1)}, bf16[2,4,128,128]{3,2,1,0:T(8,128)(2,1)S(1)}) custom-call(s32[1]{0:T(128)} %bitcast.place_ref, bf16[1024,128]{1,0:T(8,128)(2,1)S(1)} %bitcast.22, ...), custom_call_target="tpu_custom_call" | custom-call | flops 3221225472 | bytes 4194304 | tf_op jit(solution)/shard_map/delta_source/pallas_call | solution.py:384
  36.4 1.9 %collective-permute-start.14 = (bf16[2,4,128,128]{3,2,1,0:T(8,128)(2,1)S(1)}, bf16[2,4,128,128]{3,2,1,0:T(8,128)(2,1)S(1)}, u32[]{:S(2)}, u32[]{:S(2)}) collective-permute-start(bf16[2,4,128,128]{3,2,1,0:T(8,128)(2,1)S(1)} %get-tuple-element.108), channel_id=1, source_target_pairs={{4,0},{8,4},{12,8},{5,1},{9,5},{13,9},{6,2},{10,6},{14,10},{7,3},{... | collective-permute-start | bytes 786440 | tf_op jit(solution)/shard_map/ppermute | solution.py:554
  38.4 2.2 %delta_readout.1 = (f32[4,5,128,128]{3,2,1,0:T(8,128)S(1)}, f32[4,4,128,128]{3,2,1,0:T(8,128)S(1)}, f32[4,4,64,128]{3,2,1,0:T(8,128)S(1)}, f32[4,4,64,128]{3,2,1...) custom-call(s32[1]{0:T(128)} %bitcast.place_ref, ...), custom_call_target="tpu_custom_call" | custom-call | flops 3221225472 | bytes 4194304 | tf_op jit(solution)/shard_map/delta_readout/pallas_call | solution.py:372
  40.6 1.4 %collective-permute-start.5 = (bf16[256,128]{1,0:T(8,128)(2,1)S(1)}, bf16[256,128]{1,0:T(8,128)(2,1)S(1)}, u32[]{:S(2)}, u32[]{:S(2)}) collective-permute-start(bf16[256,128]{1,0:T(8,128)(2,1)S(1)} %get-tuple-element.93), channel_id=1, source_target_pairs={{0,4},{4,8},{8,12},{12,0},{1,5},{5,9},{9,13},{13,1},{2,6},{6,10},{... | collective-permute-start | bytes 196616 | tf_op jit(solution)/shard_map/ppermute | solution.py:561
  42.0 1.8 %collective-permute-start.6 = (bf16[256,128]{1,0:T(8,128)(2,1)S(1)}, bf16[256,128]{1,0:T(8,128)(2,1)S(1)}, u32[]{:S(2)}, u32[]{:S(2)}) collective-permute-start(bf16[256,128]{1,0:T(8,128)(2,1)S(1)} %get-tuple-element.94), channel_id=1, source_target_pairs={{0,8},{4,12},{8,0},{12,4},{1,9},{5,13},{9,1},{13,5},{2,10},{6,14},... | collective-permute-start | bytes 196616 | tf_op jit(solution)/shard_map/ppermute | solution.py:561
  43.9 1.4 %collective-permute-start.7 = (bf16[256,128]{1,0:T(8,128)(2,1)S(1)}, bf16[256,128]{1,0:T(8,128)(2,1)S(1)}, u32[]{:S(2)}, u32[]{:S(2)}) collective-permute-start(bf16[256,128]{1,0:T(8,128)(2,1)S(1)} %get-tuple-element.95), channel_id=1, source_target_pairs={{0,12},{4,0},{8,4},{12,8},{1,13},{5,1},{9,5},{13,9},{2,14},{6,2},{... | collective-permute-start | bytes 196616 | tf_op jit(solution)/shard_map/ppermute | solution.py:561
  46.3 1.3 %collective-permute-start.15 = (bf16[4,128,128]{2,1,0:T(8,128)(2,1)S(1)}, bf16[4,128,128]{2,1,0:T(8,128)(2,1)S(1)}, u32[]{:S(2)}, u32[]{:S(2)}) collective-permute-start(bf16[4,128,128]{2,1,0:T(8,128)(2,1)S(1)} %fusion.1), channel_id=1, source_target_pairs={{8,0},{12,4},{9,1},{13,5},{10,2},{14,6},{11,3},{15,7},{24,16},{28,... | collective-permute-start | bytes 393224 | tf_op jit(solution)/shard_map/ppermute | solution.py:554
  47.9 2.9 %collective-permute-done.7.rest_3_ = bf16[256,128]{1,0:T(8,128)(2,1)S(1)} collective-permute-done((bf16[256,128]{1,0:T(8,128)(2,1)S(1)}, bf16[256,128]{1,0:T(8,128)(2,1)S(1)}, u32[]{:S(2)}, u32[]{:S(2)}) %collective-permute-start.7) | collective-permute-done | bytes 65568 | tf_op jit(solution)/shard_map/ppermute | solution.py:561
  50.8 3.7 %attend_back.1 = (bf16[3,256,128]{2,1,0:T(8,128)(2,1)S(1)}, bf16[3,256,128]{2,1,0:T(8,128)(2,1)S(1)}, bf16[3,256,128]{2,1,0:T(8,128)(2,1)S(1)}, bf16[3,256,128]{2,1,0:T(8,128)(2,1)S(1)}) custom-call(s32[1]{0:T(128)} %bitcast.place_ref, bf16[10,256,256]{2,1,0:T(8,128)(2,1)S(1)} %get-tuple-element.78.prob_ref, f32[4,256,128]{2,1,0:T(8,128)S(1)} %get-tuple-element.79.mixed_ref, ...), custom_call_target="tpu_custom_call" | custom-call | flops 4294967296 | bytes 4194304 | tf_op jit(solution)/shard_map/attend_back/pallas_call | solution.py:539
  54.6 1.9 %collective-permute-start.9 = (bf16[3,256,128]{2,1,0:T(8,128)(2,1)S(1)}, bf16[3,256,128]{2,1,0:T(8,128)(2,1)S(1)}, u32[]{:S(2)}, u32[]{:S(2)}) collective-permute-start(bf16[3,256,128]{2,1,0:T(8,128)(2,1)S(1)} %get-tuple-element.98), channel_id=1, source_target_pairs={{0,8},{4,12},{8,0},{12,4},{1,9},{5,13},{9,1},{13,5},{2,10},{6,14},... | collective-permute-start | bytes 589832 | tf_op jit(solution)/shard_map/ppermute | solution.py:561
  56.5 6.3 %delta_final.1 = (bf16[2048,128]{1,0:T(8,128)(2,1)}, bf16[2048,128]{1,0:T(8,128)(2,1)}, f32[2,4,256]{2,1,0:T(4,128)}, f32[4,256]{1,0:T(4,128)}) custom-call(f32[4,256]{1,0:T(4,128)S(1)} %copy-done.4, bf16[2,4,128,128]{3,2,1,0:T(8,128)(2,1)S(1)} %collective-permute-done.14.near_ref, bf16[4,128,128]{2,1,0:T(8,128)(2,1)S(1)} %collective-permute-done.15.far_ref, ...), custom_call_target="tpu_custom_call" | custom-call | flops 8589934592 | bytes 4194304 | tf_op jit(solution)/shard_map/delta_final/pallas_call | solution.py:396
  62.7 1.2 %collective-permute-done.9.rest_2_ = bf16[3,256,128]{2,1,0:T(8,128)(2,1)S(1)} collective-permute-done((bf16[3,256,128]{2,1,0:T(8,128)(2,1)S(1)}, bf16[3,256,128]{2,1,0:T(8,128)(2,1)S(1)}, u32[]{:S(2)}, u32[]{:S(2)}) %collective-permute-start.9) | collective-permute-done | bytes 196640 | tf_op jit(solution)/shard_map/ppermute | solution.py:561
  63.9 11.5 %collective-permute-done.10.rest_3_ = bf16[3,256,128]{2,1,0:T(8,128)(2,1)S(1)} collective-permute-done((bf16[3,256,128]{2,1,0:T(8,128)(2,1)S(1)}, bf16[3,256,128]{2,1,0:T(8,128)(2,1)S(1)}, u32[]{:S(2)}, u32[]{:S(2)}) %collective-permute-start.10) | collective-permute-done | bytes 196640 | tf_op jit(solution)/shard_map/ppermute | solution.py:561
  (30 shorter events, 4.4 us)
Async XLA Ops:
  0.6 6.1 %copy-start = (bf16[256,2,4,128]{3,2,1,0:T(4,128)(2,1)S(1)}, bf16[256,2,4,128]{3,2,1,0:T(4,128)(2,1)}, u32[]{:S(2)}) copy-start(bf16[256,2,4,128]{3,2,1,0:T(4,128)(2,1)} %param.11) | copy-start | bytes 1572868
  0.6 6.1 %copy-start.1 = (bf16[256,2,4,128]{3,2,1,0:T(4,128)(2,1)S(1)}, bf16[256,2,4,128]{3,2,1,0:T(4,128)(2,1)}, u32[]{:S(2)}) copy-start(bf16[256,2,4,128]{3,2,1,0:T(4,128)(2,1)} %param.12) | copy-start | bytes 1572868
  0.7 6.1 %copy-start.3 = (f32[2,4,256]{2,1,0:T(4,128)S(1)}, f32[2,4,256]{2,1,0:T(4,128)}, u32[]{:S(2)}) copy-start(f32[2,4,256]{2,1,0:T(4,128)} %betas_ref.1) | copy-start | bytes 24580
  0.7 6.1 %copy-start.4 = (f32[4,256]{1,0:T(4,128)S(1)}, f32[4,256]{1,0:T(4,128)}, u32[]{:S(2)}) copy-start(f32[4,256]{1,0:T(4,128)} %decays_ref.3) | copy-start | bytes 12292
  2.9 14.1 %collective-permute-start = (bf16[3,256,128]{2,1,0:T(8,128)(2,1)}, bf16[3,256,128]{2,1,0:T(8,128)(2,1)S(1)}, u32[]{:S(2)}, u32[]{:S(2)}) collective-permute-start(bf16[3,256,128]{2,1,0:T(8,128)(2,1)} %get-tuple-element.75), channel_id=1, source_target_pairs={{0,4},{4,8},{8,12},{12,0},{1,5},{5,9},{9,13},{13,1},{2,6},{6,10},{... | collective-permute-start | bytes 589832 | tf_op jit(solution)/shard_map/ppermute | solution.py:561
  4.3 16.5 %collective-permute-start.1 = (bf16[3,256,128]{2,1,0:T(8,128)(2,1)}, bf16[3,256,128]{2,1,0:T(8,128)(2,1)S(1)}, u32[]{:S(2)}, u32[]{:S(2)}) collective-permute-start(bf16[3,256,128]{2,1,0:T(8,128)(2,1)} %get-tuple-element.76), channel_id=1, source_target_pairs={{0,8},{4,12},{8,0},{12,4},{1,9},{5,13},{9,1},{13,5},{2,10},{6,14},... | collective-permute-start | bytes 589832 | tf_op jit(solution)/shard_map/ppermute | solution.py:561
  5.4 18.2 %collective-permute-start.2 = (bf16[3,256,128]{2,1,0:T(8,128)(2,1)}, bf16[3,256,128]{2,1,0:T(8,128)(2,1)S(1)}, u32[]{:S(2)}, u32[]{:S(2)}) collective-permute-start(bf16[3,256,128]{2,1,0:T(8,128)(2,1)} %get-tuple-element.77), channel_id=1, source_target_pairs={{0,12},{4,0},{8,4},{12,8},{1,13},{5,1},{9,5},{13,9},{2,14},{6,2},{... | collective-permute-start | bytes 589832 | tf_op jit(solution)/shard_map/ppermute | solution.py:561
  6.8 16.8 %copy-start.5 = (bf16[3,256,128]{2,1,0:T(8,128)(2,1)S(1)}, bf16[3,256,128]{2,1,0:T(8,128)(2,1)}, u32[]{:S(2)}) copy-start(bf16[3,256,128]{2,1,0:T(8,128)(2,1)} %get-tuple-element.74.rest_0_) | copy-start | bytes 589828
  14.9 19.5 %copy-start.2 = (bf16[256,4,128]{2,1,0:T(4,128)(2,1)S(1)}, bf16[256,4,128]{2,1,0:T(4,128)(2,1)}, u32[]{:S(2)}) copy-start(bf16[256,4,128]{2,1,0:T(4,128)(2,1)} %param.15) | copy-start | bytes 786436
  14.9 12.7 %collective-permute-start.3 = (bf16[2,4,128,128]{3,2,1,0:T(8,128)(2,1)S(1)}, bf16[2,4,128,128]{3,2,1,0:T(8,128)(2,1)S(1)}, u32[]{:S(2)}, u32[]{:S(2)}) collective-permute-start(bf16[2,4,128,128]{3,2,1,0:T(8,128)(2,1)S(1)} %get-tuple-element.82.map_ref), channel_id=1, source_target_pairs={{0,4},{4,8},{8,12},{1,5},{5,9},{9,13},{2,6},{6,10},{10,14},{3,7},{... | collective-permute-start | bytes 786440 | tf_op jit(solution)/shard_map/ppermute | solution.py:554
  25.8 6.3 %collective-permute-start.11 = (bf16[256,128]{1,0:T(8,128)(2,1)S(1)}, bf16[256,128]{1,0:T(8,128)(2,1)S(1)}, u32[]{:S(2)}, u32[]{:S(2)}) collective-permute-start(bf16[256,128]{1,0:T(8,128)(2,1)S(1)} %get-tuple-element.101), channel_id=1, source_target_pairs={{0,4},{4,8},{8,12},{12,0},{1,5},{5,9},{9,13},{13,1},{2,6},{6,10},{... | collective-permute-start | bytes 196616 | tf_op jit(solution)/shard_map/ppermute | solution.py:561
  25.9 6.2 %collective-permute-start.12 = (bf16[256,128]{1,0:T(8,128)(2,1)S(1)}, bf16[256,128]{1,0:T(8,128)(2,1)S(1)}, u32[]{:S(2)}, u32[]{:S(2)}) collective-permute-start(bf16[256,128]{1,0:T(8,128)(2,1)S(1)} %get-tuple-element.102), channel_id=1, source_target_pairs={{0,8},{4,12},{8,0},{12,4},{1,9},{5,13},{9,1},{13,5},{2,10},{6,14},... | collective-permute-start | bytes 196616 | tf_op jit(solution)/shard_map/ppermute | solution.py:561
  26.2 8.1 %collective-permute-start.13 = (bf16[256,128]{1,0:T(8,128)(2,1)S(1)}, bf16[256,128]{1,0:T(8,128)(2,1)S(1)}, u32[]{:S(2)}, u32[]{:S(2)}) collective-permute-start(bf16[256,128]{1,0:T(8,128)(2,1)S(1)} %get-tuple-element.103), channel_id=1, source_target_pairs={{0,12},{4,0},{8,4},{12,8},{1,13},{5,1},{9,5},{13,9},{2,14},{6,2},{... | collective-permute-start | bytes 196616 | tf_op jit(solution)/shard_map/ppermute | solution.py:561
  27.9 10.6 %collective-permute-start.4 = (bf16[4,128,128]{2,1,0:T(8,128)(2,1)S(1)}, bf16[4,128,128]{2,1,0:T(8,128)(2,1)S(1)}, u32[]{:S(2)}, u32[]{:S(2)}) collective-permute-start(bf16[4,128,128]{2,1,0:T(8,128)(2,1)S(1)} %fusion), channel_id=1, source_target_pairs={{0,8},{4,12},{1,9},{5,13},{2,10},{6,14},{3,11},{7,15},{16,24},{20,... | collective-permute-start | bytes 393224 | tf_op jit(solution)/shard_map/ppermute | solution.py:554
  36.4 9.5 %collective-permute-start.14 = (bf16[2,4,128,128]{3,2,1,0:T(8,128)(2,1)S(1)}, bf16[2,4,128,128]{3,2,1,0:T(8,128)(2,1)S(1)}, u32[]{:S(2)}, u32[]{:S(2)}) collective-permute-start(bf16[2,4,128,128]{3,2,1,0:T(8,128)(2,1)S(1)} %get-tuple-element.108), channel_id=1, source_target_pairs={{4,0},{8,4},{12,8},{5,1},{9,5},{13,9},{6,2},{10,6},{14,10},{7,3},{... | collective-permute-start | bytes 786440 | tf_op jit(solution)/shard_map/ppermute | solution.py:554
  40.6 6.9 %collective-permute-start.5 = (bf16[256,128]{1,0:T(8,128)(2,1)S(1)}, bf16[256,128]{1,0:T(8,128)(2,1)S(1)}, u32[]{:S(2)}, u32[]{:S(2)}) collective-permute-start(bf16[256,128]{1,0:T(8,128)(2,1)S(1)} %get-tuple-element.93), channel_id=1, source_target_pairs={{0,4},{4,8},{8,12},{12,0},{1,5},{5,9},{9,13},{13,1},{2,6},{6,10},{... | collective-permute-start | bytes 196616 | tf_op jit(solution)/shard_map/ppermute | solution.py:561
  42.0 5.9 %collective-permute-start.6 = (bf16[256,128]{1,0:T(8,128)(2,1)S(1)}, bf16[256,128]{1,0:T(8,128)(2,1)S(1)}, u32[]{:S(2)}, u32[]{:S(2)}) collective-permute-start(bf16[256,128]{1,0:T(8,128)(2,1)S(1)} %get-tuple-element.94), channel_id=1, source_target_pairs={{0,8},{4,12},{8,0},{12,4},{1,9},{5,13},{9,1},{13,5},{2,10},{6,14},... | collective-permute-start | bytes 196616 | tf_op jit(solution)/shard_map/ppermute | solution.py:561
  43.9 6.9 %collective-permute-start.7 = (bf16[256,128]{1,0:T(8,128)(2,1)S(1)}, bf16[256,128]{1,0:T(8,128)(2,1)S(1)}, u32[]{:S(2)}, u32[]{:S(2)}) collective-permute-start(bf16[256,128]{1,0:T(8,128)(2,1)S(1)} %get-tuple-element.95), channel_id=1, source_target_pairs={{0,12},{4,0},{8,4},{12,8},{1,13},{5,1},{9,5},{13,9},{2,14},{6,2},{... | collective-permute-start | bytes 196616 | tf_op jit(solution)/shard_map/ppermute | solution.py:561
  46.3 10.2 %collective-permute-start.15 = (bf16[4,128,128]{2,1,0:T(8,128)(2,1)S(1)}, bf16[4,128,128]{2,1,0:T(8,128)(2,1)S(1)}, u32[]{:S(2)}, u32[]{:S(2)}) collective-permute-start(bf16[4,128,128]{2,1,0:T(8,128)(2,1)S(1)} %fusion.1), channel_id=1, source_target_pairs={{8,0},{12,4},{9,1},{13,5},{10,2},{14,6},{11,3},{15,7},{24,16},{28,... | collective-permute-start | bytes 393224 | tf_op jit(solution)/shard_map/ppermute | solution.py:554
  54.5 8.2 %collective-permute-start.8 = (bf16[3,256,128]{2,1,0:T(8,128)(2,1)S(1)}, bf16[3,256,128]{2,1,0:T(8,128)(2,1)S(1)}, u32[]{:S(2)}, u32[]{:S(2)}) collective-permute-start(bf16[3,256,128]{2,1,0:T(8,128)(2,1)S(1)} %get-tuple-element.97), channel_id=1, source_target_pairs={{0,4},{4,8},{8,12},{12,0},{1,5},{5,9},{9,13},{13,1},{2,6},{6,10},{... | collective-permute-start | bytes 589832 | tf_op jit(solution)/shard_map/ppermute | solution.py:561
  54.6 9.3 %collective-permute-start.9 = (bf16[3,256,128]{2,1,0:T(8,128)(2,1)S(1)}, bf16[3,256,128]{2,1,0:T(8,128)(2,1)S(1)}, u32[]{:S(2)}, u32[]{:S(2)}) collective-permute-start(bf16[3,256,128]{2,1,0:T(8,128)(2,1)S(1)} %get-tuple-element.98), channel_id=1, source_target_pairs={{0,8},{4,12},{8,0},{12,4},{1,9},{5,13},{9,1},{13,5},{2,10},{6,14},... | collective-permute-start | bytes 589832 | tf_op jit(solution)/shard_map/ppermute | solution.py:561
  56.4 19.0 %collective-permute-start.10 = (bf16[3,256,128]{2,1,0:T(8,128)(2,1)S(1)}, bf16[3,256,128]{2,1,0:T(8,128)(2,1)S(1)}, u32[]{:S(2)}, u32[]{:S(2)}) collective-permute-start(bf16[3,256,128]{2,1,0:T(8,128)(2,1)S(1)} %get-tuple-element.99), channel_id=1, source_target_pairs={{0,12},{4,0},{8,4},{12,8},{1,13},{5,1},{9,5},{13,9},{2,14},{6,2},{... | collective-permute-start | bytes 589832 | tf_op jit(solution)/shard_map/ppermute | solution.py:561

commit v5 on v4

--- a/solution.py
+++ b/solution.py
@@ -422,14 +422,19 @@
 
 
 def take_kernel(count, place_ref, *rest):
-    ins, outs, (scr,) = rest[:count], rest[count:count + 3], rest[count + 3:]
+    ins, outs, (scr, low, sem) = rest[:count], rest[count:count + 3], rest[count + 3:]
     heads = count
-    rows = outs[0].shape[0] // heads
+    rows = low.shape[1] // heads
+    copies = []
     for m in range(3):
         for s in range(count):
             head = lax.rem(place_ref[0] + count - s, count)
-            scr[pl.ds(head, rows, stride=heads), :] = ins[s][m].astype(F32)
-        outs[m][...] = scr[...].astype(BF16)
+            scr[m, pl.ds(head, rows, stride=heads), :] = ins[s][m].astype(F32)
+        low[m] = scr[m].astype(BF16)
+        copies.append(pltpu.make_async_copy(low.at[m], outs[m], sem.at[m]))
+        copies[m].start()
+    for copy in copies:
+        copy.wait()
 
 
 def attend_kernel(count, scale, place_ref, *rest):
@@ -515,8 +520,8 @@
     wide = (rows * count, N)
     return single(
         functools.partial(take_kernel, count), "take_heads",
-        [SCALAR] + [VM] * count, [shaped(wide, BF16)] * 3, [VM] * 3,
-        [pltpu.VMEM(wide, F32)], 1 << 28,
+        [SCALAR] + [VM] * count, [shaped(wide, BF16)] * 3, [HBM] * 3,
+        [pltpu.VMEM((3,) + wide, F32), pltpu.VMEM((3,) + wide, BF16), pltpu.SemaphoreType.DMA((3,))], 1 << 28,
     )(place, *parts)
 
 

time: 76.7 us -> 76.9 us (level)
  no operation moved by 1% of the time
where the time goes in v5:
time: 76.9 us; the launch traced here: 76.7 us
  Pallas kernels  27.8 us (36%)
  waiting for transfers between devices  25.5 us (33%)
  starting transfers between devices  21.7 us (28%)
  between operations  1.01 us (1%)
    ppermute x12, waiting for transfers between devices, rotated(): lax.ppermute(parts[s], axis, [(d, (d + s) % count) for d in range(count)])  24.7 us
    ppermute x12, starting transfers between devices, rotated(): lax.ppermute(parts[s], axis, [(d, (d + s) % count) for d in range(count)])  12.2 us
    ppermute x4, starting transfers between devices, shifted(): lax.ppermute(value, axis, [(source, source + steps) for source in range(i...  9.51 us
    pallas_call x1, Pallas kernels, delta_local(): single(functools.partial(local_kernel, heads, count), 'delta_local', [VM]...  8.08 us
    pallas_call x1, Pallas kernels, delta_final(): single(functools.partial(final_kernel, heads, count), 'delta_final', [VM]...  6.28 us
    pallas_call x1, Pallas kernels, attend_back(): single(functools.partial(attend_back_kernel, count, scale), 'attend_back'...  3.71 us
    pallas_call x1, Pallas kernels, attend(): single(functools.partial(attend_kernel, count, scale), 'attend', [SCALAR]...  2.27 us
    pallas_call x1, Pallas kernels, send_heads(): single(functools.partial(send_kernel, count), 'send_heads', [SCALAR, HBM,...  2.23 us
  transfers between devices with their start and end apart: 16, of which 9 were waited for; matrix products, arithmetic and copies ran while one was open for 1% of the time, Pallas kernels for 32%

profile of v5, /device:TPU:9, one launch (start us, length us, event | category | flops | bytes accessed | tf_op | source)
XLA Modules:
  0.0 76.7 jit_solution(2347009919879973406)
XLA Ops:
  0.7 2.2 %send_heads.1 = (bf16[3,256,128]{2,1,0:T(8,128)(2,1)}, bf16[3,256,128]{2,1,0:T(8,128)(2,1)}, bf16[3,256,128]{2,1,0:T(8,128)(2,1)}, bf16[3,256,128]{2,1,0:T(8,128)(2,1)}) custom-call(s32[1]{0:T(128)} %bitcast.place_ref, bf16[1024,128]{1,0:T(8,128)(2,1)} %bitcast.24, bf16[1024,128]{1,0:T(8,128)(2,1)} %bitcast.25, bf16[1024,128]{1,0:T(8,128)(2,1)} %bitcast.26), custom_call_target="tpu_custom_call" | custom-call | flops 21474836480 | bytes 4194304 | tf_op jit(solution)/shard_map/send_heads/pallas_call | solution.py:509
  2.9 1.3 %collective-permute-start = (bf16[3,256,128]{2,1,0:T(8,128)(2,1)}, bf16[3,256,128]{2,1,0:T(8,128)(2,1)S(1)}, u32[]{:S(2)}, u32[]{:S(2)}) collective-permute-start(bf16[3,256,128]{2,1,0:T(8,128)(2,1)} %get-tuple-element.75), channel_id=1, source_target_pairs={{0,4},{4,8},{8,12},{12,0},{1,5},{5,9},{9,13},{13,1},{2,6},{6,10},{... | collective-permute-start | bytes 589832 | tf_op jit(solution)/shard_map/ppermute | solution.py:566
  5.4 1.4 %collective-permute-start.2 = (bf16[3,256,128]{2,1,0:T(8,128)(2,1)}, bf16[3,256,128]{2,1,0:T(8,128)(2,1)S(1)}, u32[]{:S(2)}, u32[]{:S(2)}) collective-permute-start(bf16[3,256,128]{2,1,0:T(8,128)(2,1)} %get-tuple-element.77), channel_id=1, source_target_pairs={{0,12},{4,0},{8,4},{12,8},{1,13},{5,1},{9,5},{13,9},{2,14},{6,2},{... | collective-permute-start | bytes 589832 | tf_op jit(solution)/shard_map/ppermute | solution.py:566
  6.8 8.1 %delta_local.1 = (f32[4,4,128,128]{3,2,1,0:T(8,128)S(1)}, f32[4,4,128,128]{3,2,1,0:T(8,128)S(1)}, f32[4,4,128,128]{3,2,1,0:T(8,128)S(1)}, f32[4,4,128,128]{3,2,1...) custom-call(bf16[2048,128]{1,0:T(8,128)(2,1)S(1)} %bitcast.20, ...), custom_call_target="tpu_custom_call" | custom-call | flops 10737418240 | bytes 4194304 | tf_op jit(solution)/shard_map/delta_local/pallas_call | solution.py:358
  14.9 2.1 %collective-permute-start.3 = (bf16[2,4,128,128]{3,2,1,0:T(8,128)(2,1)S(1)}, bf16[2,4,128,128]{3,2,1,0:T(8,128)(2,1)S(1)}, u32[]{:S(2)}, u32[]{:S(2)}) collective-permute-start(bf16[2,4,128,128]{3,2,1,0:T(8,128)(2,1)S(1)} %get-tuple-element.82.map_ref), channel_id=1, source_target_pairs={{0,4},{4,8},{8,12},{1,5},{5,9},{9,13},{2,6},{6,10},{10,14},{3,7},{... | collective-permute-start | bytes 786440 | tf_op jit(solution)/shard_map/ppermute | solution.py:559
  17.0 3.8 %collective-permute-done.1.rest_2_ = bf16[3,256,128]{2,1,0:T(8,128)(2,1)S(1)} collective-permute-done((bf16[3,256,128]{2,1,0:T(8,128)(2,1)}, bf16[3,256,128]{2,1,0:T(8,128)(2,1)S(1)}, u32[]{:S(2)}, u32[]{:S(2)}) %collective-permute-start.1) | collective-permute-done | bytes 196640 | tf_op jit(solution)/shard_map/ppermute | solution.py:566
  20.8 2.7 %collective-permute-done.2.rest_3_ = bf16[3,256,128]{2,1,0:T(8,128)(2,1)S(1)} collective-permute-done((bf16[3,256,128]{2,1,0:T(8,128)(2,1)}, bf16[3,256,128]{2,1,0:T(8,128)(2,1)S(1)}, u32[]{:S(2)}, u32[]{:S(2)}) %collective-permute-start.2) | collective-permute-done | bytes 196640 | tf_op jit(solution)/shard_map/ppermute | solution.py:566
  23.5 2.3 %attend.1 = (bf16[4,3,256,128]{3,2,1,0:T(8,128)(2,1)S(1)}, bf16[10,256,256]{2,1,0:T(8,128)(2,1)S(1)}, f32[4,256,128]{2,1,0:T(8,128)S(1)}, bf16[256,128]{1,0:T(8,...) custom-call(s32[1]{0:T(128)} %bitcast.place_ref, ...), custom_call_target="tpu_custom_call" | custom-call | flops 2147483648 | bytes 4194304 | tf_op jit(solution)/shard_map/attend/pallas_call | solution.py:532
  26.2 1.4 %collective-permute-start.13 = (bf16[256,128]{1,0:T(8,128)(2,1)S(1)}, bf16[256,128]{1,0:T(8,128)(2,1)S(1)}, u32[]{:S(2)}, u32[]{:S(2)}) collective-permute-start(bf16[256,128]{1,0:T(8,128)(2,1)S(1)} %get-tuple-element.103), channel_id=1, source_target_pairs={{0,12},{4,0},{8,4},{12,8},{1,13},{5,1},{9,5},{13,9},{2,14},{6,2},{... | collective-permute-start | bytes 196616 | tf_op jit(solution)/shard_map/ppermute | solution.py:566
  27.9 4.2 %collective-permute-start.4 = (bf16[4,128,128]{2,1,0:T(8,128)(2,1)S(1)}, bf16[4,128,128]{2,1,0:T(8,128)(2,1)S(1)}, u32[]{:S(2)}, u32[]{:S(2)}) collective-permute-start(bf16[4,128,128]{2,1,0:T(8,128)(2,1)S(1)} %fusion), channel_id=1, source_target_pairs={{0,8},{4,12},{1,9},{5,13},{2,10},{6,14},{3,11},{7,15},{16,24},{20,... | collective-permute-start | bytes 393224 | tf_op jit(solution)/shard_map/ppermute | solution.py:559
  32.1 2.3 %collective-permute-done.13.rest_3_ = bf16[256,128]{1,0:T(8,128)(2,1)S(1)} collective-permute-done((bf16[256,128]{1,0:T(8,128)(2,1)S(1)}, bf16[256,128]{1,0:T(8,128)(2,1)S(1)}, u32[]{:S(2)}, u32[]{:S(2)}) %collective-permute-start.13) | collective-permute-done | bytes 65568 | tf_op jit(solution)/shard_map/ppermute | solution.py:566
  34.3 2.0 %delta_source.1 = (f32[4,4,64,128]{3,2,1,0:T(8,128)S(1)}, f32[4,4,128,128]{3,2,1,0:T(8,128)S(1)}, f32[4,4,128,128]{3,2,1,0:T(8,128)S(1)}, f32[4,128,128]{2,1,0:T(8,128)S(1)}, bf16[2,4,128,128]{3,2,1,0:T(8,128)(2,1)S(1)}) custom-call(s32[1]{0:T(128)} %bitcast.place_ref, bf16[1024,128]{1,0:T(8,128)(2,1)S(1)} %bitcast.22, ...), custom_call_target="tpu_custom_call" | custom-call | flops 3221225472 | bytes 4194304 | tf_op jit(solution)/shard_map/delta_source/pallas_call | solution.py:384
  36.4 1.9 %collective-permute-start.14 = (bf16[2,4,128,128]{3,2,1,0:T(8,128)(2,1)S(1)}, bf16[2,4,128,128]{3,2,1,0:T(8,128)(2,1)S(1)}, u32[]{:S(2)}, u32[]{:S(2)}) collective-permute-start(bf16[2,4,128,128]{3,2,1,0:T(8,128)(2,1)S(1)} %get-tuple-element.108), channel_id=1, source_target_pairs={{4,0},{8,4},{12,8},{5,1},{9,5},{13,9},{6,2},{10,6},{14,10},{7,3},{... | collective-permute-start | bytes 786440 | tf_op jit(solution)/shard_map/ppermute | solution.py:559
  38.4 2.2 %delta_readout.1 = (f32[4,5,128,128]{3,2,1,0:T(8,128)S(1)}, f32[4,4,128,128]{3,2,1,0:T(8,128)S(1)}, f32[4,4,64,128]{3,2,1,0:T(8,128)S(1)}, f32[4,4,64,128]{3,2,1...) custom-call(s32[1]{0:T(128)} %bitcast.place_ref, ...), custom_call_target="tpu_custom_call" | custom-call | flops 3221225472 | bytes 4194304 | tf_op jit(solution)/shard_map/delta_readout/pallas_call | solution.py:372
  40.6 1.4 %collective-permute-start.5 = (bf16[256,128]{1,0:T(8,128)(2,1)S(1)}, bf16[256,128]{1,0:T(8,128)(2,1)S(1)}, u32[]{:S(2)}, u32[]{:S(2)}) collective-permute-start(bf16[256,128]{1,0:T(8,128)(2,1)S(1)} %get-tuple-element.93), channel_id=1, source_target_pairs={{0,4},{4,8},{8,12},{12,0},{1,5},{5,9},{9,13},{13,1},{2,6},{6,10},{... | collective-permute-start | bytes 196616 | tf_op jit(solution)/shard_map/ppermute | solution.py:566
  42.0 1.8 %collective-permute-start.6 = (bf16[256,128]{1,0:T(8,128)(2,1)S(1)}, bf16[256,128]{1,0:T(8,128)(2,1)S(1)}, u32[]{:S(2)}, u32[]{:S(2)}) collective-permute-start(bf16[256,128]{1,0:T(8,128)(2,1)S(1)} %get-tuple-element.94), channel_id=1, source_target_pairs={{0,8},{4,12},{8,0},{12,4},{1,9},{5,13},{9,1},{13,5},{2,10},{6,14},... | collective-permute-start | bytes 196616 | tf_op jit(solution)/shard_map/ppermute | solution.py:566
  43.9 1.4 %collective-permute-start.7 = (bf16[256,128]{1,0:T(8,128)(2,1)S(1)}, bf16[256,128]{1,0:T(8,128)(2,1)S(1)}, u32[]{:S(2)}, u32[]{:S(2)}) collective-permute-start(bf16[256,128]{1,0:T(8,128)(2,1)S(1)} %get-tuple-element.95), channel_id=1, source_target_pairs={{0,12},{4,0},{8,4},{12,8},{1,13},{5,1},{9,5},{13,9},{2,14},{6,2},{... | collective-permute-start | bytes 196616 | tf_op jit(solution)/shard_map/ppermute | solution.py:566
  46.3 1.3 %collective-permute-start.15 = (bf16[4,128,128]{2,1,0:T(8,128)(2,1)S(1)}, bf16[4,128,128]{2,1,0:T(8,128)(2,1)S(1)}, u32[]{:S(2)}, u32[]{:S(2)}) collective-permute-start(bf16[4,128,128]{2,1,0:T(8,128)(2,1)S(1)} %fusion.1), channel_id=1, source_target_pairs={{8,0},{12,4},{9,1},{13,5},{10,2},{14,6},{11,3},{15,7},{24,16},{28,... | collective-permute-start | bytes 393224 | tf_op jit(solution)/shard_map/ppermute | solution.py:559
  47.9 2.9 %collective-permute-done.7.rest_3_ = bf16[256,128]{1,0:T(8,128)(2,1)S(1)} collective-permute-done((bf16[256,128]{1,0:T(8,128)(2,1)S(1)}, bf16[256,128]{1,0:T(8,128)(2,1)S(1)}, u32[]{:S(2)}, u32[]{:S(2)}) %collective-permute-start.7) | collective-permute-done | bytes 65568 | tf_op jit(solution)/shard_map/ppermute | solution.py:566
  50.8 3.7 %attend_back.1 = (bf16[3,256,128]{2,1,0:T(8,128)(2,1)S(1)}, bf16[3,256,128]{2,1,0:T(8,128)(2,1)S(1)}, bf16[3,256,128]{2,1,0:T(8,128)(2,1)S(1)}, bf16[3,256,128]{2,1,0:T(8,128)(2,1)S(1)}) custom-call(s32[1]{0:T(128)} %bitcast.place_ref, bf16[10,256,256]{2,1,0:T(8,128)(2,1)S(1)} %get-tuple-element.78.prob_ref, f32[4,256,128]{2,1,0:T(8,128)S(1)} %get-tuple-element.79.mixed_ref, ...), custom_call_target="tpu_custom_call" | custom-call | flops 4294967296 | bytes 4194304 | tf_op jit(solution)/shard_map/attend_back/pallas_call | solution.py:544
  54.6 1.9 %collective-permute-start.9 = (bf16[3,256,128]{2,1,0:T(8,128)(2,1)S(1)}, bf16[3,256,128]{2,1,0:T(8,128)(2,1)S(1)}, u32[]{:S(2)}, u32[]{:S(2)}) collective-permute-start(bf16[3,256,128]{2,1,0:T(8,128)(2,1)S(1)} %get-tuple-element.98), channel_id=1, source_target_pairs={{0,8},{4,12},{8,0},{12,4},{1,9},{5,13},{9,1},{13,5},{2,10},{6,14},... | collective-permute-start | bytes 589832 | tf_op jit(solution)/shard_map/ppermute | solution.py:566
  56.5 6.3 %delta_final.1 = (bf16[2048,128]{1,0:T(8,128)(2,1)}, bf16[2048,128]{1,0:T(8,128)(2,1)}, f32[2,4,256]{2,1,0:T(4,128)}, f32[4,256]{1,0:T(4,128)}) custom-call(f32[4,256]{1,0:T(4,128)S(1)} %copy-done.4, bf16[2,4,128,128]{3,2,1,0:T(8,128)(2,1)S(1)} %collective-permute-done.14.near_ref, bf16[4,128,128]{2,1,0:T(8,128)(2,1)S(1)} %collective-permute-done.15.far_ref, ...), custom_call_target="tpu_custom_call" | custom-call | flops 8589934592 | bytes 4194304 | tf_op jit(solution)/shard_map/delta_final/pallas_call | solution.py:396
  62.7 1.2 %collective-permute-done.9.rest_2_ = bf16[3,256,128]{2,1,0:T(8,128)(2,1)S(1)} collective-permute-done((bf16[3,256,128]{2,1,0:T(8,128)(2,1)S(1)}, bf16[3,256,128]{2,1,0:T(8,128)(2,1)S(1)}, u32[]{:S(2)}, u32[]{:S(2)}) %collective-permute-start.9) | collective-permute-done | bytes 196640 | tf_op jit(solution)/shard_map/ppermute | solution.py:566
  63.9 11.5 %collective-permute-done.10.rest_3_ = bf16[3,256,128]{2,1,0:T(8,128)(2,1)S(1)} collective-permute-done((bf16[3,256,128]{2,1,0:T(8,128)(2,1)S(1)}, bf16[3,256,128]{2,1,0:T(8,128)(2,1)S(1)}, u32[]{:S(2)}, u32[]{:S(2)}) %collective-permute-start.10) | collective-permute-done | bytes 196640 | tf_op jit(solution)/shard_map/ppermute | solution.py:566
  (30 shorter events, 4.4 us)
Async XLA Ops:
  0.6 6.1 %copy-start = (bf16[256,2,4,128]{3,2,1,0:T(4,128)(2,1)S(1)}, bf16[256,2,4,128]{3,2,1,0:T(4,128)(2,1)}, u32[]{:S(2)}) copy-start(bf16[256,2,4,128]{3,2,1,0:T(4,128)(2,1)} %param.11) | copy-start | bytes 1572868
  0.6 6.1 %copy-start.1 = (bf16[256,2,4,128]{3,2,1,0:T(4,128)(2,1)S(1)}, bf16[256,2,4,128]{3,2,1,0:T(4,128)(2,1)}, u32[]{:S(2)}) copy-start(bf16[256,2,4,128]{3,2,1,0:T(4,128)(2,1)} %param.12) | copy-start | bytes 1572868
  0.7 6.1 %copy-start.3 = (f32[2,4,256]{2,1,0:T(4,128)S(1)}, f32[2,4,256]{2,1,0:T(4,128)}, u32[]{:S(2)}) copy-start(f32[2,4,256]{2,1,0:T(4,128)} %betas_ref.1) | copy-start | bytes 24580
  0.7 6.1 %copy-start.4 = (f32[4,256]{1,0:T(4,128)S(1)}, f32[4,256]{1,0:T(4,128)}, u32[]{:S(2)}) copy-start(f32[4,256]{1,0:T(4,128)} %decays_ref.3) | copy-start | bytes 12292
  2.9 14.1 %collective-permute-start = (bf16[3,256,128]{2,1,0:T(8,128)(2,1)}, bf16[3,256,128]{2,1,0:T(8,128)(2,1)S(1)}, u32[]{:S(2)}, u32[]{:S(2)}) collective-permute-start(bf16[3,256,128]{2,1,0:T(8,128)(2,1)} %get-tuple-element.75), channel_id=1, source_target_pairs={{0,4},{4,8},{8,12},{12,0},{1,5},{5,9},{9,13},{13,1},{2,6},{6,10},{... | collective-permute-start | bytes 589832 | tf_op jit(solution)/shard_map/ppermute | solution.py:566
  4.3 16.5 %collective-permute-start.1 = (bf16[3,256,128]{2,1,0:T(8,128)(2,1)}, bf16[3,256,128]{2,1,0:T(8,128)(2,1)S(1)}, u32[]{:S(2)}, u32[]{:S(2)}) collective-permute-start(bf16[3,256,128]{2,1,0:T(8,128)(2,1)} %get-tuple-element.76), channel_id=1, source_target_pairs={{0,8},{4,12},{8,0},{12,4},{1,9},{5,13},{9,1},{13,5},{2,10},{6,14},... | collective-permute-start | bytes 589832 | tf_op jit(solution)/shard_map/ppermute | solution.py:566
  5.4 18.2 %collective-permute-start.2 = (bf16[3,256,128]{2,1,0:T(8,128)(2,1)}, bf16[3,256,128]{2,1,0:T(8,128)(2,1)S(1)}, u32[]{:S(2)}, u32[]{:S(2)}) collective-permute-start(bf16[3,256,128]{2,1,0:T(8,128)(2,1)} %get-tuple-element.77), channel_id=1, source_target_pairs={{0,12},{4,0},{8,4},{12,8},{1,13},{5,1},{9,5},{13,9},{2,14},{6,2},{... | collective-permute-start | bytes 589832 | tf_op jit(solution)/shard_map/ppermute | solution.py:566
  6.8 16.8 %copy-start.5 = (bf16[3,256,128]{2,1,0:T(8,128)(2,1)S(1)}, bf16[3,256,128]{2,1,0:T(8,128)(2,1)}, u32[]{:S(2)}) copy-start(bf16[3,256,128]{2,1,0:T(8,128)(2,1)} %get-tuple-element.74.rest_0_) | copy-start | bytes 589828
  14.9 19.5 %copy-start.2 = (bf16[256,4,128]{2,1,0:T(4,128)(2,1)S(1)}, bf16[256,4,128]{2,1,0:T(4,128)(2,1)}, u32[]{:S(2)}) copy-start(bf16[256,4,128]{2,1,0:T(4,128)(2,1)} %param.15) | copy-start | bytes 786436
  14.9 12.7 %collective-permute-start.3 = (bf16[2,4,128,128]{3,2,1,0:T(8,128)(2,1)S(1)}, bf16[2,4,128,128]{3,2,1,0:T(8,128)(2,1)S(1)}, u32[]{:S(2)}, u32[]{:S(2)}) collective-permute-start(bf16[2,4,128,128]{3,2,1,0:T(8,128)(2,1)S(1)} %get-tuple-element.82.map_ref), channel_id=1, source_target_pairs={{0,4},{4,8},{8,12},{1,5},{5,9},{9,13},{2,6},{6,10},{10,14},{3,7},{... | collective-permute-start | bytes 786440 | tf_op jit(solution)/shard_map/ppermute | solution.py:559
  25.8 6.3 %collective-permute-start.11 = (bf16[256,128]{1,0:T(8,128)(2,1)S(1)}, bf16[256,128]{1,0:T(8,128)(2,1)S(1)}, u32[]{:S(2)}, u32[]{:S(2)}) collective-permute-start(bf16[256,128]{1,0:T(8,128)(2,1)S(1)} %get-tuple-element.101), channel_id=1, source_target_pairs={{0,4},{4,8},{8,12},{12,0},{1,5},{5,9},{9,13},{13,1},{2,6},{6,10},{... | collective-permute-start | bytes 196616 | tf_op jit(solution)/shard_map/ppermute | solution.py:566
  25.9 6.2 %collective-permute-start.12 = (bf16[256,128]{1,0:T(8,128)(2,1)S(1)}, bf16[256,128]{1,0:T(8,128)(2,1)S(1)}, u32[]{:S(2)}, u32[]{:S(2)}) collective-permute-start(bf16[256,128]{1,0:T(8,128)(2,1)S(1)} %get-tuple-element.102), channel_id=1, source_target_pairs={{0,8},{4,12},{8,0},{12,4},{1,9},{5,13},{9,1},{13,5},{2,10},{6,14},... | collective-permute-start | bytes 196616 | tf_op jit(solution)/shard_map/ppermute | solution.py:566
  26.2 8.1 %collective-permute-start.13 = (bf16[256,128]{1,0:T(8,128)(2,1)S(1)}, bf16[256,128]{1,0:T(8,128)(2,1)S(1)}, u32[]{:S(2)}, u32[]{:S(2)}) collective-permute-start(bf16[256,128]{1,0:T(8,128)(2,1)S(1)} %get-tuple-element.103), channel_id=1, source_target_pairs={{0,12},{4,0},{8,4},{12,8},{1,13},{5,1},{9,5},{13,9},{2,14},{6,2},{... | collective-permute-start | bytes 196616 | tf_op jit(solution)/shard_map/ppermute | solution.py:566
  27.9 10.6 %collective-permute-start.4 = (bf16[4,128,128]{2,1,0:T(8,128)(2,1)S(1)}, bf16[4,128,128]{2,1,0:T(8,128)(2,1)S(1)}, u32[]{:S(2)}, u32[]{:S(2)}) collective-permute-start(bf16[4,128,128]{2,1,0:T(8,128)(2,1)S(1)} %fusion), channel_id=1, source_target_pairs={{0,8},{4,12},{1,9},{5,13},{2,10},{6,14},{3,11},{7,15},{16,24},{20,... | collective-permute-start | bytes 393224 | tf_op jit(solution)/shard_map/ppermute | solution.py:559
  36.4 9.5 %collective-permute-start.14 = (bf16[2,4,128,128]{3,2,1,0:T(8,128)(2,1)S(1)}, bf16[2,4,128,128]{3,2,1,0:T(8,128)(2,1)S(1)}, u32[]{:S(2)}, u32[]{:S(2)}) collective-permute-start(bf16[2,4,128,128]{3,2,1,0:T(8,128)(2,1)S(1)} %get-tuple-element.108), channel_id=1, source_target_pairs={{4,0},{8,4},{12,8},{5,1},{9,5},{13,9},{6,2},{10,6},{14,10},{7,3},{... | collective-permute-start | bytes 786440 | tf_op jit(solution)/shard_map/ppermute | solution.py:559
  40.6 6.9 %collective-permute-start.5 = (bf16[256,128]{1,0:T(8,128)(2,1)S(1)}, bf16[256,128]{1,0:T(8,128)(2,1)S(1)}, u32[]{:S(2)}, u32[]{:S(2)}) collective-permute-start(bf16[256,128]{1,0:T(8,128)(2,1)S(1)} %get-tuple-element.93), channel_id=1, source_target_pairs={{0,4},{4,8},{8,12},{12,0},{1,5},{5,9},{9,13},{13,1},{2,6},{6,10},{... | collective-permute-start | bytes 196616 | tf_op jit(solution)/shard_map/ppermute | solution.py:566
  42.0 5.9 %collective-permute-start.6 = (bf16[256,128]{1,0:T(8,128)(2,1)S(1)}, bf16[256,128]{1,0:T(8,128)(2,1)S(1)}, u32[]{:S(2)}, u32[]{:S(2)}) collective-permute-start(bf16[256,128]{1,0:T(8,128)(2,1)S(1)} %get-tuple-element.94), channel_id=1, source_target_pairs={{0,8},{4,12},{8,0},{12,4},{1,9},{5,13},{9,1},{13,5},{2,10},{6,14},... | collective-permute-start | bytes 196616 | tf_op jit(solution)/shard_map/ppermute | solution.py:566
  43.9 6.9 %collective-permute-start.7 = (bf16[256,128]{1,0:T(8,128)(2,1)S(1)}, bf16[256,128]{1,0:T(8,128)(2,1)S(1)}, u32[]{:S(2)}, u32[]{:S(2)}) collective-permute-start(bf16[256,128]{1,0:T(8,128)(2,1)S(1)} %get-tuple-element.95), channel_id=1, source_target_pairs={{0,12},{4,0},{8,4},{12,8},{1,13},{5,1},{9,5},{13,9},{2,14},{6,2},{... | collective-permute-start | bytes 196616 | tf_op jit(solution)/shard_map/ppermute | solution.py:566
  46.3 10.2 %collective-permute-start.15 = (bf16[4,128,128]{2,1,0:T(8,128)(2,1)S(1)}, bf16[4,128,128]{2,1,0:T(8,128)(2,1)S(1)}, u32[]{:S(2)}, u32[]{:S(2)}) collective-permute-start(bf16[4,128,128]{2,1,0:T(8,128)(2,1)S(1)} %fusion.1), channel_id=1, source_target_pairs={{8,0},{12,4},{9,1},{13,5},{10,2},{14,6},{11,3},{15,7},{24,16},{28,... | collective-permute-start | bytes 393224 | tf_op jit(solution)/shard_map/ppermute | solution.py:559
  54.5 8.2 %collective-permute-start.8 = (bf16[3,256,128]{2,1,0:T(8,128)(2,1)S(1)}, bf16[3,256,128]{2,1,0:T(8,128)(2,1)S(1)}, u32[]{:S(2)}, u32[]{:S(2)}) collective-permute-start(bf16[3,256,128]{2,1,0:T(8,128)(2,1)S(1)} %get-tuple-element.97), channel_id=1, source_target_pairs={{0,4},{4,8},{8,12},{12,0},{1,5},{5,9},{9,13},{13,1},{2,6},{6,10},{... | collective-permute-start | bytes 589832 | tf_op jit(solution)/shard_map/ppermute | solution.py:566
  54.6 9.3 %collective-permute-start.9 = (bf16[3,256,128]{2,1,0:T(8,128)(2,1)S(1)}, bf16[3,256,128]{2,1,0:T(8,128)(2,1)S(1)}, u32[]{:S(2)}, u32[]{:S(2)}) collective-permute-start(bf16[3,256,128]{2,1,0:T(8,128)(2,1)S(1)} %get-tuple-element.98), channel_id=1, source_target_pairs={{0,8},{4,12},{8,0},{12,4},{1,9},{5,13},{9,1},{13,5},{2,10},{6,14},... | collective-permute-start | bytes 589832 | tf_op jit(solution)/shard_map/ppermute | solution.py:566
  56.4 19.0 %collective-permute-start.10 = (bf16[3,256,128]{2,1,0:T(8,128)(2,1)S(1)}, bf16[3,256,128]{2,1,0:T(8,128)(2,1)S(1)}, u32[]{:S(2)}, u32[]{:S(2)}) collective-permute-start(bf16[3,256,128]{2,1,0:T(8,128)(2,1)S(1)} %get-tuple-element.99), channel_id=1, source_target_pairs={{0,12},{4,0},{8,4},{12,8},{1,13},{5,1},{9,5},{13,9},{2,14},{6,2},{... | collective-permute-start | bytes 589832 | tf_op jit(solution)/shard_map/ppermute | solution.py:566
